TPU v7x, 32 devices: a whole 2x2x4 slice. The times are simulated.
32 devices in a mesh: dir: 2 (over x), gx: 16 (over z, y, core).
Axes of the slice: x: 2, y: 2, z: 4, core: 2. Of those that a mesh axis runs over, the one named last changes fastest.
Arguments:
- pops: float32 [19, 128, 64, 128], P(None, ('dir', 'gx')), parts along dimension 1, may hold values from 0.5 to 1.5
- heights: int32 [128, 128], P(('dir', 'gx')), parts along dimension 0, may hold values from 0 to 32
Outputs:
- pops_out: float32 [19, 128, 64, 128], P(None, ('dir', 'gx')), parts along dimension 1
There are 2 independent parts, one for each index of `dir`. A program takes and returns all parts, laid end to end along the dimension named above; each array names one. Nothing has to cross between parts.
All inputs are finite; a program needn't handle non-finite values.
Results may differ from a plain program's by a relative error of at most 0.0003.
Values sent between devices are 32-bit elements; how exact they have to be, the bound alone decides.
No kernel may reach another device: no remote copies, remote signals or barrier semaphores. Data moves between devices by JAX's collectives and lax.ppermute only.
A program may use at most 64 MiB of HBM per device.

v0:
```python
import jax
import jax.numpy as jnp
from jax import lax
from jax.sharding import PartitionSpec as P

STEPS = 6


velocity_table = [
    (0, 0, 0),
    (1, 0, 0),
    (-1, 0, 0),
    (0, 1, 0),
    (0, -1, 0),
    (0, 0, 1),
    (0, 0, -1),
    (1, 1, 0),
    (-1, -1, 0),
    (1, -1, 0),
    (-1, 1, 0),
    (1, 0, 1),
    (-1, 0, -1),
    (1, 0, -1),
    (-1, 0, 1),
    (0, 1, 1),
    (0, -1, -1),
    (0, 1, -1),
    (0, -1, 1),
]
weight_table = [1.0 / 3.0] + [1.0 / 18.0] * 6 + [1.0 / 36.0] * 12
omega_rate = 1.9
plus_list = [1, 7, 9, 11, 13]
minus_list = [2, 8, 10, 12, 14]


def padded(x, sides, width):
    for axis, dim in sides:
        devices, length = (lax.axis_size(axis), x.shape[dim])
        up = [(i, (i + 1) % devices) for i in range(devices)]
        down = [(j, i) for i, j in up]
        last = lax.slice_in_dim(x, length - width, length, axis=dim)
        initial = lax.slice_in_dim(x, 0, width, axis=dim)
        before = lax.ppermute(last, axis, up)
        after = lax.ppermute(initial, axis, down)
        x = jnp.concatenate([before, x, after], axis=dim)
    return x


def passed_along(block, axis, distance):
    devices = range(lax.axis_size(axis))
    route = [((i - distance) % len(devices), i) for i in devices]
    return lax.ppermute(block, axis, route)


def opposite(component):
    if component == 0:
        return 0
    return component + 1 if component % 2 == 1 else component - 1


def collide(populations):
    density = jnp.zeros_like(populations[0])
    moment_x = jnp.zeros_like(populations[0])
    moment_y = jnp.zeros_like(populations[0])
    moment_z = jnp.zeros_like(populations[0])
    for component in range(19):
        step_x, step_y, step_z = velocity_table[component]
        term = weight_table[component] * populations[component]
        density = density + term
        if step_x != 0:
            moment_x = moment_x + step_x * term
        if step_y != 0:
            moment_y = moment_y + step_y * term
        if step_z != 0:
            moment_z = moment_z + step_z * term
    speed_x = moment_x / density
    speed_y = moment_y / density
    speed_z = moment_z / density
    speed_sq = speed_x * speed_x + speed_y * speed_y + speed_z * speed_z
    result = []
    for component in range(19):
        step_x, step_y, step_z = velocity_table[component]
        along = step_x * speed_x + step_y * speed_y + step_z * speed_z
        equil = density * (1.0 + 3.0 * along + 4.5 * along * along - 1.5 * speed_sq)
        result.append(populations[component] + omega_rate * (equil - populations[component]))
    return result


def shift_local(field, step_z, step_y, fill):
    moved = jnp.roll(field, step_y, axis=2)
    if step_z == 1:
        moved = jnp.concatenate([jnp.full_like(moved[:, :1], fill), moved[:, :-1]], axis=1)
    elif step_z == -1:
        moved = jnp.concatenate([moved[:, 1:], jnp.full_like(moved[:, :1], fill)], axis=1)
    return moved


def per_device(pops, heights):
    width = pops.shape[1]
    height_ext = padded(heights, (("gx", 0),), 1)
    zcoord = lax.broadcasted_iota(jnp.int32, (width + 2, pops.shape[2], pops.shape[3]), 1)
    fluid_ext = (zcoord >= height_ext[:, None, :]).astype(jnp.float32)
    current = [pops[component] for component in range(19)]
    for step_count in range(STEPS):
        post = collide(current)
        stacked = jnp.stack(post)
        left_planes = passed_along(
            jnp.stack([stacked[component, width - 1 :] for component in plus_list]), "gx", 1
        )
        right_planes = passed_along(
            jnp.stack([stacked[component, :1] for component in minus_list]), "gx", -1
        )
        moved_x = []
        for component in range(19):
            step_x = velocity_table[component][0]
            if step_x == 1:
                slot = plus_list.index(component)
                moved_x.append(
                    jnp.concatenate([left_planes[slot], post[component][: width - 1]], axis=0)
                )
            elif step_x == -1:
                slot = minus_list.index(component)
                moved_x.append(jnp.concatenate([post[component][1:], right_planes[slot]], axis=0))
            else:
                moved_x.append(post[component])
        current = []
        for component in range(19):
            step_x, step_y, step_z = velocity_table[component]
            source_fluid = shift_local(
                fluid_ext[1 - step_x : 1 - step_x + width], step_z, step_y, 0.0
            )
            moved = shift_local(moved_x[component], step_z, step_y, 0.0)
            current.append(jnp.where(source_fluid > 0.5, moved, post[opposite(component)]))
    return jnp.stack(current)


def solution(mesh):
    placed = (P(None, ("dir", "gx"), None, None), P(("dir", "gx"), None))
    return jax.shard_map(
        per_device,
        mesh=mesh,
        in_specs=placed,
        out_specs=P(None, ("dir", "gx"), None, None),
        check_vma=False,
    )
```

profile of v0, /device:TPU:0, one launch (start us, length us, event | category | flops | bytes accessed | tf_op | source)
XLA Modules:
  0.0 92.2 jit_solution(16460348759297599917)
XLA Ops:
  0.0 0.8 fusion.974
  1.3 5.0 %collective-permute-start.1 = (s32[1,128]{1,0:T(1,128)S(1)}, s32[1,128]{1,0:T(1,128)S(1)}, u32[]{:S(2)}, u32[]{:S(2)}) collective-permute-start(s32[1,128]{1,0:T(1,128)S(1)} %get-tuple-element.401), channel_id=1, source_target_pairs={{1,0},{2,1},{3,2},{4,3},{5,4},{6,5},{7,6},{8,7},{9,8},{10,9},{11,1... | collective-permute-start | bytes 1544 | tf_op jit(solution)/shard_map/ppermute | solution.py:44
  6.3 2.1 %multiply_add_fusion.5 = (f32[1,4,64,128]{3,2,1,0:T(8,128)S(1)}, f32[1,4,64,128]{3,2,1,0:T(8,128)S(1)}, f32[1,4,64,128]{3,2,1,0:T(8,128)S(1)}, f32[1,4,64,128]{3...) fusion(f32[19,4,64,128]{3,2,1,0:T(8,128)} %param.2), kind=kLoop, calls=%fused_computation.1267 | loop fusion | flops 2785280 | bytes 3276800 | tf_op jit(solution)/shard_map/add | solution.py:84
  9.1 0.8 collective-permute-start.3
  11.9 5.4 %collective-permute-done.2 = f32[5,1,64,128]{3,2,1,0:T(8,128)S(1)} collective-permute-done((f32[5,1,64,128]{3,2,1,0:T(8,128)S(1)}, f32[5,1,64,128]{3,2,1,0:T(8,128)S(1)}, u32[]{:S(2)}, u32[]{:S(2)}) %collective-permute-start.2) | collective-permute-done | bytes 163872 | tf_op jit(solution)/shard_map/ppermute | solution.py:52
  18.6 1.9 %fusion.138 = (f32[4,64,128]{2,1,0:T(8,128)S(1)}, f32[4,64,128]{2,1,0:T(8,128)S(1)}, f32[4,64,128]{2,1,0:T(8,128)S(1)}, f32[4,64,128]{2,1,0:T(8,128)S(1)}, f32[4...) fusion(f32[4,64,128]{2,1,0:T(8,128)S(1)} %get-tuple-element.182, ...), kind=kLoop, calls=%fused_computation.342 | loop fusion | flops 6193152 | bytes 11412480 | tf_op jit(solution)/shard_map/add | solution.py:85
  21.0 7.5 %collective-permute-done.4 = f32[5,1,64,128]{3,2,1,0:T(8,128)S(1)} collective-permute-done((f32[5,1,64,128]{3,2,1,0:T(8,128)S(1)}, f32[5,1,64,128]{3,2,1,0:T(8,128)S(1)}, u32[]{:S(2)}, u32[]{:S(2)}) %collective-permute-start.4) | collective-permute-done | bytes 163872 | tf_op jit(solution)/shard_map/ppermute | solution.py:52
  30.3 1.9 %collective-permute-done.5 = f32[5,1,64,128]{3,2,1,0:T(8,128)S(1)} collective-permute-done((f32[5,1,64,128]{3,2,1,0:T(8,128)S(1)}, f32[5,1,64,128]{3,2,1,0:T(8,128)S(1)}, u32[]{:S(2)}, u32[]{:S(2)}) %collective-permute-start.5) | collective-permute-done | bytes 163872 | tf_op jit(solution)/shard_map/ppermute | solution.py:52
  32.4 1.4 %fusion.252 = (f32[4,64,128]{2,1,0:T(8,128)S(1)}, f32[4,64,128]{2,1,0:T(8,128)S(1)}, f32[4,64,128]{2,1,0:T(8,128)S(1)}, f32[4,64,128]{2,1,0:T(8,128)S(1)}, f32[4...) fusion(f32[4,64,128]{2,1,0:T(8,128)S(1)} %get-tuple-element.277, ...), kind=kLoop, calls=%fused_computation.456 | loop fusion | flops 5472256 | bytes 9204736 | tf_op jit(solution)/shard_map/add | solution.py:85
  34.4 7.8 %collective-permute-done.6 = f32[5,1,64,128]{3,2,1,0:T(8,128)S(1)} collective-permute-done((f32[5,1,64,128]{3,2,1,0:T(8,128)S(1)}, f32[5,1,64,128]{3,2,1,0:T(8,128)S(1)}, u32[]{:S(2)}, u32[]{:S(2)}) %collective-permute-start.6) | collective-permute-done | bytes 163872 | tf_op jit(solution)/shard_map/ppermute | solution.py:52
  44.1 1.9 %collective-permute-done.7 = f32[5,1,64,128]{3,2,1,0:T(8,128)S(1)} collective-permute-done((f32[5,1,64,128]{3,2,1,0:T(8,128)S(1)}, f32[5,1,64,128]{3,2,1,0:T(8,128)S(1)}, u32[]{:S(2)}, u32[]{:S(2)}) %collective-permute-start.7) | collective-permute-done | bytes 163872 | tf_op jit(solution)/shard_map/ppermute | solution.py:52
  46.2 1.4 %fusion.366 = (f32[4,64,128]{2,1,0:T(8,128)S(1)}, f32[4,64,128]{2,1,0:T(8,128)S(1)}, f32[4,64,128]{2,1,0:T(8,128)S(1)}, f32[4,64,128]{2,1,0:T(8,128)S(1)}, f32[4...) fusion(f32[4,64,128]{2,1,0:T(8,128)S(1)} %get-tuple-element.259, ...), kind=kLoop, calls=%fused_computation.570 | loop fusion | flops 5472256 | bytes 9204736 | tf_op jit(solution)/shard_map/add | solution.py:85
  48.2 7.8 %collective-permute-done.8 = f32[5,1,64,128]{3,2,1,0:T(8,128)S(1)} collective-permute-done((f32[5,1,64,128]{3,2,1,0:T(8,128)S(1)}, f32[5,1,64,128]{3,2,1,0:T(8,128)S(1)}, u32[]{:S(2)}, u32[]{:S(2)}) %collective-permute-start.8) | collective-permute-done | bytes 163872 | tf_op jit(solution)/shard_map/ppermute | solution.py:52
  57.7 1.9 %collective-permute-done.9 = f32[5,1,64,128]{3,2,1,0:T(8,128)S(1)} collective-permute-done((f32[5,1,64,128]{3,2,1,0:T(8,128)S(1)}, f32[5,1,64,128]{3,2,1,0:T(8,128)S(1)}, u32[]{:S(2)}, u32[]{:S(2)}) %collective-permute-start.9) | collective-permute-done | bytes 163872 | tf_op jit(solution)/shard_map/ppermute | solution.py:52
  59.9 1.4 %fusion.480 = (f32[4,64,128]{2,1,0:T(8,128)S(1)}, f32[4,64,128]{2,1,0:T(8,128)S(1)}, f32[4,64,128]{2,1,0:T(8,128)S(1)}, f32[4,64,128]{2,1,0:T(8,128)S(1)}, f32[4...) fusion(f32[4,64,128]{2,1,0:T(8,128)S(1)} %get-tuple-element.241, ...), kind=kLoop, calls=%fused_computation.684 | loop fusion | flops 5472256 | bytes 9204736 | tf_op jit(solution)/shard_map/add | solution.py:85
  61.3 0.7 fusion.522
  62.6 4.7 %collective-permute-start.11 = (f32[5,1,64,128]{3,2,1,0:T(8,128)S(1)}, f32[5,1,64,128]{3,2,1,0:T(8,128)S(1)}, u32[]{:S(2)}, u32[]{:S(2)}) collective-permute-start(f32[5,1,64,128]{3,2,1,0:T(8,128)S(1)} %constant_dynamic-update-slice_fusion.45), channel_id=1, source_target_pairs={{1,0},{2,1},{3,2},{4,3},{5,4},{6,5},{7,6},{8,7},{9,8},{10,9},{11,1... | collective-permute-start | bytes 491528 | tf_op jit(solution)/shard_map/ppermute | solution.py:52
  67.9 2.2 %collective-permute-done.11 = f32[5,1,64,128]{3,2,1,0:T(8,128)S(1)} collective-permute-done((f32[5,1,64,128]{3,2,1,0:T(8,128)S(1)}, f32[5,1,64,128]{3,2,1,0:T(8,128)S(1)}, u32[]{:S(2)}, u32[]{:S(2)}) %collective-permute-start.11) | collective-permute-done | bytes 163872 | tf_op jit(solution)/shard_map/ppermute | solution.py:52
  70.3 4.5 %collective-permute-done.10 = f32[5,1,64,128]{3,2,1,0:T(8,128)S(1)} collective-permute-done((f32[5,1,64,128]{3,2,1,0:T(8,128)S(1)}, f32[5,1,64,128]{3,2,1,0:T(8,128)S(1)}, u32[]{:S(2)}, u32[]{:S(2)}) %collective-permute-start.10) | collective-permute-done | bytes 163872 | tf_op jit(solution)/shard_map/ppermute | solution.py:52
  75.0 1.4 %fusion.679 = (f32[4,64,128]{2,1,0:T(8,128)S(1)}, f32[4,64,128]{2,1,0:T(8,128)S(1)}, f32[4,64,128]{2,1,0:T(8,128)S(1)}, f32[4,64,128]{2,1,0:T(8,128)S(1)}, f32[4...) fusion(f32[4,64,128]{2,1,0:T(8,128)S(1)} %get-tuple-element.63,, ...), kind=kLoop, calls=%fused_computation.883 | loop fusion | flops 5439488 | bytes 9334784 | tf_op jit(solution)/shard_map/add | solution.py:85
  77.7 7.4 %collective-permute-done.12 = f32[5,1,64,128]{3,2,1,0:T(8,128)S(1)} collective-permute-done((f32[5,1,64,128]{3,2,1,0:T(8,128)S(1)}, f32[5,1,64,128]{3,2,1,0:T(8,128)S(1)}, u32[]{:S(2)}, u32[]{:S(2)}) %collective-permute-start.12) | collective-permute-done | bytes 163872 | tf_op jit(solution)/shard_map/ppermute | solution.py:52
  85.6 2.6 %collective-permute-done.13 = f32[5,1,64,128]{3,2,1,0:T(8,128)S(1)} collective-permute-done((f32[5,1,64,128]{3,2,1,0:T(8,128)S(1)}, f32[5,1,64,128]{3,2,1,0:T(8,128)S(1)}, u32[]{:S(2)}, u32[]{:S(2)}) %collective-permute-start.13) | collective-permute-done | bytes 163872 | tf_op jit(solution)/shard_map/ppermute | solution.py:52
  90.1 1.3 %copy-done.1 = f32[19,4,64,128]{3,2,1,0:T(8,128)} copy-done((f32[19,4,64,128]{3,2,1,0:T(8,128)}, f32[19,4,64,128]{3,2,1,0:T(8,128)S(1)}, u32[]{:S(2)}) %copy-start.1) | copy-done | bytes 2490392
  91.5 0.8 constant_dynamic-update-slice_fusion.60
  (253 shorter events, 15.6 us)
Async XLA Ops:
  0.8 10.5 %collective-permute-start = (s32[1,128]{1,0:T(1,128)S(1)}, s32[1,128]{1,0:T(1,128)S(1)}, u32[]{:S(2)}, u32[]{:S(2)}) collective-permute-start(s32[1,128]{1,0:T(1,128)S(1)} %get-tuple-element.400), channel_id=1, source_target_pairs={{0,1},{1,2},{2,3},{3,4},{4,5},{5,6},{6,7},{7,8},{8,9},{9,10},{10,1... | collective-permute-start | bytes 1544 | tf_op jit(solution)/shard_map/ppermute | solution.py:43
  1.3 7.3 %copy-start = (f32[19,4,64,128]{3,2,1,0:T(8,128)S(1)}, f32[19,4,64,128]{3,2,1,0:T(8,128)}, u32[]{:S(2)}) copy-start(f32[19,4,64,128]{3,2,1,0:T(8,128)} %param.2) | copy-start | bytes 7471108
  1.3 10.0 %collective-permute-start.1 = (s32[1,128]{1,0:T(1,128)S(1)}, s32[1,128]{1,0:T(1,128)S(1)}, u32[]{:S(2)}, u32[]{:S(2)}) collective-permute-start(s32[1,128]{1,0:T(1,128)S(1)} %get-tuple-element.401), channel_id=1, source_target_pairs={{1,0},{2,1},{3,2},{4,3},{5,4},{6,5},{7,6},{8,7},{9,8},{10,9},{11,1... | collective-permute-start | bytes 1544 | tf_op jit(solution)/shard_map/ppermute | solution.py:44
  9.1 9.3 %collective-permute-start.3 = (f32[5,1,64,128]{3,2,1,0:T(8,128)S(1)}, f32[5,1,64,128]{3,2,1,0:T(8,128)S(1)}, u32[]{:S(2)}, u32[]{:S(2)}) collective-permute-start(f32[5,1,64,128]{3,2,1,0:T(8,128)S(1)} %get-tuple-element.303), channel_id=1, source_target_pairs={{1,0},{2,1},{3,2},{4,3},{5,4},{6,5},{7,6},{8,7},{9,8},{10,9},{11,1... | collective-permute-start | bytes 491528 | tf_op jit(solution)/shard_map/ppermute | solution.py:52
  9.8 7.4 %collective-permute-start.2 = (f32[5,1,64,128]{3,2,1,0:T(8,128)S(1)}, f32[5,1,64,128]{3,2,1,0:T(8,128)S(1)}, u32[]{:S(2)}, u32[]{:S(2)}) collective-permute-start(f32[5,1,64,128]{3,2,1,0:T(8,128)S(1)} %get-tuple-element.304), channel_id=1, source_target_pairs={{15,0},{0,1},{1,2},{2,3},{3,4},{4,5},{5,6},{6,7},{7,8},{8,9},{9,10... | collective-permute-start | bytes 491528 | tf_op jit(solution)/shard_map/ppermute | solution.py:52
  10.3 0.9 %copy-start.2 = (s32[4,128]{1,0:T(4,128)S(1)}, s32[4,128]{1,0:T(4,128)}, u32[]{:S(2)}) copy-start(s32[4,128]{1,0:T(4,128)} %param.3) | copy-start | bytes 6148
  21.0 7.6 %collective-permute-start.4 = (f32[5,1,64,128]{3,2,1,0:T(8,128)S(1)}, f32[5,1,64,128]{3,2,1,0:T(8,128)S(1)}, u32[]{:S(2)}, u32[]{:S(2)}) collective-permute-start(f32[5,1,64,128]{3,2,1,0:T(8,128)S(1)} %constant_dynamic-update-slice_fusion.10), channel_id=1, source_target_pairs={{15,0},{0,1},{1,2},{2,3},{3,4},{4,5},{5,6},{6,7},{7,8},{8,9},{9,10... | collective-permute-start | bytes 491528 | tf_op jit(solution)/shard_map/ppermute | solution.py:52
  29.3 2.9 %collective-permute-start.5 = (f32[5,1,64,128]{3,2,1,0:T(8,128)S(1)}, f32[5,1,64,128]{3,2,1,0:T(8,128)S(1)}, u32[]{:S(2)}, u32[]{:S(2)}) collective-permute-start(f32[5,1,64,128]{3,2,1,0:T(8,128)S(1)} %constant_dynamic-update-slice_fusion.15), channel_id=1, source_target_pairs={{1,0},{2,1},{3,2},{4,3},{5,4},{6,5},{7,6},{8,7},{9,8},{10,9},{11,1... | collective-permute-start | bytes 491528 | tf_op jit(solution)/shard_map/ppermute | solution.py:52
  34.3 7.9 %collective-permute-start.6 = (f32[5,1,64,128]{3,2,1,0:T(8,128)S(1)}, f32[5,1,64,128]{3,2,1,0:T(8,128)S(1)}, u32[]{:S(2)}, u32[]{:S(2)}) collective-permute-start(f32[5,1,64,128]{3,2,1,0:T(8,128)S(1)} %constant_dynamic-update-slice_fusion.20), channel_id=1, source_target_pairs={{15,0},{0,1},{1,2},{2,3},{3,4},{4,5},{5,6},{6,7},{7,8},{8,9},{9,10... | collective-permute-start | bytes 491528 | tf_op jit(solution)/shard_map/ppermute | solution.py:52
  42.9 3.1 %collective-permute-start.7 = (f32[5,1,64,128]{3,2,1,0:T(8,128)S(1)}, f32[5,1,64,128]{3,2,1,0:T(8,128)S(1)}, u32[]{:S(2)}, u32[]{:S(2)}) collective-permute-start(f32[5,1,64,128]{3,2,1,0:T(8,128)S(1)} %constant_dynamic-update-slice_fusion.25), channel_id=1, source_target_pairs={{1,0},{2,1},{3,2},{4,3},{5,4},{6,5},{7,6},{8,7},{9,8},{10,9},{11,1... | collective-permute-start | bytes 491528 | tf_op jit(solution)/shard_map/ppermute | solution.py:52
  48.1 7.9 %collective-permute-start.8 = (f32[5,1,64,128]{3,2,1,0:T(8,128)S(1)}, f32[5,1,64,128]{3,2,1,0:T(8,128)S(1)}, u32[]{:S(2)}, u32[]{:S(2)}) collective-permute-start(f32[5,1,64,128]{3,2,1,0:T(8,128)S(1)} %constant_dynamic-update-slice_fusion.30), channel_id=1, source_target_pairs={{15,0},{0,1},{1,2},{2,3},{3,4},{4,5},{5,6},{6,7},{7,8},{8,9},{9,10... | collective-permute-start | bytes 491528 | tf_op jit(solution)/shard_map/ppermute | solution.py:52
  56.7 2.9 %collective-permute-start.9 = (f32[5,1,64,128]{3,2,1,0:T(8,128)S(1)}, f32[5,1,64,128]{3,2,1,0:T(8,128)S(1)}, u32[]{:S(2)}, u32[]{:S(2)}) collective-permute-start(f32[5,1,64,128]{3,2,1,0:T(8,128)S(1)} %constant_dynamic-update-slice_fusion.35), channel_id=1, source_target_pairs={{1,0},{2,1},{3,2},{4,3},{5,4},{6,5},{7,6},{8,7},{9,8},{10,9},{11,1... | collective-permute-start | bytes 491528 | tf_op jit(solution)/shard_map/ppermute | solution.py:52
  62.6 7.5 %collective-permute-start.11 = (f32[5,1,64,128]{3,2,1,0:T(8,128)S(1)}, f32[5,1,64,128]{3,2,1,0:T(8,128)S(1)}, u32[]{:S(2)}, u32[]{:S(2)}) collective-permute-start(f32[5,1,64,128]{3,2,1,0:T(8,128)S(1)} %constant_dynamic-update-slice_fusion.45), channel_id=1, source_target_pairs={{1,0},{2,1},{3,2},{4,3},{5,4},{6,5},{7,6},{8,7},{9,8},{10,9},{11,1... | collective-permute-start | bytes 491528 | tf_op jit(solution)/shard_map/ppermute | solution.py:52
  67.3 7.5 %collective-permute-start.10 = (f32[5,1,64,128]{3,2,1,0:T(8,128)S(1)}, f32[5,1,64,128]{3,2,1,0:T(8,128)S(1)}, u32[]{:S(2)}, u32[]{:S(2)}) collective-permute-start(f32[5,1,64,128]{3,2,1,0:T(8,128)S(1)} %constant_dynamic-update-slice_fusion.40), channel_id=1, source_target_pairs={{15,0},{0,1},{1,2},{2,3},{3,4},{4,5},{5,6},{6,7},{7,8},{8,9},{9,10... | collective-permute-start | bytes 491528 | tf_op jit(solution)/shard_map/ppermute | solution.py:52
  77.6 7.6 %collective-permute-start.12 = (f32[5,1,64,128]{3,2,1,0:T(8,128)S(1)}, f32[5,1,64,128]{3,2,1,0:T(8,128)S(1)}, u32[]{:S(2)}, u32[]{:S(2)}) collective-permute-start(f32[5,1,64,128]{3,2,1,0:T(8,128)S(1)} %constant_dynamic-update-slice_fusion.50), channel_id=1, source_target_pairs={{15,0},{0,1},{1,2},{2,3},{3,4},{4,5},{5,6},{6,7},{7,8},{8,9},{9,10... | collective-permute-start | bytes 491528 | tf_op jit(solution)/shard_map/ppermute | solution.py:52
  85.3 2.9 %collective-permute-start.13 = (f32[5,1,64,128]{3,2,1,0:T(8,128)S(1)}, f32[5,1,64,128]{3,2,1,0:T(8,128)S(1)}, u32[]{:S(2)}, u32[]{:S(2)}) collective-permute-start(f32[5,1,64,128]{3,2,1,0:T(8,128)S(1)} %constant_dynamic-update-slice_fusion.55), channel_id=1, source_target_pairs={{1,0},{2,1},{3,2},{4,3},{5,4},{6,5},{7,6},{8,7},{9,8},{10,9},{11,1... | collective-permute-start | bytes 491528 | tf_op jit(solution)/shard_map/ppermute | solution.py:52
  90.0 1.5 %copy-start.1 = (f32[19,4,64,128]{3,2,1,0:T(8,128)}, f32[19,4,64,128]{3,2,1,0:T(8,128)S(1)}, u32[]{:S(2)}) copy-start(f32[19,4,64,128]{3,2,1,0:T(8,128)S(1)} %get-tuple-element.5) | copy-start | bytes 7471108
where the time goes:
time: 92.4 us; the launch traced here: 92.2 us
  waiting for transfers between devices  51 us (55%)
  other arithmetic  20.9 us (23%)
  starting transfers between devices  11.6 us (13%)
  local copies, waits for them, and re-layouts  6.85 us (7%)
  between operations  1.88 us (2%)
    ppermute x12, waiting for transfers between devices, passed_along(): return lax.ppermute(block, axis, route)  51 us
    add x17, other arithmetic, collide(): populations[component] + omega_rate * (equil - populations[component])  13.4 us
    ppermute x12, starting transfers between devices, passed_along(): return lax.ppermute(block, axis, route)  6.12 us
    ppermute x1, starting transfers between devices, padded(): after = lax.ppermute(initial, axis, down)  5.01 us
    slice x38, local copies, waits for them, and re-layouts, shift_local(): moved = jnp.roll(field, step_y, axis=2)  3.7 us
    add x2, other arithmetic, collide(): equil = density * (1.0 + 3.0 * along + 4.5 * along * along - 1.5 * speed_sq)  2.31 us
  transfers between devices with their start and end apart: 14, of which 11 were waited for; matrix products, arithmetic and copies ran while one was open for 10% of the time, Pallas kernels for 0%

commit v1 on v0

v1 whole, which is shorter than its diff:
```python
import functools

import jax
import jax.numpy as jnp
from jax import lax
from jax.experimental import pallas as pl
from jax.experimental.pallas import tpu as pltpu
from jax.sharding import PartitionSpec as P

STEPS = 6
Q = 19
SUB = 8

velocity_table = [
    (0, 0, 0),
    (1, 0, 0),
    (-1, 0, 0),
    (0, 1, 0),
    (0, -1, 0),
    (0, 0, 1),
    (0, 0, -1),
    (1, 1, 0),
    (-1, -1, 0),
    (1, -1, 0),
    (-1, 1, 0),
    (1, 0, 1),
    (-1, 0, -1),
    (1, 0, -1),
    (-1, 0, 1),
    (0, 1, 1),
    (0, -1, -1),
    (0, 1, -1),
    (0, -1, 1),
]
W0, W1, W2 = 1.0 / 3.0, 1.0 / 18.0, 1.0 / 36.0
OMEGA = 1.9
KEEP = OMEGA - 1.0
PLUS = [1, 7, 9, 11, 13]
MINUS = [2, 8, 10, 12, 14]
FLAT = [0, 3, 4, 5, 6, 15, 16, 17, 18]
NP = len(PLUS)


def opp(i):
    if i == 0:
        return 0
    return i + 1 if i % 2 == 1 else i - 1


def sums_plus(g):
    a, b, c, d, e = g
    x = W1 * a + W2 * ((b + c) + (d + e))
    return x, W2 * (b - c), W2 * (d - e)


def sums_flat(g):
    g0, g3, g4, g5, g6, g15, g16, g17, g18 = g
    s15, s17 = g15 + g16, g17 + g18
    d15, d17 = g15 - g16, g17 - g18
    rho = W0 * g0 + W1 * ((g3 + g4) + (g5 + g6)) + W2 * (s15 + s17)
    my = W1 * (g3 - g4) + W2 * (d15 + d17)
    mz = W1 * (g5 - g6) + W2 * (d15 - d17)
    return rho, my, mz


def equilibrium(rho, mx, my, mz):
    inv = 1.0 / rho
    k = 3.0 * OMEGA
    m = (mx * k, my * k, mz * k)
    half = inv * (1.5 / k)
    v = (m[0] * half, m[1] * half, m[2] * half)
    mv = m[0] * v[0] + m[1] * v[1] + m[2] * v[2]
    base = OMEGA * rho - mv * (1.0 / 3.0)
    return m, v, base


def along(c, m):
    total = None
    for step, value in zip(c, m):
        if step:
            if total is None:
                total = value if step == 1 else -value
            else:
                total = total + value if step == 1 else total - value
    return total


def collide_all(g):
    sp = sums_plus([g[i] for i in PLUS])
    sm = sums_plus([g[i] for i in MINUS])
    rho, my, mz = sums_flat([g[i] for i in FLAT])
    rho = rho + (sp[0] + sm[0])
    mx = sp[0] - sm[0]
    my = my + (sp[1] - sm[1])
    mz = mz + (sp[2] - sm[2])
    m, v, base = equilibrium(rho, mx, my, mz)
    post = [None] * Q
    post[0] = base - KEEP * g[0]
    for i in range(1, Q, 2):
        cm, cv = along(velocity_table[i], m), along(velocity_table[i], v)
        even = base + cm * cv
        post[i] = (even + cm) - KEEP * g[i]
        post[i + 1] = (even - cm) - KEEP * g[i + 1]
    return post


def collide_some(g, comps, rho, mx, my, mz):
    m, v, base = equilibrium(rho, mx, my, mz)
    post = []
    for value, i in zip(g, comps):
        first = i if i % 2 == 1 else i - 1
        cm, cv = along(velocity_table[first], m), along(velocity_table[first], v)
        even = base + cm * cv
        both = even + cm if i == first else even - cm
        post.append(both - KEEP * value)
    return post


class Field:
    def __init__(self, width, nz, edge, inner, low=None, high=None):
        self.width, self.nz = width, nz
        self.edge, self.inner, self.low, self.high = edge, inner, low, high

    def place(self, i, p):
        w, nz = self.width, self.nz
        if p == -1:
            ref, slot = self.low
            return ref, slot(i)
        if p == w:
            ref, slot = self.high
            return ref, slot(i)
        if p in (0, w - 1):
            return self.edge, SUB + (2 * i + (p != 0)) * nz
        return self.inner, SUB + (i * (w - 2) + p - 1) * nz

    def load(self, i, p, z, shift=0):
        ref, base = self.place(i, p)
        if shift == 0:
            return ref[pl.ds(pl.multiple_of(base + z, SUB), SUB), :]
        return ref[pl.ds(base + z - shift, SUB), :]

    def store(self, i, p, z, value):
        ref, base = self.place(i, p)
        ref[pl.ds(pl.multiple_of(base + z, SUB), SUB), :] = value


class Heights:
    def __init__(self, width, own, beside):
        self.width, self.own, self.beside = width, own, beside

    def get(self, p, roll):
        if p in (-1, self.width):
            row = (3 * (p != -1) + roll + 1) * SUB
            return self.beside[pl.ds(row, SUB), :]
        return self.own[pl.ds((3 * p + roll + 1) * SUB, SUB), :]


def roll_lanes(x, step):
    if step == 0:
        return x
    return pltpu.roll(x, step % x.shape[1], 1)


def levels(z, nz, ny):
    at = (lax.broadcasted_iota(jnp.int32, (SUB, ny), 0) + z).astype(jnp.float32)
    return {0: at, 1: at - 1.0, -1: jnp.where(at == nz - 1.0, -1.0, at + 1.0)}


def pull(field, heights, lev, i, p, z):
    cx, cy, cz = velocity_table[i]
    if i == 0:
        return field.load(0, p, z)
    moved = roll_lanes(field.load(i, p - cx, z, cz), cy)
    back = field.load(opp(i), p, z)
    return jnp.where(lev[cz] >= heights.get(p - cx, cy), moved, back)


def over_z(nz, body, unroll):
    blocks = nz // SUB

    def step(k, carry):
        body(pl.multiple_of(k * SUB, SUB))
        return carry

    lax.fori_loop(0, blocks, step, 0, unroll=min(unroll, blocks))


def first_edge_kernel(width, nz, pops, h, edge, up, down, own, buf, sem):
    ny = h.shape[1]
    copies = []
    for e, p in enumerate((0, width - 1)):
        copies.append(pltpu.make_async_copy(pops.at[:, p], buf.at[:, e], sem.at[e]))
        copies[-1].start()
    hf = h[...].astype(jnp.float32)
    for p in range(width):
        row = jnp.broadcast_to(hf[p : p + 1], (SUB, ny))
        for k in (-1, 0, 1):
            own[pl.ds((3 * p + k + 1) * SUB, SUB), :] = roll_lanes(row, k)
        if p == 0:
            down[pl.ds(NP * nz, SUB), :] = row
        if p == width - 1:
            up[pl.ds(NP * nz, SUB), :] = row
    field = Field(width, nz, edge, None)
    for c in copies:
        c.wait()

    def body(z):
        for e, p in enumerate((0, width - 1)):
            post = collide_all([buf[i, e, pl.ds(z, SUB), :] for i in range(Q)])
            for i in range(Q):
                field.store(i, p, z, post[i])
            send(post, p, width, nz, z, up, down)

    over_z(nz, body, UNROLL)


def send(post, p, width, nz, z, up, down):
    if p == 0:
        for k, i in enumerate(MINUS):
            down[pl.ds(pl.multiple_of(k * nz + z, SUB), SUB), :] = post[i]
    if p == width - 1:
        for k, i in enumerate(PLUS):
            up[pl.ds(pl.multiple_of(k * nz + z, SUB), SUB), :] = post[i]


def ahead(field, heights, lev, width, nz, z, up, down):
    for p, comps, out in ((width - 1, PLUS, up), (0, MINUS, down)):
        rows = [pull(field, heights, lev, i, p, z) for i in comps]
        rows += sums_flat([pull(field, heights, lev, i, p, z) for i in FLAT])
        for k, row in enumerate(rows):
            out[pl.ds(pl.multiple_of(k * nz + z, SUB), SUB), :] = row


def first_inner_kernel(width, nz, pops, own, edge, inner, up, down, buf, sem):
    ny = own.shape[1]
    copy = pltpu.make_async_copy(pops.at[:, 1 : width - 1], buf, sem)
    copy.start()
    field = Field(width, nz, edge, inner)
    heights = Heights(width, own, None)
    copy.wait()

    def body(z):
        for p in range(1, width - 1):
            post = collide_all([buf[i, p - 1, pl.ds(z, SUB), :] for i in range(Q)])
            for i in range(Q):
                field.store(i, p, z, post[i])

    over_z(nz, body, UNROLL)

    def body_ahead(z):
        ahead(field, heights, levels(z, nz, ny), width, nz, z, up, down)

    over_z(nz, body_ahead, UNROLL)


def inner_step(width, nz, field, new, heights, ny):
    def body(z):
        lev = levels(z, nz, ny)
        for p in range(1, width - 1):
            post = collide_all([pull(field, heights, lev, i, p, z) for i in range(Q)])
            for i in range(Q):
                new.store(i, p, z, post[i])

    over_z(nz, body, UNROLL)


def inner_kernel(width, nz, own, edge, inner, new_inner):
    field = Field(width, nz, edge, inner)
    inner_step(width, nz, field, Field(width, nz, None, new_inner), Heights(width, own, None), own.shape[1])


def inner_ahead_kernel(width, nz, own, edge, inner, new_edge, new_inner, up, down):
    ny = own.shape[1]
    heights = Heights(width, own, None)
    new = Field(width, nz, new_edge, new_inner)
    inner_step(width, nz, Field(width, nz, edge, inner), new, heights, ny)

    def body_ahead(z):
        ahead(new, heights, levels(z, nz, ny), width, nz, z, up, down)

    over_z(nz, body_ahead, UNROLL)


def slot_of(comps, nz, base=0):
    return lambda i: base + comps.index(i) * nz


def padded_low(nz, from_low, from_high, low, high):
    rows = NP * nz
    low[pl.ds(SUB, rows), :] = from_low[pl.ds(0, rows), :]
    high[pl.ds(SUB, rows), :] = from_high[pl.ds(0, rows), :]


def edge_kernel(first, width, nz, *refs):
    ny = refs[0].shape[1]
    if first:
        own, edge, inner, from_low, from_high, new_edge, sums_low, sums_high, beside, low, high = refs
        for s, ref in enumerate((from_low, from_high)):
            row = ref[pl.ds(NP * nz, SUB), :]
            for k in (-1, 0, 1):
                beside[pl.ds((3 * s + k + 1) * SUB, SUB), :] = roll_lanes(row, k)
    else:
        own, beside, edge, inner, from_low, from_high, new_edge, sums_low, sums_high, low, high = refs
    padded_low(nz, from_low, from_high, low, high)
    field = Field(
        width,
        nz,
        edge,
        inner,
        (low, slot_of(PLUS, nz, SUB)),
        (high, slot_of(MINUS, nz, SUB)),
    )
    heights = Heights(width, own, beside)
    new = Field(width, nz, new_edge, None)

    def body(z):
        lev = levels(z, nz, ny)
        for p in (0, width - 1):
            post = collide_all([pull(field, heights, lev, i, p, z) for i in range(Q)])
            for i in range(Q):
                new.store(i, p, z, post[i])
        for p, comps, out in ((-1, MINUS, sums_low), (width, PLUS, sums_high)):
            totals = sums_plus([pull(field, heights, lev, i, p, z) for i in comps])
            for k, row in enumerate(totals):
                out[pl.ds(pl.multiple_of(k * nz + z, SUB), SUB), :] = row

    over_z(nz, body, UNROLL)


def halo(nz, got, sums, sign, out):
    comps = PLUS if sign > 0 else MINUS

    def body(z):
        def row(ref, k):
            return ref[pl.ds(pl.multiple_of(k * nz + z, SUB), SUB), :]

        g = [row(got, k) for k in range(NP)]
        x, y1, z1 = sums_plus(g)
        x2, y2, z2 = (row(sums, k) for k in range(3))
        rho = row(got, NP) + (x + x2)
        mx = (x - x2) * sign if sign < 0 else x - x2
        my = row(got, NP + 1) + ((y1 - y2) if sign > 0 else (y2 - y1))
        mz = row(got, NP + 2) + ((z1 - z2) if sign > 0 else (z2 - z1))
        post = collide_some(g, comps, rho, mx, my, mz)
        for k in range(NP):
            out[pl.ds(pl.multiple_of(SUB + k * nz + z, SUB), SUB), :] = post[k]

    over_z(nz, body, UNROLL)


def halo_field(width, nz, edge, inner, got_low, got_high, sums_low, sums_high, low, high):
    halo(nz, got_low, sums_low, 1, low)
    halo(nz, got_high, sums_high, -1, high)
    return Field(
        width,
        nz,
        edge,
        inner,
        (low, slot_of(PLUS, nz, SUB)),
        (high, slot_of(MINUS, nz, SUB)),
    )


def next_edge_kernel(
    width, nz, own, beside, edge, inner, got_low, got_high, sums_low, sums_high, new_edge, up, down, low, high
):
    ny = own.shape[1]
    field = halo_field(width, nz, edge, inner, got_low, got_high, sums_low, sums_high, low, high)
    heights = Heights(width, own, beside)
    new = Field(width, nz, new_edge, None)

    def body(z):
        lev = levels(z, nz, ny)
        for p in (0, width - 1):
            post = collide_all([pull(field, heights, lev, i, p, z) for i in range(Q)])
            for i in range(Q):
                new.store(i, p, z, post[i])
            send(post, p, width, nz, z, up, down)

    over_z(nz, body, UNROLL)
    zero = jnp.zeros((SUB, ny), jnp.float32)
    up[pl.ds(NP * nz, SUB), :] = zero
    down[pl.ds(NP * nz, SUB), :] = zero


def write_planes(field, heights, nz, ny, planes, out, buf, sem):
    copies = []
    for k, p in enumerate(planes):

        def body(z, p=p, k=k):
            lev = levels(z, nz, ny)
            for i in range(Q):
                buf[i, k, pl.ds(z, SUB), :] = pull(field, heights, lev, i, p, z)

        over_z(nz, body, UNROLL)
        copies.append(pltpu.make_async_copy(buf.at[:, k], out.at[:, p], sem.at[k]))
        copies[-1].start()
    for c in copies:
        c.wait()


def last_inner_kernel(width, nz, own, edge, inner, out, buf, sem):
    field = Field(width, nz, edge, inner)
    write_planes(field, Heights(width, own, None), nz, own.shape[1], range(1, width - 1), out, buf, sem)


def last_edge_kernel(
    width,
    nz,
    own,
    beside,
    edge,
    inner,
    got_low,
    got_high,
    sums_low,
    sums_high,
    _,
    out,
    low,
    high,
    buf,
    sem,
):
    field = halo_field(width, nz, edge, inner, got_low, got_high, sums_low, sums_high, low, high)
    write_planes(field, Heights(width, own, beside), nz, own.shape[1], (0, width - 1), out, buf, sem)


UNROLL = 2
VMEM_LIMIT = 24 * 1024 * 1024


def per_device(pops, heights):
    _, width, nz, ny = pops.shape
    assert width >= 3 and nz % SUB == 0 and STEPS % 2 == 0
    devices = lax.axis_size("gx")
    to_up = [(i, (i + 1) % devices) for i in range(devices)]
    to_down = [(j, i) for i, j in to_up]

    def rows(n):
        return jax.ShapeDtypeStruct((n, ny), jnp.float32)

    vmem = pl.BlockSpec(memory_space=pltpu.VMEM)
    anywhere = pl.BlockSpec(memory_space=pl.ANY)
    edge_t = rows(Q * 2 * nz + 2 * SUB)
    inner_t = rows(Q * (width - 2) * nz + 2 * SUB)
    near_t = rows(NP * nz + SUB)
    far_t = rows((NP + 3) * nz)
    sums_t = rows(3 * nz)
    own_t = rows(3 * width * SUB)
    beside_t = rows(6 * SUB)
    halo_scratch = [pltpu.VMEM((NP * nz + 2 * SUB, ny), jnp.float32)] * 2

    def call(kernel, name, in_specs, outs, planes, scratch=(), out_specs=None, **kw):
        return pl.pallas_call(
            functools.partial(kernel, width, nz),
            out_shape=outs,
            in_specs=in_specs,
            out_specs=[vmem] * len(outs) if out_specs is None else out_specs,
            scratch_shapes=list(scratch),
            name=name,
            compiler_params=pltpu.CompilerParams(vmem_limit_bytes=VMEM_LIMIT),
            cost_estimate=pl.CostEstimate(
                flops=planes * nz * ny * 250, bytes_accessed=planes * nz * ny * 4 * Q * 2, transcendentals=0
            ),
            **kw,
        )

    def exchange(up, down):
        return lax.ppermute(up, "gx", to_up), lax.ppermute(down, "gx", to_down)

    dma = pltpu.SemaphoreType.DMA
    edge, up, down, own = call(
        first_edge_kernel,
        "first_edge",
        [anywhere, vmem],
        [edge_t, near_t, near_t, own_t],
        2,
        [pltpu.VMEM((Q, 2, nz, ny), jnp.float32), dma((2,))],
    )(pops, heights)
    near = exchange(up, down)
    inner, up, down = call(
        first_inner_kernel,
        "first_inner",
        [anywhere, vmem, vmem],
        [inner_t, far_t, far_t],
        width - 1,
        [pltpu.VMEM((Q, width - 2, nz, ny), jnp.float32), dma],
    )(pops, own, edge)
    far = exchange(up, down)
    beside = None
    for t in range(0, STEPS, 2):
        last = t + 2 == STEPS
        inner1 = call(inner_kernel, "inner", [vmem] * 3, [inner_t], width - 2)(own, edge, inner)[0]
        if t == 0:
            edge1, sums_low, sums_high, beside = call(
                functools.partial(edge_kernel, True),
                "edge_first",
                [vmem] * 5,
                [edge_t, sums_t, sums_t, beside_t],
                3,
                halo_scratch,
            )(own, edge, inner, *near)
        else:
            edge1, sums_low, sums_high = call(
                functools.partial(edge_kernel, False),
                "edge",
                [vmem] * 6,
                [edge_t, sums_t, sums_t],
                3,
                halo_scratch,
            )(own, beside, edge, inner, *near)
        if last:
            break
        edge, up, down = call(
            next_edge_kernel, "next_edge", [vmem] * 8, [edge_t, near_t, near_t], 3, halo_scratch
        )(own, beside, edge1, inner1, *far, sums_low, sums_high)
        near = exchange(up, down)
        inner, up, down = call(
            inner_ahead_kernel, "inner_ahead", [vmem] * 4, [inner_t, far_t, far_t], width - 1
        )(own, edge1, inner1, edge)
        far = exchange(up, down)
    out_t = jax.ShapeDtypeStruct(pops.shape, pops.dtype)
    out = call(
        last_inner_kernel,
        "last_inner",
        [vmem] * 3,
        [out_t],
        width - 2,
        [pltpu.VMEM((Q, width - 2, nz, ny), jnp.float32), dma((width - 2,))],
        out_specs=[anywhere],
    )(own, edge1, inner1)[0]
    return call(
        last_edge_kernel,
        "last_edge",
        [vmem] * 8 + [anywhere],
        [out_t],
        3,
        halo_scratch + [pltpu.VMEM((Q, 2, nz, ny), jnp.float32), dma((2,))],
        out_specs=[anywhere],
        input_output_aliases={8: 0},
    )(own, beside, edge1, inner1, *far, sums_low, sums_high, out)[0]


def solution(mesh):
    placed = (P(None, ("dir", "gx"), None, None), P(("dir", "gx"), None))
    return jax.shard_map(
        per_device,
        mesh=mesh,
        in_specs=placed,
        out_specs=P(None, ("dir", "gx"), None, None),
        check_vma=False,
    )
```

time: 92.4 us -> 53.9 us (0.58)
  the two profiles are of different devices: /device:TPU:0 before, /device:TPU:1 now
where the time goes in v1:
time: 53.9 us; the launch traced here: 53.8 us
  waiting for transfers between devices  26 us (48%)
  Pallas kernels  14 us (26%)
  starting transfers between devices  11.2 us (21%)
  local copies, waits for them, and re-layouts  2.38 us (4%)
    ppermute x12, waiting for transfers between devices, exchange(): return (lax.ppermute(up, 'gx', to_up), lax.ppermute(down, 'gx', to_down))  26 us
    ppermute x12, starting transfers between devices, exchange(): return (lax.ppermute(up, 'gx', to_up), lax.ppermute(down, 'gx', to_down))  11.2 us
    unnamed x4, local copies, waits for them, and re-layouts  2.38 us
    pallas_call x2, Pallas kernels, per_device(): call(inner_ahead_kernel, 'inner_ahead', [vmem] * 4, [inner_t, far_t, far_...  2.35 us
    pallas_call x3, Pallas kernels, per_device(): call(inner_kernel, 'inner', [vmem] * 3, [inner_t], width - 2)  2.26 us
    pallas_call x2, Pallas kernels, per_device(): call(next_edge_kernel, 'next_edge', [vmem] * 8, [edge_t, near_t, near_t],...  1.99 us
    pallas_call x1, Pallas kernels, per_device(): call(last_edge_kernel, 'last_edge', [vmem] * 8 + [anywhere], [out_t], 3,...  1.81 us
    pallas_call x1, Pallas kernels, per_device(): call(last_inner_kernel, 'last_inner', [vmem] * 3, [out_t], width - 2, [pl...  1.59 us
  transfers between devices with their start and end apart: 12, of which 6 were waited for; matrix products, arithmetic and copies ran while one was open for 0% of the time, Pallas kernels for 12%

profile of v1, /device:TPU:1, one launch (start us, length us, event | category | flops | bytes accessed | tf_op | source)
XLA Modules:
  0.0 53.8 jit_solution(12157482765038657400)
XLA Ops:
  0.0 1.7 %copy-done = f32[19,4,64,128]{3,2,1,0:T(8,128)S(1)} copy-done((f32[19,4,64,128]{3,2,1,0:T(8,128)S(1)}, f32[19,4,64,128]{3,2,1,0:T(8,128)}, u32[]{:S(2)}) %copy-start) | copy-done | bytes 2490392
  3.0 1.0 %first_inner.1 = (f32[2448,128]{1,0:T(8,128)S(1)}, f32[512,128]{1,0:T(8,128)S(1)}, f32[512,128]{1,0:T(8,128)S(1)}) custom-call(f32[19,4,64,128]{3,2,1,0:T(8,128)S(1)} %copy-done, f32[96,128]{1,0:T(8,128)S(1)} %get-tuple-element.34.own.refs_0_, f32[2448,128]{1,0:T(8,128)S(1)} %get-tuple-element.35.edge.refs_1_), custom_call_target="tpu_custom_call" | custom-call | flops 6144000 | bytes 3735552 | tf_op jit(solution)/shard_map/first_inner/pallas_call | solution.py:482
  4.0 2.7 %collective-permute-start.2 = (f32[512,128]{1,0:T(8,128)S(1)}, f32[512,128]{1,0:T(8,128)S(1)}, u32[]{:S(2)}, u32[]{:S(2)}) collective-permute-start(f32[512,128]{1,0:T(8,128)S(1)} %get-tuple-element.41), channel_id=1, source_target_pairs={{0,1},{1,2},{2,3},{3,4},{4,5},{5,6},{6,7},{7,8},{8,9},{9,10},{10,1... | collective-permute-start | bytes 786440 | tf_op jit(solution)/shard_map/ppermute | solution.py:470
  6.6 1.7 %collective-permute-start = (f32[328,128]{1,0:T(8,128)S(1)}, f32[328,128]{1,0:T(8,128)S(1)}, u32[]{:S(2)}, u32[]{:S(2)}) collective-permute-start(f32[328,128]{1,0:T(8,128)S(1)} %get-tuple-element.37), channel_id=1, source_target_pairs={{0,1},{1,2},{2,3},{3,4},{4,5},{5,6},{6,7},{7,8},{8,9},{9,10},{10,1... | collective-permute-start | bytes 503816 | tf_op jit(solution)/shard_map/ppermute | solution.py:470
  8.4 1.2 %collective-permute-start.1 = (f32[328,128]{1,0:T(8,128)S(1)}, f32[328,128]{1,0:T(8,128)S(1)}, u32[]{:S(2)}, u32[]{:S(2)}) collective-permute-start(f32[328,128]{1,0:T(8,128)S(1)} %get-tuple-element.38), channel_id=1, source_target_pairs={{1,0},{2,1},{3,2},{4,3},{5,4},{6,5},{7,6},{8,7},{9,8},{10,9},{11,1... | collective-permute-start | bytes 503816 | tf_op jit(solution)/shard_map/ppermute | solution.py:470
  10.3 6.0 %collective-permute-done.refs_3_ = f32[328,128]{1,0:T(8,128)S(1)} collective-permute-done((f32[328,128]{1,0:T(8,128)S(1)}, f32[328,128]{1,0:T(8,128)S(1)}, u32[]{:S(2)}, u32[]{:S(2)}) %collective-permute-start) | collective-permute-done | bytes 167968 | tf_op jit(solution)/shard_map/ppermute | solution.py:470
  16.4 2.5 %collective-permute-done.1.refs_4_ = f32[328,128]{1,0:T(8,128)S(1)} collective-permute-done((f32[328,128]{1,0:T(8,128)S(1)}, f32[328,128]{1,0:T(8,128)S(1)}, u32[]{:S(2)}, u32[]{:S(2)}) %collective-permute-start.1) | collective-permute-done | bytes 167968 | tf_op jit(solution)/shard_map/ppermute | solution.py:470
  18.8 0.8 %edge_first.1 = (f32[2448,128]{1,0:T(8,128)S(1)}, f32[192,128]{1,0:T(8,128)S(1)}, f32[192,128]{1,0:T(8,128)S(1)}, f32[48,128]{1,0:T(8,128)S(1)}) custom-call(f32[96,128]{1,0:T(8,128)S(1)} %get-tuple-element.34.own.refs_0_, f32[2448,128]{1,0:T(8,128)S(1)} %get-tuple-element.35.edge.refs_1_, f32[2448,128]{1,0:T(8,128)S(1)} %get-tuple-element.36.refs_2_.inner, ...), custom_call_target="tpu_custom_call" | custom-call | flops 6144000 | bytes 3735552 | tf_op jit(solution)/shard_map/edge_first/pallas_call | solution.py:496
  19.7 1.0 %next_edge.2 = (f32[2448,128]{1,0:T(8,128)S(1)}, f32[328,128]{1,0:T(8,128)S(1)}, f32[328,128]{1,0:T(8,128)S(1)}) custom-call(f32[96,128]{1,0:T(8,128)S(1)} %get-tuple-element.34.own.refs_0_, f32[48,128]{1,0:T(8,128)S(1)} %get-tuple-element.39.beside.refs_1_, f32[2448,128]{1,0:T(8,128)S(1)} %get-tuple-element.40.edge, f32[2448,128]{1,0:T(8,128)S(1)} %inner.3, ...), custom_call_target="tpu_custom_call" | custom-call | flops 6144000 | bytes 3735552 | tf_op jit(solution)/shard_map/next_edge/pallas_call | solution.py:515
  20.7 1.2 %inner_ahead.2 = (f32[2448,128]{1,0:T(8,128)S(1)}, f32[512,128]{1,0:T(8,128)S(1)}, f32[512,128]{1,0:T(8,128)S(1)}) custom-call(f32[96,128]{1,0:T(8,128)S(1)} %get-tuple-element.34.own.refs_0_, f32[2448,128]{1,0:T(8,128)S(1)} %get-tuple-element.40.edge, f32[2448,128]{1,0:T(8,128)S(1)} %inner.3, f32[2448,128]{1,0:T(8,128)S(1)} %get-tuple-element.45.new_edge.refs_2_.edge), custom_call_target="tpu_custom_call" | custom-call | flops 6144000 | bytes 3735552 | tf_op jit(solution)/shard_map/inner_ahead/pallas_call | solution.py:519
  22.5 1.3 %collective-permute-start.4 = (f32[328,128]{1,0:T(8,128)S(1)}, f32[328,128]{1,0:T(8,128)S(1)}, u32[]{:S(2)}, u32[]{:S(2)}) collective-permute-start(f32[328,128]{1,0:T(8,128)S(1)} %get-tuple-element.47), channel_id=1, source_target_pairs={{0,1},{1,2},{2,3},{3,4},{4,5},{5,6},{6,7},{7,8},{8,9},{9,10},{10,1... | collective-permute-start | bytes 503816 | tf_op jit(solution)/shard_map/ppermute | solution.py:470
  23.8 1.0 %collective-permute-start.5 = (f32[328,128]{1,0:T(8,128)S(1)}, f32[328,128]{1,0:T(8,128)S(1)}, u32[]{:S(2)}, u32[]{:S(2)}) collective-permute-start(f32[328,128]{1,0:T(8,128)S(1)} %get-tuple-element.48), channel_id=1, source_target_pairs={{1,0},{2,1},{3,2},{4,3},{5,4},{6,5},{7,6},{8,7},{9,8},{10,9},{11,1... | collective-permute-start | bytes 503816 | tf_op jit(solution)/shard_map/ppermute | solution.py:470
  25.5 6.1 %collective-permute-done.4.refs_4_ = f32[328,128]{1,0:T(8,128)S(1)} collective-permute-done((f32[328,128]{1,0:T(8,128)S(1)}, f32[328,128]{1,0:T(8,128)S(1)}, u32[]{:S(2)}, u32[]{:S(2)}) %collective-permute-start.4) | collective-permute-done | bytes 167968 | tf_op jit(solution)/shard_map/ppermute | solution.py:470
  31.7 2.5 %collective-permute-done.5.refs_5_ = f32[328,128]{1,0:T(8,128)S(1)} collective-permute-done((f32[328,128]{1,0:T(8,128)S(1)}, f32[328,128]{1,0:T(8,128)S(1)}, u32[]{:S(2)}, u32[]{:S(2)}) %collective-permute-start.5) | collective-permute-done | bytes 167968 | tf_op jit(solution)/shard_map/ppermute | solution.py:470
  34.2 0.8 %edge.2 = (f32[2448,128]{1,0:T(8,128)S(1)}, f32[192,128]{1,0:T(8,128)S(1)}, f32[192,128]{1,0:T(8,128)S(1)}) custom-call(f32[96,128]{1,0:T(8,128)S(1)} %get-tuple-element.34.own.refs_0_, f32[48,128]{1,0:T(8,128)S(1)} %get-tuple-element.39.beside.refs_1_, f32[2448,128]{1,0:T(8,128)S(1)} %get-tuple-element.45.new_edge.refs_2_.edge, ...), custom_call_target="tpu_custom_call" | custom-call | flops 6144000 | bytes 3735552 | tf_op jit(solution)/shard_map/edge/pallas_call | solution.py:505
  35.0 1.0 %next_edge.3 = (f32[2448,128]{1,0:T(8,128)S(1)}, f32[328,128]{1,0:T(8,128)S(1)}, f32[328,128]{1,0:T(8,128)S(1)}) custom-call(f32[96,128]{1,0:T(8,128)S(1)} %get-tuple-element.34.own.refs_0_, f32[48,128]{1,0:T(8,128)S(1)} %get-tuple-element.39.beside.refs_1_, f32[2448,128]{1,0:T(8,128)S(1)} %get-tuple-element.49.edge, f32[2448,128]{1,0:T(8,128)S(1)} %inner.4, ...), custom_call_target="tpu_custom_call" | custom-call | flops 6144000 | bytes 3735552 | tf_op jit(solution)/shard_map/next_edge/pallas_call | solution.py:515
  36.0 1.2 %inner_ahead.3 = (f32[2448,128]{1,0:T(8,128)S(1)}, f32[512,128]{1,0:T(8,128)S(1)}, f32[512,128]{1,0:T(8,128)S(1)}) custom-call(f32[96,128]{1,0:T(8,128)S(1)} %get-tuple-element.34.own.refs_0_, f32[2448,128]{1,0:T(8,128)S(1)} %get-tuple-element.49.edge, f32[2448,128]{1,0:T(8,128)S(1)} %inner.4, f32[2448,128]{1,0:T(8,128)S(1)} %get-tuple-element.54.new_edge.refs_2_.edge), custom_call_target="tpu_custom_call" | custom-call | flops 6144000 | bytes 3735552 | tf_op jit(solution)/shard_map/inner_ahead/pallas_call | solution.py:519
  37.8 1.3 %collective-permute-start.8 = (f32[328,128]{1,0:T(8,128)S(1)}, f32[328,128]{1,0:T(8,128)S(1)}, u32[]{:S(2)}, u32[]{:S(2)}) collective-permute-start(f32[328,128]{1,0:T(8,128)S(1)} %get-tuple-element.56), channel_id=1, source_target_pairs={{0,1},{1,2},{2,3},{3,4},{4,5},{5,6},{6,7},{7,8},{8,9},{9,10},{10,1... | collective-permute-start | bytes 503816 | tf_op jit(solution)/shard_map/ppermute | solution.py:470
  39.1 0.8 %collective-permute-start.9 = (f32[328,128]{1,0:T(8,128)S(1)}, f32[328,128]{1,0:T(8,128)S(1)}, u32[]{:S(2)}, u32[]{:S(2)}) collective-permute-start(f32[328,128]{1,0:T(8,128)S(1)} %get-tuple-element.57), channel_id=1, source_target_pairs={{1,0},{2,1},{3,2},{4,3},{5,4},{6,5},{7,6},{8,7},{9,8},{10,9},{11,1... | collective-permute-start | bytes 503816 | tf_op jit(solution)/shard_map/ppermute | solution.py:470
  40.7 5.5 %collective-permute-done.8.refs_4_ = f32[328,128]{1,0:T(8,128)S(1)} collective-permute-done((f32[328,128]{1,0:T(8,128)S(1)}, f32[328,128]{1,0:T(8,128)S(1)}, u32[]{:S(2)}, u32[]{:S(2)}) %collective-permute-start.8) | collective-permute-done | bytes 167968 | tf_op jit(solution)/shard_map/ppermute | solution.py:470
  46.2 3.4 %collective-permute-done.9.refs_5_ = f32[328,128]{1,0:T(8,128)S(1)} collective-permute-done((f32[328,128]{1,0:T(8,128)S(1)}, f32[328,128]{1,0:T(8,128)S(1)}, u32[]{:S(2)}, u32[]{:S(2)}) %collective-permute-start.9) | collective-permute-done | bytes 167968 | tf_op jit(solution)/shard_map/ppermute | solution.py:470
  49.5 0.8 %edge.3 = (f32[2448,128]{1,0:T(8,128)S(1)}, f32[192,128]{1,0:T(8,128)S(1)}, f32[192,128]{1,0:T(8,128)S(1)}) custom-call(f32[96,128]{1,0:T(8,128)S(1)} %get-tuple-element.34.own.refs_0_, f32[48,128]{1,0:T(8,128)S(1)} %get-tuple-element.39.beside.refs_1_, f32[2448,128]{1,0:T(8,128)S(1)} %get-tuple-element.54.new_edge.refs_2_.edge, ...), custom_call_target="tpu_custom_call" | custom-call | flops 6144000 | bytes 3735552 | tf_op jit(solution)/shard_map/edge/pallas_call | solution.py:505
  50.3 1.6 %last_inner.1._ = f32[19,4,64,128]{3,2,1,0:T(8,128)} custom-call(f32[96,128]{1,0:T(8,128)S(1)} %get-tuple-element.34.own.refs_0_, f32[2448,128]{1,0:T(8,128)S(1)} %get-tuple-element.58.edge, f32[2448,128]{1,0:T(8,128)S(1)} %inner.5), custom_call_target="tpu_custom_call" | custom-call | flops 4096000 | bytes 2490368 | tf_op jit(solution)/shard_map/last_inner/pallas_call | solution.py:524
  51.9 1.8 %last_edge.1 = f32[19,4,64,128]{3,2,1,0:T(8,128)} custom-call(f32[96,128]{1,0:T(8,128)S(1)} %get-tuple-element.34.own.refs_0_, f32[48,128]{1,0:T(8,128)S(1)} %get-tuple-element.39.beside.refs_1_, f32[2448,128]{1,0:T(8,128)S(1)} %get-tuple-element.58.edge, f32[2448,128]{1,0:T(8,128)S(1)} %inner.5, ...), custom_call_target="tpu_custom_call", output_to_operand_aliasing={{}: (8, {})} | custom-call | flops 6144000 | bytes 3735552 | tf_op jit(solution)/shard_map/last_edge/pallas_call | solution.py:533
  (18 shorter events, 4.7 us)
Async XLA Ops:
  0.0 1.7 %copy-start = (f32[19,4,64,128]{3,2,1,0:T(8,128)S(1)}, f32[19,4,64,128]{3,2,1,0:T(8,128)}, u32[]{:S(2)}) copy-start(f32[19,4,64,128]{3,2,1,0:T(8,128)} %pops.3) | copy-start | bytes 7471108
  1.7 0.7 %copy-start.1 = (s32[4,128]{1,0:T(4,128)S(1)}, s32[4,128]{1,0:T(4,128)}, u32[]{:S(2)}) copy-start(s32[4,128]{1,0:T(4,128)} %h.1) | copy-start | bytes 6148
  4.0 15.7 %collective-permute-start.2 = (f32[512,128]{1,0:T(8,128)S(1)}, f32[512,128]{1,0:T(8,128)S(1)}, u32[]{:S(2)}, u32[]{:S(2)}) collective-permute-start(f32[512,128]{1,0:T(8,128)S(1)} %get-tuple-element.41), channel_id=1, source_target_pairs={{0,1},{1,2},{2,3},{3,4},{4,5},{5,6},{6,7},{7,8},{8,9},{9,10},{10,1... | collective-permute-start | bytes 786440 | tf_op jit(solution)/shard_map/ppermute | solution.py:470
  6.6 13.1 %collective-permute-start.3 = (f32[512,128]{1,0:T(8,128)S(1)}, f32[512,128]{1,0:T(8,128)S(1)}, u32[]{:S(2)}, u32[]{:S(2)}) collective-permute-start(f32[512,128]{1,0:T(8,128)S(1)} %get-tuple-element.42), channel_id=1, source_target_pairs={{1,0},{2,1},{3,2},{4,3},{5,4},{6,5},{7,6},{8,7},{9,8},{10,9},{11,1... | collective-permute-start | bytes 786440 | tf_op jit(solution)/shard_map/ppermute | solution.py:470
  6.6 9.7 %collective-permute-start = (f32[328,128]{1,0:T(8,128)S(1)}, f32[328,128]{1,0:T(8,128)S(1)}, u32[]{:S(2)}, u32[]{:S(2)}) collective-permute-start(f32[328,128]{1,0:T(8,128)S(1)} %get-tuple-element.37), channel_id=1, source_target_pairs={{0,1},{1,2},{2,3},{3,4},{4,5},{5,6},{6,7},{7,8},{8,9},{9,10},{10,1... | collective-permute-start | bytes 503816 | tf_op jit(solution)/shard_map/ppermute | solution.py:470
  8.4 10.5 %collective-permute-start.1 = (f32[328,128]{1,0:T(8,128)S(1)}, f32[328,128]{1,0:T(8,128)S(1)}, u32[]{:S(2)}, u32[]{:S(2)}) collective-permute-start(f32[328,128]{1,0:T(8,128)S(1)} %get-tuple-element.38), channel_id=1, source_target_pairs={{1,0},{2,1},{3,2},{4,3},{5,4},{6,5},{7,6},{8,7},{9,8},{10,9},{11,1... | collective-permute-start | bytes 503816 | tf_op jit(solution)/shard_map/ppermute | solution.py:470
  21.9 13.1 %collective-permute-start.6 = (f32[512,128]{1,0:T(8,128)S(1)}, f32[512,128]{1,0:T(8,128)S(1)}, u32[]{:S(2)}, u32[]{:S(2)}) collective-permute-start(f32[512,128]{1,0:T(8,128)S(1)} %get-tuple-element.50), channel_id=1, source_target_pairs={{0,1},{1,2},{2,3},{3,4},{4,5},{5,6},{6,7},{7,8},{8,9},{9,10},{10,1... | collective-permute-start | bytes 786440 | tf_op jit(solution)/shard_map/ppermute | solution.py:470
  22.0 13.1 %collective-permute-start.7 = (f32[512,128]{1,0:T(8,128)S(1)}, f32[512,128]{1,0:T(8,128)S(1)}, u32[]{:S(2)}, u32[]{:S(2)}) collective-permute-start(f32[512,128]{1,0:T(8,128)S(1)} %get-tuple-element.51), channel_id=1, source_target_pairs={{1,0},{2,1},{3,2},{4,3},{5,4},{6,5},{7,6},{8,7},{9,8},{10,9},{11,1... | collective-permute-start | bytes 786440 | tf_op jit(solution)/shard_map/ppermute | solution.py:470
  22.5 9.2 %collective-permute-start.4 = (f32[328,128]{1,0:T(8,128)S(1)}, f32[328,128]{1,0:T(8,128)S(1)}, u32[]{:S(2)}, u32[]{:S(2)}) collective-permute-start(f32[328,128]{1,0:T(8,128)S(1)} %get-tuple-element.47), channel_id=1, source_target_pairs={{0,1},{1,2},{2,3},{3,4},{4,5},{5,6},{6,7},{7,8},{8,9},{9,10},{10,1... | collective-permute-start | bytes 503816 | tf_op jit(solution)/shard_map/ppermute | solution.py:470
  23.8 10.5 %collective-permute-start.5 = (f32[328,128]{1,0:T(8,128)S(1)}, f32[328,128]{1,0:T(8,128)S(1)}, u32[]{:S(2)}, u32[]{:S(2)}) collective-permute-start(f32[328,128]{1,0:T(8,128)S(1)} %get-tuple-element.48), channel_id=1, source_target_pairs={{1,0},{2,1},{3,2},{4,3},{5,4},{6,5},{7,6},{8,7},{9,8},{10,9},{11,1... | collective-permute-start | bytes 503816 | tf_op jit(solution)/shard_map/ppermute | solution.py:470
  37.2 14.7 %collective-permute-start.10 = (f32[512,128]{1,0:T(8,128)S(1)}, f32[512,128]{1,0:T(8,128)S(1)}, u32[]{:S(2)}, u32[]{:S(2)}) collective-permute-start(f32[512,128]{1,0:T(8,128)S(1)} %get-tuple-element.59), channel_id=1, source_target_pairs={{0,1},{1,2},{2,3},{3,4},{4,5},{5,6},{6,7},{7,8},{8,9},{9,10},{10,1... | collective-permute-start | bytes 786440 | tf_op jit(solution)/shard_map/ppermute | solution.py:470
  37.3 14.7 %collective-permute-start.11 = (f32[512,128]{1,0:T(8,128)S(1)}, f32[512,128]{1,0:T(8,128)S(1)}, u32[]{:S(2)}, u32[]{:S(2)}) collective-permute-start(f32[512,128]{1,0:T(8,128)S(1)} %get-tuple-element.60), channel_id=1, source_target_pairs={{1,0},{2,1},{3,2},{4,3},{5,4},{6,5},{7,6},{8,7},{9,8},{10,9},{11,1... | collective-permute-start | bytes 786440 | tf_op jit(solution)/shard_map/ppermute | solution.py:470
  37.8 8.4 %collective-permute-start.8 = (f32[328,128]{1,0:T(8,128)S(1)}, f32[328,128]{1,0:T(8,128)S(1)}, u32[]{:S(2)}, u32[]{:S(2)}) collective-permute-start(f32[328,128]{1,0:T(8,128)S(1)} %get-tuple-element.56), channel_id=1, source_target_pairs={{0,1},{1,2},{2,3},{3,4},{4,5},{5,6},{6,7},{7,8},{8,9},{9,10},{10,1... | collective-permute-start | bytes 503816 | tf_op jit(solution)/shard_map/ppermute | solution.py:470
  39.1 10.5 %collective-permute-start.9 = (f32[328,128]{1,0:T(8,128)S(1)}, f32[328,128]{1,0:T(8,128)S(1)}, u32[]{:S(2)}, u32[]{:S(2)}) collective-permute-start(f32[328,128]{1,0:T(8,128)S(1)} %get-tuple-element.57), channel_id=1, source_target_pairs={{1,0},{2,1},{3,2},{4,3},{5,4},{6,5},{7,6},{8,7},{9,8},{10,9},{11,1... | collective-permute-start | bytes 503816 | tf_op jit(solution)/shard_map/ppermute | solution.py:470

commit v2 on v0

v2 whole, which is shorter than its diff:
```python
import functools

import jax
import jax.numpy as jnp
from jax import lax
from jax.experimental import pallas as pl
from jax.experimental.pallas import tpu as pltpu
from jax.sharding import PartitionSpec as P


STEPS = 6
Q = 19
SUB = 8

velocity_table = [
    (0, 0, 0),
    (1, 0, 0),
    (-1, 0, 0),
    (0, 1, 0),
    (0, -1, 0),
    (0, 0, 1),
    (0, 0, -1),
    (1, 1, 0),
    (-1, -1, 0),
    (1, -1, 0),
    (-1, 1, 0),
    (1, 0, 1),
    (-1, 0, -1),
    (1, 0, -1),
    (-1, 0, 1),
    (0, 1, 1),
    (0, -1, -1),
    (0, 1, -1),
    (0, -1, 1),
]
W0, W1, W2 = 1.0 / 3.0, 1.0 / 18.0, 1.0 / 36.0
OMEGA = 1.9
KEEP = OMEGA - 1.0
PLUS = [1, 11, 13, 7, 9]
MINUS = [2, 12, 14, 8, 10]
FLAT = [0, 3, 4, 5, 6, 15, 16, 17, 18]
NP = len(PLUS)


def opp(i):
    if i == 0:
        return 0
    return i + 1 if i % 2 == 1 else i - 1


def sums_side(g):
    a, b, c, d, e = g
    return W1 * a + W2 * ((b + c) + (d + e)), W2 * (d - e), W2 * (b - c)


def sums_flat(g):
    g0, g3, g4, g5, g6, g15, g16, g17, g18 = g
    s15, s17 = g15 + g16, g17 + g18
    d15, d17 = g15 - g16, g17 - g18
    rho = W0 * g0 + W1 * ((g3 + g4) + (g5 + g6)) + W2 * (s15 + s17)
    my = W1 * (g3 - g4) + W2 * (d15 + d17)
    mz = W1 * (g5 - g6) + W2 * (d15 - d17)
    return rho, my, mz


def equilibrium(rho, mx, my, mz):
    inv = 1.0 / rho
    k = 3.0 * OMEGA
    m = (mx * k, my * k, mz * k)
    half = inv * (1.5 / k)
    v = (m[0] * half, m[1] * half, m[2] * half)
    mv = m[0] * v[0] + m[1] * v[1] + m[2] * v[2]
    base = OMEGA * rho - mv * (1.0 / 3.0)
    return m, v, base


def along(c, m):
    total = None
    for step, value in zip(c, m):
        if step:
            if total is None:
                total = value if step == 1 else -value
            else:
                total = total + value if step == 1 else total - value
    return total


def collide_all(g):
    sp = sums_side([g[i] for i in PLUS])
    sm = sums_side([g[i] for i in MINUS])
    rho, my, mz = sums_flat([g[i] for i in FLAT])
    rho = rho + (sp[0] + sm[0])
    mx = sp[0] - sm[0]
    my = my + (sp[1] - sm[1])
    mz = mz + (sp[2] - sm[2])
    m, v, base = equilibrium(rho, mx, my, mz)
    post = [None] * Q
    post[0] = base - KEEP * g[0]
    for i in range(1, Q, 2):
        cm, cv = along(velocity_table[i], m), along(velocity_table[i], v)
        even = base + cm * cv
        post[i] = (even + cm) - KEEP * g[i]
        post[i + 1] = (even - cm) - KEEP * g[i + 1]
    return post


class Field:
    def __init__(self, width, nz, edge=None, inner=None, ghost=None, near=None, far=None):
        self.width, self.nz = width, nz
        self.edge, self.inner, self.ghost, self.near, self.far = edge, inner, ghost, near, far

    def place(self, i, p):
        w, nz = self.width, self.nz
        if p in (-1, w) and self.ghost is not None:
            return self.ghost, (2 * i + (p == w)) * nz
        if p in (-2, -1):
            return (self.near if p == -1 else self.far)[0], PLUS.index(i) * nz
        if p in (w, w + 1):
            return (self.near if p == w else self.far)[1], MINUS.index(i) * nz
        if p in (0, w - 1):
            return self.edge, (2 * i + (p != 0)) * nz
        return self.inner, (i * (w - 2) + p - 1) * nz

    def load(self, i, p, z, shift=0):
        ref, base = self.place(i, p)
        if shift:
            return ref[pl.ds(base + z - shift, SUB), :]
        return rows_at(ref, base + z)

    def store(self, i, p, z, value):
        ref, base = self.place(i, p)
        put_rows(ref, base + z, value)


def rows_at(ref, row):
    return ref[pl.ds(pl.multiple_of(row, SUB), SUB), :]


def put_rows(ref, row, value):
    ref[pl.ds(pl.multiple_of(row, SUB), SUB), :] = value


class Heights:
    def __init__(self, width, own, beside=None):
        self.width, self.own, self.beside = width, own, beside

    def get(self, p, roll):
        if 0 <= p < self.width:
            return rows_at(self.own, (3 * p + roll + 1) * SUB)
        k = p + 2 if p < 0 else p - self.width + 2
        return rows_at(self.beside, (3 * k + roll + 1) * SUB)


def roll_lanes(x, step):
    if step == 0:
        return x
    return pltpu.roll(x, step % x.shape[1], 1)


def put_heights(ref, k, row):
    for roll in (-1, 0, 1):
        put_rows(ref, (3 * k + roll + 1) * SUB, roll_lanes(row, roll))


def levels(z, nz, ny):
    at = (lax.broadcasted_iota(jnp.int32, (SUB, ny), 0) + z).astype(jnp.float32)
    return {0: at, 1: at - 1.0, -1: jnp.where(at == nz - 1.0, -1.0, at + 1.0)}


def pull(field, heights, lev, i, p, z):
    cx, cy, cz = velocity_table[i]
    if i == 0:
        return field.load(0, p, z)
    moved = roll_lanes(field.load(i, p - cx, z, cz), cy)
    back = field.load(opp(i), p, z)
    return jnp.where(lev[cz] >= heights.get(p - cx, cy), moved, back)


def over_rows(rows, body):
    blocks = rows // SUB

    def step(k, carry):
        body(pl.multiple_of(k * SUB, SUB))
        return carry

    lax.fori_loop(0, blocks, step, 0, unroll=min(UNROLL, blocks))


def give(up, down, out_a, out_b):
    even = lax.rem(lax.axis_index("gx"), 2) == 0
    for cond, first, second in ((even, up, down), (jnp.logical_not(even), down, up)):

        @pl.when(cond)
        def _(first=first, second=second):
            def body(z):
                put_rows(out_a, z, rows_at(first, z))
                put_rows(out_b, z, rows_at(second, z))

            over_rows(up.shape[0], body)


def take(got_a, got_b, low, high):
    even = lax.rem(lax.axis_index("gx"), 2) == 0
    for cond, first, second in ((even, high, low), (jnp.logical_not(even), low, high)):

        @pl.when(cond)
        def _(first=first, second=second):
            def body(z):
                put_rows(first, z, rows_at(got_a, z))
                put_rows(second, z, rows_at(got_b, z))

            over_rows(low.shape[0], body)


def step_planes(field, new, heights, planes, nz, ny):
    def body(z):
        lev = levels(z, nz, ny)
        for p in planes:
            post = collide_all([pull(field, heights, lev, i, p, z) for i in range(Q)])
            for i in range(Q):
                new.store(i, p, z, post[i])

    over_rows(nz, body)


def give_second(inner, width, nz, out_a, out_b):
    field = Field(width, nz, None, inner)

    def copy(refs, p_up, p_down):
        def body(z):
            for k in range(NP):
                put_rows(refs[0], k * nz + z, field.load(PLUS[k], p_up, z))
                put_rows(refs[1], k * nz + z, field.load(MINUS[k], p_down, z))

        over_rows(nz, body)

    even = lax.rem(lax.axis_index("gx"), 2) == 0

    @pl.when(even)
    def _():
        copy((out_a, out_b), width - 2, 1)

    @pl.when(jnp.logical_not(even))
    def _():
        copy((out_b, out_a), width - 2, 1)


def edge0_kernel(width, nz, pops, h_hbm, edge, out_a, out_b, own, buf, h, up, down, sem):
    ny = h.shape[1]
    edges = (0, width - 1)
    copies = [pltpu.make_async_copy(pops.at[:, p], buf.at[:, e], sem.at[e]) for e, p in enumerate(edges)]
    copies.append(pltpu.make_async_copy(h_hbm, h, sem.at[2]))
    for c in copies:
        c.start()
    copies[2].wait()
    hf = h[...].astype(jnp.float32)
    for p in range(width):
        row = jnp.broadcast_to(hf[p : p + 1], (SUB, ny))
        put_heights(own, p, row)
        for out, first in ((down, 0), (up, width - 2)):
            if first <= p < first + 2:
                put_rows(out, NP * nz + (p - first) * SUB, row)
    field = Field(width, nz, edge)
    copies[0].wait()
    copies[1].wait()

    def body(z):
        for e, p in enumerate(edges):
            post = collide_all([buf[i, e, pl.ds(z, SUB), :] for i in range(Q)])
            for i in range(Q):
                field.store(i, p, z, post[i])
            for k in range(NP):
                if e:
                    put_rows(up, k * nz + z, post[PLUS[k]])
                else:
                    put_rows(down, k * nz + z, post[MINUS[k]])

    over_rows(nz, body)
    give(up, down, out_a, out_b)


def inner0_kernel(width, nz, pops, own, edge, inner, out_a, out_b, buf, up, down, sem):
    ny = own.shape[1]
    copy = pltpu.make_async_copy(pops.at[:, 1 : width - 1], buf, sem)
    copy.start()
    field = Field(width, nz, edge, inner)
    heights = Heights(width, own)
    copy.wait()

    def body(z):
        for p in range(1, width - 1):
            post = collide_all([buf[i, p - 1, pl.ds(z, SUB), :] for i in range(Q)])
            for i in range(Q):
                field.store(i, p, z, post[i])

    over_rows(nz, body)

    def body_ghost(z):
        lev = levels(z, nz, ny)
        for p, comps, out in ((width - 1, PLUS, up), (0, MINUS, down)):
            for k, i in enumerate(comps + FLAT):
                put_rows(out, k * nz + z, pull(field, heights, lev, i, p, z))

    over_rows(nz, body_ghost)
    give(up, down, out_a, out_b)


def inner1_kernel(width, nz, own, edge, inner, new_inner, out_a, out_b):
    ny = own.shape[1]
    new = Field(width, nz, None, new_inner)
    step_planes(Field(width, nz, edge, inner), new, Heights(width, own), range(1, width - 1), nz, ny)
    give_second(new_inner, width, nz, out_a, out_b)


def edge1_kernel(
    width, nz, own, edge0, inner0, inner1, got_a, got_b, edge1, inner2, out_a, out_b, beside, near_low, near_high
):
    ny = own.shape[1]
    take(got_a, got_b, near_low, near_high)
    for k in range(2):
        put_heights(beside, k, rows_at(near_low, NP * nz + k * SUB))
        put_heights(beside, k + 2, rows_at(near_high, NP * nz + k * SUB))
    heights = Heights(width, own, beside)
    old = Field(width, nz, edge0, inner0, near=(near_low, near_high))
    step_planes(old, Field(width, nz, edge1), heights, (0, width - 1), nz, ny)
    step_planes(Field(width, nz, edge1, inner1), Field(width, nz, None, inner2), heights, range(1, width - 1), nz, ny)
    give_second(inner2, width, nz, out_a, out_b)


def first_ghost(width, nz, ny, heights, edge0, near, got, ghost):
    old = Field(width, nz, edge0, near=near)
    new = Field(width, nz, ghost=ghost)

    def body(z):
        lev = levels(z, nz, ny)
        for p, known, own, ref in ((-1, PLUS, MINUS, got[0]), (width, MINUS, PLUS, got[1])):
            g = [None] * Q
            for k, i in enumerate(known + FLAT):
                g[i] = rows_at(ref, k * nz + z)
            for i in own:
                g[i] = pull(old, heights, lev, i, p, z)
            post = collide_all(g)
            for i in range(Q):
                new.store(i, p, z, post[i])

    over_rows(nz, body)


def write_planes(field, heights, nz, ny, planes, out, buf, sem):
    copies = []
    for k, p in enumerate(planes):

        def body(z, p=p, k=k):
            lev = levels(z, nz, ny)
            for i in range(Q):
                buf[i, k, pl.ds(z, SUB), :] = pull(field, heights, lev, i, p, z)

        over_rows(nz, body)
        copies.append(pltpu.make_async_copy(buf.at[:, k], out.at[:, p], sem.at[k]))
        copies[-1].start()
    return copies


def step_kernel(s, steps, width, nz, *refs):
    refs = list(refs)

    def pop(n):
        taken = refs[:n]
        del refs[:n]
        return taken

    own, beside, edge_old, edge, inner = pop(5)
    inner_next = pop(1)[0] if s + 2 <= steps else None
    extra = pop(2) if s == 1 else pop(1)
    got_a, got_b = pop(2)
    if s + 1 == steps:
        pop(1)
    ny = own.shape[1]
    heights = Heights(width, own, beside)
    ghost = edge_new = inner_new = out = out_a = out_b = None
    if s + 1 < steps:
        ghost, edge_new = pop(2)
    if s + 2 < steps:
        (inner_new,) = pop(1)
    else:
        (out,) = pop(1)
    if s + 3 < steps:
        out_a, out_b = pop(2)
    low, high = pop(2)
    if s + 1 == steps:
        (ghost,) = pop(1)
    take(got_a, got_b, low, high)
    if s == 1:
        first_ghost(width, nz, ny, heights, edge_old, extra, (low, high), ghost)
    else:
        old = Field(width, nz, edge_old, ghost=extra[0], far=(low, high))
        step_planes(old, Field(width, nz, ghost=ghost), heights, (-1, width), nz, ny)
    field = Field(width, nz, edge, inner, ghost)
    if s + 1 == steps:
        buf, sem = refs
        for c in write_planes(field, heights, nz, ny, (0, width - 1), out, buf, sem):
            c.wait()
        return
    step_planes(field, Field(width, nz, edge_new), heights, (0, width - 1), nz, ny)
    field = Field(width, nz, edge_new, inner_next)
    if s + 2 == steps:
        buf, sem = refs
        for c in write_planes(field, heights, nz, ny, range(1, width - 1), out, buf, sem):
            c.wait()
        return
    step_planes(field, Field(width, nz, None, inner_new), heights, range(1, width - 1), nz, ny)
    if s + 3 < steps:
        give_second(inner_new, width, nz, out_a, out_b)


UNROLL = 2
VMEM_LIMIT = 24 * 1024 * 1024


def per_device(pops, heights):
    _, width, nz, ny = pops.shape
    pops, heights = (pltpu.with_memory_space_constraint(x, pltpu.HBM) for x in (pops, heights))
    devices = lax.axis_size("gx")
    assert width >= 3 and nz % SUB == 0 and devices % 2 == 0 and STEPS >= 4
    pair_a = [(i, i ^ 1) for i in range(devices)]
    pair_b = [(i, (i + 1 if i % 2 else i - 1) % devices) for i in range(devices)]

    def rows(n):
        return jax.ShapeDtypeStruct((n, ny), jnp.float32)

    def scratch(n):
        return pltpu.VMEM((n, ny), jnp.float32)

    vmem = pl.BlockSpec(memory_space=pltpu.VMEM)
    hbm = pl.BlockSpec(memory_space=pltpu.HBM)
    edge_t = rows(Q * 2 * nz)
    inner_t = rows(Q * (width - 2) * nz)
    near_n = NP * nz + 2 * SUB
    set_n = (NP + len(FLAT)) * nz
    far_n = NP * nz
    dma = pltpu.SemaphoreType.DMA

    def call(kernel, args, outs, planes, scratch_shapes=(), in_specs=None, out_specs=None, **kw):
        return pl.pallas_call(
            functools.partial(kernel, width, nz),
            out_shape=outs,
            in_specs=[vmem] * len(args) if in_specs is None else in_specs,
            out_specs=[vmem] * len(outs) if out_specs is None else out_specs,
            scratch_shapes=list(scratch_shapes),
            compiler_params=pltpu.CompilerParams(vmem_limit_bytes=VMEM_LIMIT),
            cost_estimate=pl.CostEstimate(
                flops=planes * nz * ny * 250, bytes_accessed=planes * nz * ny * 4 * Q * 2, transcendentals=0
            ),
            **kw,
        )(*args)

    def exchange(a, b):
        a = lax.ppermute(a, "gx", pair_a)
        b = lax.ppermute(b, "gx", pair_b)
        return [a, b]

    edge0, a, b, own = call(
        edge0_kernel,
        [pops, heights],
        [edge_t, rows(near_n), rows(near_n), rows(3 * width * SUB)],
        2,
        [
            pltpu.VMEM((Q, 2, nz, ny), jnp.float32),
            pltpu.VMEM((width, ny), jnp.int32),
            scratch(near_n),
            scratch(near_n),
            dma((3,)),
        ],
        in_specs=[hbm, hbm],
    )
    near = exchange(a, b)
    inner0, a, b = call(
        inner0_kernel,
        [pops, own, edge0],
        [inner_t, rows(set_n), rows(set_n)],
        width,
        [pltpu.VMEM((Q, width - 2, nz, ny), jnp.float32), scratch(set_n), scratch(set_n), dma],
        in_specs=[hbm, vmem, vmem],
    )
    messages = {1: exchange(a, b)}
    inner1, a, b = call(inner1_kernel, [own, edge0, inner0], [inner_t, rows(far_n), rows(far_n)], width - 2)
    messages[2] = exchange(a, b)
    edge1, inner2, a, b, beside, low, high = call(
        edge1_kernel,
        [own, edge0, inner0, inner1, *near],
        [edge_t, inner_t, rows(far_n), rows(far_n), rows(12 * SUB), rows(near_n), rows(near_n)],
        width,
    )
    messages[3] = exchange(a, b)
    edges, inners, ghost = {0: edge0, 1: edge1}, {1: inner1, 2: inner2}, None
    out_t = jax.ShapeDtypeStruct(pops.shape, pops.dtype)
    out = None
    for s in range(1, STEPS):
        args = [own, beside, edges[s - 1], edges[s], inners[s]]
        if s + 2 <= STEPS:
            args.append(inners[s + 1])
        args += [low, high] if s == 1 else [ghost]
        args += messages[s]
        outs, spaces, aliases = [], [], {}
        n = set_n if s == 1 else far_n
        extra = [scratch(n), scratch(n)]
        specs = [vmem] * len(args)
        if s + 1 < STEPS:
            outs += [edge_t, edge_t]
        else:
            aliases = {len(args): 0}
            args.append(out)
            specs.append(hbm)
            extra.append(scratch(Q * 2 * nz))
        spaces = [vmem] * len(outs)
        if s + 2 < STEPS:
            outs.append(inner_t)
            spaces.append(vmem)
        else:
            outs.append(out_t)
            spaces.append(hbm)
            planes = 2 if s + 1 == STEPS else width - 2
            extra += [pltpu.VMEM((Q, planes, nz, ny), jnp.float32), dma((planes,))]
        if s + 3 < STEPS:
            outs += [rows(far_n), rows(far_n)]
            spaces += [vmem, vmem]
        got = list(call(
            functools.partial(step_kernel, s, STEPS),
            args,
            outs,
            width + 2,
            extra,
            in_specs=specs,
            out_specs=spaces,
            input_output_aliases=aliases,
        ))
        if s + 1 < STEPS:
            ghost, edges[s + 1] = got[0], got[1]
            del got[:2]
        if s + 2 < STEPS:
            inners[s + 2] = got[0]
        else:
            out = got[0]
        if s + 3 < STEPS:
            messages[s + 3] = exchange(got[1], got[2])
    return out


def solution(mesh):
    placed = (P(None, ("dir", "gx"), None, None), P(("dir", "gx"), None))

    return jax.shard_map(
        per_device,
        mesh=mesh,
        in_specs=placed,
        out_specs=P(None, ("dir", "gx"), None, None),
        check_vma=False,
    )
```

time: 92.4 us -> 48.9 us (0.53)
  waiting for transfers between devices: 51 us -> 2.74 us
  other arithmetic: 20.9 us -> 0 us
  Pallas kernels: 0 us -> 20 us
  starting transfers between devices: 11.6 us -> 25.8 us
  local copies, waits for them, and re-layouts: 6.85 us -> 0 us
  between operations: 1.88 us -> 0.15 us
    ppermute x14 -> x12, waiting for transfers between devices: 51 us -> 2.74 us  [the longest x6 2.72 us: exchange(): b = lax.ppermute(b, 'gx', pair_b)]
    pallas_call x0 -> x9, Pallas kernels: none -> 20 us  [call(): pl.pallas_call(functools.partial(kernel, width, nz), out_shape=outs, in_s...]
    add x19 -> x0, other arithmetic: 15.7 us -> none  [the longest x17 13.4 us: collide(): populations[component] + omega_rate * (equil - populations[component])]
    ppermute x14 -> x12, starting transfers between devices: 11.6 us -> 25.8 us  [the longest x6 19.5 us: exchange(): b = lax.ppermute(b, 'gx', pair_b)]
    slice x106 -> x0, local copies, waits for them, and re-layouts: 5.11 us -> none  [the longest x38 3.7 us: shift_local(): moved = jnp.roll(field, step_y, axis=2)]
    concatenate x26 -> x0, other arithmetic: 2.45 us -> none  [the longest x12 1.12 us: per_device(): jnp.concatenate([post[component][1:], right_planes[slot]], axis=0)]
    unnamed x25 -> x0, other arithmetic: 1.56 us -> none
    unnamed x46 -> x0, local copies, waits for them, and re-layouts: 1.55 us -> none
  transfers between devices with their start and end apart: 14 -> 12, of which waited for: 11 -> 1; matrix products, arithmetic and copies ran while one was open for 10% -> 0% of each run, Pallas kernels for 0% -> 27%
where the time goes in v2:
time: 48.9 us; the launch traced here: 48.7 us
  starting transfers between devices  25.8 us (53%)
  Pallas kernels  20 us (41%)
  waiting for transfers between devices  2.74 us (6%)
    pallas_call x9, Pallas kernels, call(): pl.pallas_call(functools.partial(kernel, width, nz), out_shape=outs, in_s...  20 us
    ppermute x6, starting transfers between devices, exchange(): b = lax.ppermute(b, 'gx', pair_b)  19.5 us
    ppermute x6, starting transfers between devices, exchange(): a = lax.ppermute(a, 'gx', pair_a)  6.29 us
    ppermute x6, waiting for transfers between devices, exchange(): b = lax.ppermute(b, 'gx', pair_b)  2.72 us
  transfers between devices with their start and end apart: 12, of which 1 were waited for; matrix products, arithmetic and copies ran while one was open for 0% of the time, Pallas kernels for 27%

profile of v2, /device:TPU:0, one launch (start us, length us, event | category | flops | bytes accessed | tf_op | source)
XLA Modules:
  0.0 48.7 jit_solution(3035876528093286054)
XLA Ops:
  0.0 1.9 %shard_map.28 = (f32[2432,128]{1,0:T(8,128)S(1)}, f32[336,128]{1,0:T(8,128)S(1)}, f32[336,128]{1,0:T(8,128)S(1)}, f32[96,128]{1,0:T(8,128)S(1)}) custom-call(f32[19,4,64,128]{3,2,1,0:T(8,128)} %pops.3, s32[4,128]{1,0:T(4,128)} %h_hbm.1), custom_call_target="tpu_custom_call" | custom-call | flops 4096000 | bytes 2490368 | tf_op jit(solution)/shard_map/pallas_call | solution.py:444
  1.9 2.5 %shard_map.29 = (f32[2432,128]{1,0:T(8,128)S(1)}, f32[896,128]{1,0:T(8,128)S(1)}, f32[896,128]{1,0:T(8,128)S(1)}) custom-call(f32[19,4,64,128]{3,2,1,0:T(8,128)} %pops.3, f32[96,128]{1,0:T(8,128)S(1)} %get-tuple-element.38.own.refs_0_, f32[2432,128]{1,0:T(8,128)S(1)} %get-tuple-element.39.edge.edge0.refs_2_), custom_call_target="tpu_custom_call" | custom-call | flops 8192000 | bytes 4980736 | tf_op jit(solution)/shard_map/pallas_call | solution.py:444
  4.4 0.6 %collective-permute-start.2 = (f32[896,128]{1,0:T(8,128)S(1)}, f32[896,128]{1,0:T(8,128)S(1)}, u32[]{:S(2)}, u32[]{:S(2)}) collective-permute-start(f32[896,128]{1,0:T(8,128)S(1)} %get-tuple-element.49), channel_id=1, source_target_pairs={{0,1},{1,0},{2,3},{3,2},{4,5},{5,4},{6,7},{7,6},{8,9},{9,8},{10,11... | collective-permute-start | bytes 1376264 | tf_op jit(solution)/shard_map/ppermute | solution.py:458
  5.0 5.7 %collective-permute-start.3 = (f32[896,128]{1,0:T(8,128)S(1)}, f32[896,128]{1,0:T(8,128)S(1)}, u32[]{:S(2)}, u32[]{:S(2)}) collective-permute-start(f32[896,128]{1,0:T(8,128)S(1)} %get-tuple-element.50), channel_id=1, source_target_pairs={{0,15},{1,2},{2,1},{3,4},{4,3},{5,6},{6,5},{7,8},{8,7},{9,10},{10,... | collective-permute-start | bytes 1376264 | tf_op jit(solution)/shard_map/ppermute | solution.py:459
  10.6 0.6 %collective-permute-start.1 = (f32[336,128]{1,0:T(8,128)S(1)}, f32[336,128]{1,0:T(8,128)S(1)}, u32[]{:S(2)}, u32[]{:S(2)}) collective-permute-start(f32[336,128]{1,0:T(8,128)S(1)} %get-tuple-element.43), channel_id=1, source_target_pairs={{0,15},{1,2},{2,1},{3,4},{4,3},{5,6},{6,5},{7,8},{8,7},{9,10},{10,... | collective-permute-start | bytes 516104 | tf_op jit(solution)/shard_map/ppermute | solution.py:459
  11.3 0.8 %shard_map.30 = (f32[2432,128]{1,0:T(8,128)S(1)}, f32[320,128]{1,0:T(8,128)S(1)}, f32[320,128]{1,0:T(8,128)S(1)}) custom-call(f32[96,128]{1,0:T(8,128)S(1)} %get-tuple-element.38.own.refs_0_, f32[2432,128]{1,0:T(8,128)S(1)} %get-tuple-element.39.edge.edge0.refs_2_, f32[2432,128]{1,0:T(8,128)S(1)} %get-tuple-element.40.inner.inner0), custom_call_target="tpu_custom_call" | custom-call | flops 4096000 | bytes 2490368 | tf_op jit(solution)/shard_map/pallas_call | solution.py:444
  12.1 0.1 collective-permute-start.4
  12.1 0.0 collective-permute-done.got_a
  12.1 3.9 %collective-permute-start.5 = (f32[320,128]{1,0:T(8,128)S(1)}, f32[320,128]{1,0:T(8,128)S(1)}, u32[]{:S(2)}, u32[]{:S(2)}) collective-permute-start(f32[320,128]{1,0:T(8,128)S(1)} %get-tuple-element.55), channel_id=1, source_target_pairs={{0,15},{1,2},{2,1},{3,4},{4,3},{5,6},{6,5},{7,8},{8,7},{9,10},{10,... | collective-permute-start | bytes 491528 | tf_op jit(solution)/shard_map/ppermute | solution.py:459
  16.0 2.7 %collective-permute-done.1.got_b = f32[336,128]{1,0:T(8,128)S(1)} collective-permute-done((f32[336,128]{1,0:T(8,128)S(1)}, f32[336,128]{1,0:T(8,128)S(1)}, u32[]{:S(2)}, u32[]{:S(2)}) %collective-permute-start.1) | collective-permute-done | bytes 172064 | tf_op jit(solution)/shard_map/ppermute | solution.py:459
  18.7 1.7 %shard_map.31 = (f32[2432,128]{1,0:T(8,128)S(1)}, f32[2432,128]{1,0:T(8,128)S(1)}, f32[320,128]{1,0:T(8,128)S(1)}, f32[320,128]{1,0:T(8,128)S(1)}, f32[96,128]{1...) custom-call(f32[96,128]{1,0:T(8,128)S(1)} %get-tuple-element.38.own.refs_0_, ...), custom_call_target="tpu_custom_call" | custom-call | flops 8192000 | bytes 4980736 | tf_op jit(solution)/shard_map/pallas_call | solution.py:444
  20.5 5.5 %collective-permute-start.6 = (f32[320,128]{1,0:T(8,128)S(1)}, f32[320,128]{1,0:T(8,128)S(1)}, u32[]{:S(2)}, u32[]{:S(2)}) collective-permute-start(f32[320,128]{1,0:T(8,128)S(1)} %get-tuple-element.59), channel_id=1, source_target_pairs={{0,1},{1,0},{2,3},{3,2},{4,5},{5,4},{6,7},{7,6},{8,9},{9,8},{10,11... | collective-permute-start | bytes 491528 | tf_op jit(solution)/shard_map/ppermute | solution.py:458
  26.0 0.0 collective-permute-done.2.refs_8_
  26.0 4.8 %collective-permute-start.7 = (f32[320,128]{1,0:T(8,128)S(1)}, f32[320,128]{1,0:T(8,128)S(1)}, u32[]{:S(2)}, u32[]{:S(2)}) collective-permute-start(f32[320,128]{1,0:T(8,128)S(1)} %get-tuple-element.60), channel_id=1, source_target_pairs={{0,15},{1,2},{2,1},{3,4},{4,3},{5,6},{6,5},{7,8},{8,7},{9,10},{10,... | collective-permute-start | bytes 491528 | tf_op jit(solution)/shard_map/ppermute | solution.py:459
  30.8 2.5 %shard_map.32 = (f32[2432,128]{1,0:T(8,128)S(1)}, f32[2432,128]{1,0:T(8,128)S(1)}, f32[2432,128]{1,0:T(8,128)S(1)}, f32[320,128]{1,0:T(8,128)S(1)}, f32[320,128]{1,0:T(8,128)S(1)}) custom-call(f32[96,128]{1,0:T(8,128)S(1)} %get-tuple-element.38.own.refs_0_, f32[96,128]{1,0:T(8,128)S(1)} %get-tuple-element.44.refs_1_, ...), custom_call_target="tpu_custom_call" | custom-call | flops 12288000 | bytes 7471104 | tf_op jit(solution)/shard_map/pallas_call | solution.py:444
  33.3 0.1 collective-permute-start.8
  33.4 0.0 collective-permute-done.4.refs_7_
  33.4 0.6 %collective-permute-start.9 = (f32[320,128]{1,0:T(8,128)S(1)}, f32[320,128]{1,0:T(8,128)S(1)}, u32[]{:S(2)}, u32[]{:S(2)}) collective-permute-start(f32[320,128]{1,0:T(8,128)S(1)} %get-tuple-element.65), channel_id=1, source_target_pairs={{0,15},{1,2},{2,1},{3,4},{4,3},{5,6},{6,5},{7,8},{8,7},{9,10},{10,... | collective-permute-start | bytes 491528 | tf_op jit(solution)/shard_map/ppermute | solution.py:459
  34.0 2.4 %shard_map.33 = (f32[2432,128]{1,0:T(8,128)S(1)}, f32[2432,128]{1,0:T(8,128)S(1)}, f32[2432,128]{1,0:T(8,128)S(1)}, f32[320,128]{1,0:T(8,128)S(1)}, f32[320,128]{1,0:T(8,128)S(1)}) custom-call(f32[96,128]{1,0:T(8,128)S(1)} %get-tuple-element.38.own.refs_0_, f32[96,128]{1,0:T(8,128)S(1)} %get-tuple-element.44.refs_1_, ...), custom_call_target="tpu_custom_call" | custom-call | flops 12288000 | bytes 7471104 | tf_op jit(solution)/shard_map/pallas_call | solution.py:444
  36.5 0.1 collective-permute-start.10
  36.5 4.0 %collective-permute-start.11 = (f32[320,128]{1,0:T(8,128)S(1)}, f32[320,128]{1,0:T(8,128)S(1)}, u32[]{:S(2)}, u32[]{:S(2)}) collective-permute-start(f32[320,128]{1,0:T(8,128)S(1)} %get-tuple-element.69), channel_id=1, source_target_pairs={{0,15},{1,2},{2,1},{3,4},{4,3},{5,6},{6,5},{7,8},{8,7},{9,10},{10,... | collective-permute-start | bytes 491528 | tf_op jit(solution)/shard_map/ppermute | solution.py:459
  40.5 2.4 %shard_map.34 = (f32[2432,128]{1,0:T(8,128)S(1)}, f32[2432,128]{1,0:T(8,128)S(1)}, f32[2432,128]{1,0:T(8,128)S(1)}) custom-call(f32[96,128]{1,0:T(8,128)S(1)} %get-tuple-element.38.own.refs_0_, f32[96,128]{1,0:T(8,128)S(1)} %get-tuple-element.44.refs_1_, f32[2432,128]{1,0:T(8,128)S(1)} %get-tuple-element.51.refs_3_.refs_2_, ...), custom_call_target="tpu_custom_call" | custom-call | flops 12288000 | bytes 7471104 | tf_op jit(solution)/shard_map/pallas_call | solution.py:444
  42.9 3.3 %shard_map.35 = (f32[2432,128]{1,0:T(8,128)S(1)}, f32[2432,128]{1,0:T(8,128)S(1)}, f32[19,4,64,128]{3,2,1,0:T(8,128)}) custom-call(f32[96,128]{1,0:T(8,128)S(1)} %get-tuple-element.38.own.refs_0_, f32[96,128]{1,0:T(8,128)S(1)} %get-tuple-element.44.refs_1_, f32[2432,128]{1,0:T(8,128)S(1)} %get-tuple-element.56.refs_3_.refs_2_, ...), custom_call_target="tpu_custom_call" | custom-call | flops 12288000 | bytes 7471104 | tf_op jit(solution)/shard_map/pallas_call | solution.py:444
  46.2 2.5 %shard_map.36 = f32[19,4,64,128]{3,2,1,0:T(8,128)} custom-call(f32[96,128]{1,0:T(8,128)S(1)} %get-tuple-element.38.own.refs_0_, f32[96,128]{1,0:T(8,128)S(1)} %get-tuple-element.44.refs_1_, f32[2432,128]{1,0:T(8,128)S(1)} %get-tuple-element.61.refs_3_.refs_2_, f32[2432,128]{1,0:T(8,128)S(1)} %get-tuple-element.66.refs_3_, ...), custom_call_target="tpu_custom_call", output_to_operand_aliasing={{}: (8, {})} | custom-call | flops 12288000 | bytes 7471104 | tf_op jit(solution)/shard_map/pallas_call | solution.py:444
  (9 shorter events, 0.0 us)
Async XLA Ops:
  4.4 21.6 %collective-permute-start.2 = (f32[896,128]{1,0:T(8,128)S(1)}, f32[896,128]{1,0:T(8,128)S(1)}, u32[]{:S(2)}, u32[]{:S(2)}) collective-permute-start(f32[896,128]{1,0:T(8,128)S(1)} %get-tuple-element.49), channel_id=1, source_target_pairs={{0,1},{1,0},{2,3},{3,2},{4,5},{5,4},{6,7},{7,6},{8,9},{9,8},{10,11... | collective-permute-start | bytes 1376264 | tf_op jit(solution)/shard_map/ppermute | solution.py:458
  5.0 25.8 %collective-permute-start.3 = (f32[896,128]{1,0:T(8,128)S(1)}, f32[896,128]{1,0:T(8,128)S(1)}, u32[]{:S(2)}, u32[]{:S(2)}) collective-permute-start(f32[896,128]{1,0:T(8,128)S(1)} %get-tuple-element.50), channel_id=1, source_target_pairs={{0,15},{1,2},{2,1},{3,4},{4,3},{5,6},{6,5},{7,8},{8,7},{9,10},{10,... | collective-permute-start | bytes 1376264 | tf_op jit(solution)/shard_map/ppermute | solution.py:459
  10.6 1.5 %collective-permute-start = (f32[336,128]{1,0:T(8,128)S(1)}, f32[336,128]{1,0:T(8,128)S(1)}, u32[]{:S(2)}, u32[]{:S(2)}) collective-permute-start(f32[336,128]{1,0:T(8,128)S(1)} %get-tuple-element.42), channel_id=1, source_target_pairs={{0,1},{1,0},{2,3},{3,2},{4,5},{5,4},{6,7},{7,6},{8,9},{9,8},{10,11... | collective-permute-start | bytes 516104 | tf_op jit(solution)/shard_map/ppermute | solution.py:458
  10.6 8.1 %collective-permute-start.1 = (f32[336,128]{1,0:T(8,128)S(1)}, f32[336,128]{1,0:T(8,128)S(1)}, u32[]{:S(2)}, u32[]{:S(2)}) collective-permute-start(f32[336,128]{1,0:T(8,128)S(1)} %get-tuple-element.43), channel_id=1, source_target_pairs={{0,15},{1,2},{2,1},{3,4},{4,3},{5,6},{6,5},{7,8},{8,7},{9,10},{10,... | collective-permute-start | bytes 516104 | tf_op jit(solution)/shard_map/ppermute | solution.py:459
  12.1 21.3 %collective-permute-start.4 = (f32[320,128]{1,0:T(8,128)S(1)}, f32[320,128]{1,0:T(8,128)S(1)}, u32[]{:S(2)}, u32[]{:S(2)}) collective-permute-start(f32[320,128]{1,0:T(8,128)S(1)} %get-tuple-element.54), channel_id=1, source_target_pairs={{0,1},{1,0},{2,3},{3,2},{4,5},{5,4},{6,7},{7,6},{8,9},{9,8},{10,11... | collective-permute-start | bytes 491528 | tf_op jit(solution)/shard_map/ppermute | solution.py:458
  12.1 21.9 %collective-permute-start.5 = (f32[320,128]{1,0:T(8,128)S(1)}, f32[320,128]{1,0:T(8,128)S(1)}, u32[]{:S(2)}, u32[]{:S(2)}) collective-permute-start(f32[320,128]{1,0:T(8,128)S(1)} %get-tuple-element.55), channel_id=1, source_target_pairs={{0,15},{1,2},{2,1},{3,4},{4,3},{5,6},{6,5},{7,8},{8,7},{9,10},{10,... | collective-permute-start | bytes 491528 | tf_op jit(solution)/shard_map/ppermute | solution.py:459
  20.5 16.0 %collective-permute-start.6 = (f32[320,128]{1,0:T(8,128)S(1)}, f32[320,128]{1,0:T(8,128)S(1)}, u32[]{:S(2)}, u32[]{:S(2)}) collective-permute-start(f32[320,128]{1,0:T(8,128)S(1)} %get-tuple-element.59), channel_id=1, source_target_pairs={{0,1},{1,0},{2,3},{3,2},{4,5},{5,4},{6,7},{7,6},{8,9},{9,8},{10,11... | collective-permute-start | bytes 491528 | tf_op jit(solution)/shard_map/ppermute | solution.py:458
  26.0 14.5 %collective-permute-start.7 = (f32[320,128]{1,0:T(8,128)S(1)}, f32[320,128]{1,0:T(8,128)S(1)}, u32[]{:S(2)}, u32[]{:S(2)}) collective-permute-start(f32[320,128]{1,0:T(8,128)S(1)} %get-tuple-element.60), channel_id=1, source_target_pairs={{0,15},{1,2},{2,1},{3,4},{4,3},{5,6},{6,5},{7,8},{8,7},{9,10},{10,... | collective-permute-start | bytes 491528 | tf_op jit(solution)/shard_map/ppermute | solution.py:459
  33.3 9.6 %collective-permute-start.8 = (f32[320,128]{1,0:T(8,128)S(1)}, f32[320,128]{1,0:T(8,128)S(1)}, u32[]{:S(2)}, u32[]{:S(2)}) collective-permute-start(f32[320,128]{1,0:T(8,128)S(1)} %get-tuple-element.64), channel_id=1, source_target_pairs={{0,1},{1,0},{2,3},{3,2},{4,5},{5,4},{6,7},{7,6},{8,9},{9,8},{10,11... | collective-permute-start | bytes 491528 | tf_op jit(solution)/shard_map/ppermute | solution.py:458
  33.4 9.5 %collective-permute-start.9 = (f32[320,128]{1,0:T(8,128)S(1)}, f32[320,128]{1,0:T(8,128)S(1)}, u32[]{:S(2)}, u32[]{:S(2)}) collective-permute-start(f32[320,128]{1,0:T(8,128)S(1)} %get-tuple-element.65), channel_id=1, source_target_pairs={{0,15},{1,2},{2,1},{3,4},{4,3},{5,6},{6,5},{7,8},{8,7},{9,10},{10,... | collective-permute-start | bytes 491528 | tf_op jit(solution)/shard_map/ppermute | solution.py:459
  36.5 9.8 %collective-permute-start.10 = (f32[320,128]{1,0:T(8,128)S(1)}, f32[320,128]{1,0:T(8,128)S(1)}, u32[]{:S(2)}, u32[]{:S(2)}) collective-permute-start(f32[320,128]{1,0:T(8,128)S(1)} %get-tuple-element.68), channel_id=1, source_target_pairs={{0,1},{1,0},{2,3},{3,2},{4,5},{5,4},{6,7},{7,6},{8,9},{9,8},{10,11... | collective-permute-start | bytes 491528 | tf_op jit(solution)/shard_map/ppermute | solution.py:458
  36.5 9.7 %collective-permute-start.11 = (f32[320,128]{1,0:T(8,128)S(1)}, f32[320,128]{1,0:T(8,128)S(1)}, u32[]{:S(2)}, u32[]{:S(2)}) collective-permute-start(f32[320,128]{1,0:T(8,128)S(1)} %get-tuple-element.69), channel_id=1, source_target_pairs={{0,15},{1,2},{2,1},{3,4},{4,3},{5,6},{6,5},{7,8},{8,7},{9,10},{10,... | collective-permute-start | bytes 491528 | tf_op jit(solution)/shard_map/ppermute | solution.py:459

commit v3 on v2

--- a/solution.py
+++ b/solution.py
@@ -33,12 +33,13 @@
     (0, 1, -1),
     (0, -1, 1),
 ]
-W0, W1, W2 = 1.0 / 3.0, 1.0 / 18.0, 1.0 / 36.0
 OMEGA = 1.9
 KEEP = OMEGA - 1.0
+MAX_HEIGHT = 32
 PLUS = [1, 11, 13, 7, 9]
 MINUS = [2, 12, 14, 8, 10]
 FLAT = [0, 3, 4, 5, 6, 15, 16, 17, 18]
+REST = [4, 6, 15, 16, 17, 18]
 NP = len(PLUS)
 
 
@@ -48,69 +49,96 @@
     return i + 1 if i % 2 == 1 else i - 1
 
 
-def sums_side(g):
-    a, b, c, d, e = g
-    return W1 * a + W2 * ((b + c) + (d + e)), W2 * (d - e), W2 * (b - c)
-
-
-def sums_flat(g):
-    g0, g3, g4, g5, g6, g15, g16, g17, g18 = g
-    s15, s17 = g15 + g16, g17 + g18
-    d15, d17 = g15 - g16, g17 - g18
-    rho = W0 * g0 + W1 * ((g3 + g4) + (g5 + g6)) + W2 * (s15 + s17)
-    my = W1 * (g3 - g4) + W2 * (d15 + d17)
-    mz = W1 * (g5 - g6) + W2 * (d15 - d17)
-    return rho, my, mz
-
-
-def equilibrium(rho, mx, my, mz):
-    inv = 1.0 / rho
-    k = 3.0 * OMEGA
-    m = (mx * k, my * k, mz * k)
-    half = inv * (1.5 / k)
-    v = (m[0] * half, m[1] * half, m[2] * half)
-    mv = m[0] * v[0] + m[1] * v[1] + m[2] * v[2]
-    base = OMEGA * rho - mv * (1.0 / 3.0)
-    return m, v, base
-
-
-def along(c, m):
-    total = None
-    for step, value in zip(c, m):
-        if step:
-            if total is None:
-                total = value if step == 1 else -value
-            else:
-                total = total + value if step == 1 else total - value
-    return total
-
-
-def collide_all(g):
-    sp = sums_side([g[i] for i in PLUS])
-    sm = sums_side([g[i] for i in MINUS])
-    rho, my, mz = sums_flat([g[i] for i in FLAT])
-    rho = rho + (sp[0] + sm[0])
-    mx = sp[0] - sm[0]
-    my = my + (sp[1] - sm[1])
-    mz = mz + (sp[2] - sm[2])
-    m, v, base = equilibrium(rho, mx, my, mz)
-    post = [None] * Q
-    post[0] = base - KEEP * g[0]
-    for i in range(1, Q, 2):
-        cm, cv = along(velocity_table[i], m), along(velocity_table[i], v)
-        even = base + cm * cv
-        post[i] = (even + cm) - KEEP * g[i]
-        post[i + 1] = (even - cm) - KEEP * g[i + 1]
+def factors(t, steps):
+    if t + 1 < steps:
+        return None, -OMEGA / KEEP
+    scale = (-1.0 / KEEP) ** t
+    return -KEEP / scale, OMEGA / scale
+
+
+def moments(g):
+    s = {i: g[i] + g[i + 1] for i in range(1, Q, 2)}
+    d = {i: g[i] - g[i + 1] for i in range(1, Q, 2)}
+    axes = (s[1] + s[3]) + s[5]
+    rho = (axes + axes) + ((s[7] + s[9]) + (s[11] + s[13])) + ((s[15] + s[17]) + g[0] * 12.0)
+    x = (d[1] + d[1]) + ((d[7] + d[9]) + (d[11] + d[13]))
+    y = (d[3] + d[3]) + ((d[7] - d[9]) + (d[15] + d[17]))
+    z = (d[5] + d[5]) + ((d[11] - d[13]) + (d[15] - d[17]))
+    return rho, x, y, z
+
+
+def side_moments(g, comps):
+    a, b, c, d, e = (g[i] for i in comps)
+    rho = (a + a) + ((b + c) + (d + e))
+    return (rho, d - e, b - c) if comps is PLUS else (rho, e - d, c - b)
+
+
+def flat_moments(g):
+    axes = (g[3] + g[4]) + (g[5] + g[6])
+    rho = (axes + axes) + ((g[15] + g[16]) + (g[17] + g[18])) + g[0] * 12.0
+    a, b, y, z = g[15] - g[16], g[17] - g[18], g[3] - g[4], g[5] - g[6]
+    return rho, (y + y) + (a + b), (z + z) + (a - b)
+
+
+def flat_from_rest(g, rho, y, z):
+    a, b = g[15] - g[16], g[17] - g[18]
+    g[3] = g[4] + (y - (a + b)) * 0.5
+    g[5] = g[6] + (z - (a - b)) * 0.5
+    axes = (g[3] + g[4]) + (g[5] + g[6])
+    g[0] = (rho - (axes + axes) - ((g[15] + g[16]) + (g[17] + g[18]))) * (1.0 / 12.0)
+
+
+def terms(rho, x, y, z, rate):
+    half = 1.5 / rho
+    mx, my, mz = (value * (rate / 12.0) for value in (x, y, z))
+    vx, vy, vz = x * half, y * half, z * half
+    xx, yy, zz = mx * vx, my * vy, mz * vz
+    base = rho * (rate / 36.0) - ((xx + yy) + zz) * (1.0 / 3.0)
+    ex, ey, ez = base + xx, base + yy, base + zz
+    mx2, my2 = mx + mx, my + my
+    exy, exz, eyz = ex + yy, ex + zz, ey + zz
+    xy, xz, yz = mx2 * vy, mx2 * vz, my2 * vz
+    return base, {
+        1: (ex, mx),
+        3: (ey, my),
+        5: (ez, mz),
+        7: (exy + xy, mx + my),
+        9: (exy - xy, mx - my),
+        11: (exz + xz, mx + mz),
+        13: (exz - xz, mx - mz),
+        15: (eyz + yz, my + mz),
+        17: (eyz - yz, my - mz),
+    }
+
+
+def after(g, sums, t, steps, comps=range(Q)):
+    keep, rate = factors(t, steps)
+    base, parts = terms(*sums, rate)
+    post = {}
+    for i in comps:
+        own = g[i] if keep is None else g[i] * keep
+        if i == 0:
+            post[i] = own + base
+        elif i % 2:
+            post[i] = own + (parts[i][0] + parts[i][1])
+        else:
+            post[i] = own + (parts[i - 1][0] - parts[i - 1][1])
     return post
 
 
+def collide(g, t, steps):
+    return after(g, moments(g), t, steps)
+
+
 class Field:
-    def __init__(self, width, nz, edge=None, inner=None, ghost=None, near=None, far=None):
+    def __init__(self, width, nz, edge=None, inner=None, ghost=None, near=None, far=None, flats=None):
         self.width, self.nz = width, nz
-        self.edge, self.inner, self.ghost, self.near, self.far = edge, inner, ghost, near, far
+        self.edge, self.inner, self.ghost, self.near, self.far, self.flats = edge, inner, ghost, near, far, flats
 
     def place(self, i, p):
         w, nz = self.width, self.nz
+        if p in (-1, w) and self.flats is not None and i in FLAT:
+            return self.flats, (2 * FLAT.index(i) + (p == w)) * nz
         if p in (-1, w) and self.ghost is not None:
             return self.ghost, (2 * i + (p == w)) * nz
         if p in (-2, -1):
@@ -164,7 +192,13 @@
 
 def levels(z, nz, ny):
     at = (lax.broadcasted_iota(jnp.int32, (SUB, ny), 0) + z).astype(jnp.float32)
-    return {0: at, 1: at - 1.0, -1: jnp.where(at == nz - 1.0, -1.0, at + 1.0)}
+    top = z + SUB == nz
+    return {
+        0: at,
+        1: at - 1.0,
+        -1: jnp.where(at == nz - 1.0, -1.0, at + 1.0) if top else at + 1.0,
+        "inside": at < nz - 1.0 if top else None,
+    }
 
 
 def pull(field, heights, lev, i, p, z):
@@ -172,18 +206,18 @@
     if i == 0:
         return field.load(0, p, z)
     moved = roll_lanes(field.load(i, p - cx, z, cz), cy)
-    back = field.load(opp(i), p, z)
-    return jnp.where(lev[cz] >= heights.get(p - cx, cy), moved, back)
+    if z - cz < MAX_HEIGHT:
+        fluid = lev[cz] >= heights.get(p - cx, cy)
+    elif cz == -1 and lev["inside"] is not None:
+        fluid = lev["inside"]
+    else:
+        return moved
+    return jnp.where(fluid, moved, field.load(opp(i), p, z))
 
 
 def over_rows(rows, body):
-    blocks = rows // SUB
-
-    def step(k, carry):
-        body(pl.multiple_of(k * SUB, SUB))
-        return carry
-
-    lax.fori_loop(0, blocks, step, 0, unroll=min(UNROLL, blocks))
+    for z in range(0, rows, SUB):
+        body(z)
 
 
 def give(up, down, out_a, out_b):
@@ -212,18 +246,18 @@
             over_rows(low.shape[0], body)
 
 
-def step_planes(field, new, heights, planes, nz, ny):
+def step_planes(t, steps, field, new, heights, planes, nz, ny):
     def body(z):
         lev = levels(z, nz, ny)
         for p in planes:
-            post = collide_all([pull(field, heights, lev, i, p, z) for i in range(Q)])
+            post = collide([pull(field, heights, lev, i, p, z) for i in range(Q)], t, steps)
             for i in range(Q):
                 new.store(i, p, z, post[i])
 
     over_rows(nz, body)
 
 
-def give_second(inner, width, nz, out_a, out_b):
+def give_second(inner, width, nz, out_a, out_b, rest=None):
     field = Field(width, nz, None, inner)
 
     def copy(refs, p_up, p_down):
@@ -231,6 +265,10 @@
             for k in range(NP):
                 put_rows(refs[0], k * nz + z, field.load(PLUS[k], p_up, z))
                 put_rows(refs[1], k * nz + z, field.load(MINUS[k], p_down, z))
+            if rest is not None:
+                for e, ref in enumerate(refs):
+                    for k in range(len(REST)):
+                        put_rows(ref, (NP + k) * nz + z, rows_at(rest, (e * len(REST) + k) * nz + z))
 
         over_rows(nz, body)
 
@@ -266,7 +304,7 @@
 
     def body(z):
         for e, p in enumerate(edges):
-            post = collide_all([buf[i, e, pl.ds(z, SUB), :] for i in range(Q)])
+            post = collide([buf[i, e, pl.ds(z, SUB), :] for i in range(Q)], 0, STEPS)
             for i in range(Q):
                 field.store(i, p, z, post[i])
             for k in range(NP):
@@ -279,7 +317,7 @@
     give(up, down, out_a, out_b)
 
 
-def inner0_kernel(width, nz, pops, own, edge, inner, out_a, out_b, buf, up, down, sem):
+def inner0_kernel(width, nz, pops, own, edge, inner, out_a, out_b, rest, buf, up, down, sem):
     ny = own.shape[1]
     copy = pltpu.make_async_copy(pops.at[:, 1 : width - 1], buf, sem)
     copy.start()
@@ -289,7 +327,7 @@
 
     def body(z):
         for p in range(1, width - 1):
-            post = collide_all([buf[i, p - 1, pl.ds(z, SUB), :] for i in range(Q)])
+            post = collide([buf[i, p - 1, pl.ds(z, SUB), :] for i in range(Q)], 0, STEPS)
             for i in range(Q):
                 field.store(i, p, z, post[i])
 
@@ -297,19 +335,24 @@
 
     def body_ghost(z):
         lev = levels(z, nz, ny)
-        for p, comps, out in ((width - 1, PLUS, up), (0, MINUS, down)):
-            for k, i in enumerate(comps + FLAT):
+        for e, (p, comps, out) in enumerate(((width - 1, PLUS, up), (0, MINUS, down))):
+            for k, i in enumerate(comps):
                 put_rows(out, k * nz + z, pull(field, heights, lev, i, p, z))
+            g = {i: pull(field, heights, lev, i, p, z) for i in FLAT}
+            for k, row in enumerate(flat_moments(g)):
+                put_rows(out, (NP + k) * nz + z, row)
+            for k, i in enumerate(REST):
+                put_rows(rest, (e * len(REST) + k) * nz + z, g[i])
 
     over_rows(nz, body_ghost)
     give(up, down, out_a, out_b)
 
 
-def inner1_kernel(width, nz, own, edge, inner, new_inner, out_a, out_b):
+def inner1_kernel(width, nz, own, edge, inner, rest, new_inner, out_a, out_b):
     ny = own.shape[1]
     new = Field(width, nz, None, new_inner)
-    step_planes(Field(width, nz, edge, inner), new, Heights(width, own), range(1, width - 1), nz, ny)
-    give_second(new_inner, width, nz, out_a, out_b)
+    step_planes(1, STEPS, Field(width, nz, edge, inner), new, Heights(width, own), range(1, width - 1), nz, ny)
+    give_second(new_inner, width, nz, out_a, out_b, rest)
 
 
 def edge1_kernel(
@@ -322,25 +365,77 @@
         put_heights(beside, k + 2, rows_at(near_high, NP * nz + k * SUB))
     heights = Heights(width, own, beside)
     old = Field(width, nz, edge0, inner0, near=(near_low, near_high))
-    step_planes(old, Field(width, nz, edge1), heights, (0, width - 1), nz, ny)
-    step_planes(Field(width, nz, edge1, inner1), Field(width, nz, None, inner2), heights, range(1, width - 1), nz, ny)
+    step_planes(1, STEPS, old, Field(width, nz, edge1), heights, (0, width - 1), nz, ny)
+    both = Field(width, nz, edge1, inner1)
+    step_planes(2, STEPS, both, Field(width, nz, None, inner2), heights, range(1, width - 1), nz, ny)
     give_second(inner2, width, nz, out_a, out_b)
 
 
-def first_ghost(width, nz, ny, heights, edge0, near, got, ghost):
-    old = Field(width, nz, edge0, near=near)
-    new = Field(width, nz, ghost=ghost)
+def edge2_kernel(
+    width,
+    nz,
+    own,
+    beside,
+    near_low,
+    near_high,
+    edge0,
+    edge1,
+    inner1,
+    inner2,
+    got_a,
+    got_b,
+    ghost1,
+    sums,
+    edge2,
+    inner3,
+    out_a,
+    out_b,
+    low,
+    high,
+):
+    ny = own.shape[1]
+    take(got_a, got_b, low, high)
+    heights = Heights(width, own, beside)
+    old = Field(width, nz, edge0, near=(near_low, near_high))
+    ghost = Field(width, nz, ghost=ghost1)
 
     def body(z):
         lev = levels(z, nz, ny)
-        for p, known, own, ref in ((-1, PLUS, MINUS, got[0]), (width, MINUS, PLUS, got[1])):
-            g = [None] * Q
-            for k, i in enumerate(known + FLAT):
-                g[i] = rows_at(ref, k * nz + z)
-            for i in own:
+        for e, (p, known, mine, ref) in enumerate(((-1, PLUS, MINUS, low), (width, MINUS, PLUS, high))):
+            g = {i: rows_at(ref, k * nz + z) for k, i in enumerate(known)}
+            for i in mine:
                 g[i] = pull(old, heights, lev, i, p, z)
-            post = collide_all(g)
-            for i in range(Q):
+            flat = [rows_at(ref, (NP + k) * nz + z) for k in range(3)]
+            plus, minus = side_moments(g, PLUS), side_moments(g, MINUS)
+            total = (
+                flat[0] + (plus[0] + minus[0]),
+                plus[0] - minus[0],
+                flat[1] + (plus[1] + minus[1]),
+                flat[2] + (plus[2] + minus[2]),
+            )
+            post = after(g, total, 1, STEPS, known + mine)
+            for i in known + mine:
+                ghost.store(i, p, z, post[i])
+            for k, row in enumerate(total + tuple(flat)):
+                put_rows(sums, (7 * e + k) * nz + z, row)
+
+    over_rows(nz, body)
+    step_planes(2, STEPS, Field(width, nz, edge1, inner1, ghost1), Field(width, nz, edge2), heights, (0, width - 1), nz, ny)
+    both = Field(width, nz, edge2, inner2)
+    step_planes(3, STEPS, both, Field(width, nz, None, inner3), heights, range(1, width - 1), nz, ny)
+    give_second(inner3, width, nz, out_a, out_b)
+
+
+def ghost_flats(width, nz, sums, low, high, flats):
+    new = Field(width, nz, flats=flats)
+
+    def body(z):
+        for e, (p, ref) in enumerate(((-1, low), (width, high))):
+            g = {i: rows_at(ref, (NP + k) * nz + z) for k, i in enumerate(REST)}
+            row = [rows_at(sums, (7 * e + k) * nz + z) for k in range(7)]
+            flat_from_rest(g, *row[4:])
+            post = after(g, row[:4], 1, STEPS, FLAT)
+            for i in FLAT:
                 new.store(i, p, z, post[i])
 
     over_rows(nz, body)
@@ -371,7 +466,8 @@
 
     own, beside, edge_old, edge, inner = pop(5)
     inner_next = pop(1)[0] if s + 2 <= steps else None
-    extra = pop(2) if s == 1 else pop(1)
+    (ghost_old,) = pop(1)
+    sums = pop(1)[0] if s == 2 else None
     got_a, got_b = pop(2)
     if s + 1 == steps:
         pop(1)
@@ -390,30 +486,29 @@
     if s + 1 == steps:
         (ghost,) = pop(1)
     take(got_a, got_b, low, high)
-    if s == 1:
-        first_ghost(width, nz, ny, heights, edge_old, extra, (low, high), ghost)
-    else:
-        old = Field(width, nz, edge_old, ghost=extra[0], far=(low, high))
-        step_planes(old, Field(width, nz, ghost=ghost), heights, (-1, width), nz, ny)
+    flats = pop(1)[0] if s == 2 else None
+    if s == 2:
+        ghost_flats(width, nz, sums, low, high, flats)
+    old = Field(width, nz, edge_old, ghost=ghost_old, far=(low, high), flats=flats)
+    step_planes(s, steps, old, Field(width, nz, ghost=ghost), heights, (-1, width), nz, ny)
     field = Field(width, nz, edge, inner, ghost)
     if s + 1 == steps:
         buf, sem = refs
         for c in write_planes(field, heights, nz, ny, (0, width - 1), out, buf, sem):
             c.wait()
         return
-    step_planes(field, Field(width, nz, edge_new), heights, (0, width - 1), nz, ny)
+    step_planes(s + 1, steps, field, Field(width, nz, edge_new), heights, (0, width - 1), nz, ny)
     field = Field(width, nz, edge_new, inner_next)
     if s + 2 == steps:
         buf, sem = refs
         for c in write_planes(field, heights, nz, ny, range(1, width - 1), out, buf, sem):
             c.wait()
         return
-    step_planes(field, Field(width, nz, None, inner_new), heights, range(1, width - 1), nz, ny)
+    step_planes(s + 2, steps, field, Field(width, nz, None, inner_new), heights, range(1, width - 1), nz, ny)
     if s + 3 < steps:
         give_second(inner_new, width, nz, out_a, out_b)
 
 
-UNROLL = 2
 VMEM_LIMIT = 24 * 1024 * 1024
 
 
@@ -421,7 +516,7 @@
     _, width, nz, ny = pops.shape
     pops, heights = (pltpu.with_memory_space_constraint(x, pltpu.HBM) for x in (pops, heights))
     devices = lax.axis_size("gx")
-    assert width >= 3 and nz % SUB == 0 and devices % 2 == 0 and STEPS >= 4
+    assert width >= 3 and nz % SUB == 0 and devices % 2 == 0 and STEPS >= 5
     pair_a = [(i, i ^ 1) for i in range(devices)]
     pair_b = [(i, (i + 1 if i % 2 else i - 1) % devices) for i in range(devices)]
 
@@ -436,7 +531,8 @@
     edge_t = rows(Q * 2 * nz)
     inner_t = rows(Q * (width - 2) * nz)
     near_n = NP * nz + 2 * SUB
-    set_n = (NP + len(FLAT)) * nz
+    sums_n = (NP + 3) * nz
+    rest_n = (NP + len(REST)) * nz
     far_n = NP * nz
     dma = pltpu.SemaphoreType.DMA
 
@@ -474,17 +570,17 @@
         in_specs=[hbm, hbm],
     )
     near = exchange(a, b)
-    inner0, a, b = call(
+    inner0, a, b, rest = call(
         inner0_kernel,
         [pops, own, edge0],
-        [inner_t, rows(set_n), rows(set_n)],
+        [inner_t, rows(sums_n), rows(sums_n), rows(2 * len(REST) * nz)],
         width,
-        [pltpu.VMEM((Q, width - 2, nz, ny), jnp.float32), scratch(set_n), scratch(set_n), dma],
+        [pltpu.VMEM((Q, width - 2, nz, ny), jnp.float32), scratch(sums_n), scratch(sums_n), dma],
         in_specs=[hbm, vmem, vmem],
     )
-    messages = {1: exchange(a, b)}
-    inner1, a, b = call(inner1_kernel, [own, edge0, inner0], [inner_t, rows(far_n), rows(far_n)], width - 2)
-    messages[2] = exchange(a, b)
+    first = exchange(a, b)
+    inner1, a, b = call(inner1_kernel, [own, edge0, inner0, rest], [inner_t, rows(rest_n), rows(rest_n)], width - 2)
+    messages = {2: exchange(a, b)}
     edge1, inner2, a, b, beside, low, high = call(
         edge1_kernel,
         [own, edge0, inner0, inner1, *near],
@@ -492,18 +588,28 @@
         width,
     )
     messages[3] = exchange(a, b)
-    edges, inners, ghost = {0: edge0, 1: edge1}, {1: inner1, 2: inner2}, None
+    ghost, sums, edge2, inner3, a, b = call(
+        edge2_kernel,
+        [own, beside, low, high, edge0, edge1, inner1, inner2, *first],
+        [edge_t, rows(14 * nz), edge_t, inner_t, rows(far_n), rows(far_n)],
+        width + 2,
+        [scratch(sums_n), scratch(sums_n)],
+    )
+    messages[4] = exchange(a, b)
+    edges, inners = {1: edge1, 2: edge2}, {2: inner2, 3: inner3}
     out_t = jax.ShapeDtypeStruct(pops.shape, pops.dtype)
     out = None
-    for s in range(1, STEPS):
+    for s in range(2, STEPS):
         args = [own, beside, edges[s - 1], edges[s], inners[s]]
         if s + 2 <= STEPS:
             args.append(inners[s + 1])
-        args += [low, high] if s == 1 else [ghost]
+        args += [ghost, sums] if s == 2 else [ghost]
         args += messages[s]
         outs, spaces, aliases = [], [], {}
-        n = set_n if s == 1 else far_n
+        n = rest_n if s == 2 else far_n
         extra = [scratch(n), scratch(n)]
+        if s == 2:
+            extra.append(scratch(2 * len(FLAT) * nz))
         specs = [vmem] * len(args)
         if s + 1 < STEPS:
             outs += [edge_t, edge_t]

time: 48.9 us -> 43.1 us (0.88)
  Pallas kernels: 20 us -> 12.7 us
  waiting for transfers between devices: 2.74 us -> 4.53 us
    pallas_call x9, Pallas kernels: 20 us -> 12.7 us  [call(): pl.pallas_call(functools.partial(kernel, width, nz), out_shape=outs, in_s...]
    ppermute x6, waiting for transfers between devices: 2.72 us -> 4.51 us  [exchange(): b = lax.ppermute(b, 'gx', pair_b)]
  transfers between devices with their start and end apart: 12 -> 12, of which waited for: 1 -> 2; matrix products, arithmetic and copies ran while one was open for 0% -> 0% of each run, Pallas kernels for 27% -> 22%
where the time goes in v3:
time: 43.1 us; the launch traced here: 42.9 us
  starting transfers between devices  25.6 us (59%)
  Pallas kernels  12.7 us (29%)
  waiting for transfers between devices  4.53 us (11%)
    ppermute x6, starting transfers between devices, exchange(): b = lax.ppermute(b, 'gx', pair_b)  19.5 us
    pallas_call x9, Pallas kernels, call(): pl.pallas_call(functools.partial(kernel, width, nz), out_shape=outs, in_s...  12.7 us
    ppermute x6, starting transfers between devices, exchange(): a = lax.ppermute(a, 'gx', pair_a)  6.09 us
    ppermute x6, waiting for transfers between devices, exchange(): b = lax.ppermute(b, 'gx', pair_b)  4.51 us
  transfers between devices with their start and end apart: 12, of which 2 were waited for; matrix products, arithmetic and copies ran while one was open for 0% of the time, Pallas kernels for 22%

profile of v3, /device:TPU:0, one launch (start us, length us, event | category | flops | bytes accessed | tf_op | source)
XLA Modules:
  0.0 42.9 jit_solution(6011393107092483872)
XLA Ops:
  0.0 1.7 %shard_map.28 = (f32[2432,128]{1,0:T(8,128)S(1)}, f32[336,128]{1,0:T(8,128)S(1)}, f32[336,128]{1,0:T(8,128)S(1)}, f32[96,128]{1,0:T(8,128)S(1)}) custom-call(f32[19,4,64,128]{3,2,1,0:T(8,128)} %pops.3, s32[4,128]{1,0:T(4,128)} %h_hbm.1), custom_call_target="tpu_custom_call" | custom-call | flops 4096000 | bytes 2490368 | tf_op jit(solution)/shard_map/pallas_call | solution.py:540
  1.7 0.6 %collective-permute-start = (f32[336,128]{1,0:T(8,128)S(1)}, f32[336,128]{1,0:T(8,128)S(1)}, u32[]{:S(2)}, u32[]{:S(2)}) collective-permute-start(f32[336,128]{1,0:T(8,128)S(1)} %get-tuple-element.45), channel_id=1, source_target_pairs={{0,1},{1,0},{2,3},{3,2},{4,5},{5,4},{6,7},{7,6},{8,9},{9,8},{10,11... | collective-permute-start | bytes 516104 | tf_op jit(solution)/shard_map/ppermute | solution.py:554
  2.3 1.8 %shard_map.29 = (f32[2432,128]{1,0:T(8,128)S(1)}, f32[512,128]{1,0:T(8,128)S(1)}, f32[512,128]{1,0:T(8,128)S(1)}, f32[768,128]{1,0:T(8,128)S(1)}) custom-call(f32[19,4,64,128]{3,2,1,0:T(8,128)} %pops.3, f32[96,128]{1,0:T(8,128)S(1)} %get-tuple-element.40.own.refs_0_, f32[2432,128]{1,0:T(8,128)S(1)} %get-tuple-element.41.edge.edge0), custom_call_target="tpu_custom_call" | custom-call | flops 8192000 | bytes 4980736 | tf_op jit(solution)/shard_map/pallas_call | solution.py:540
  4.1 0.5 %shard_map.30 = (f32[2432,128]{1,0:T(8,128)S(1)}, f32[704,128]{1,0:T(8,128)S(1)}, f32[704,128]{1,0:T(8,128)S(1)}) custom-call(f32[96,128]{1,0:T(8,128)S(1)} %get-tuple-element.40.own.refs_0_, f32[2432,128]{1,0:T(8,128)S(1)} %get-tuple-element.41.edge.edge0, f32[2432,128]{1,0:T(8,128)S(1)} %get-tuple-element.42.inner.inner0, ...), custom_call_target="tpu_custom_call" | custom-call | flops 4096000 | bytes 2490368 | tf_op jit(solution)/shard_map/pallas_call | solution.py:540
  4.7 0.1 collective-permute-start.4
  4.8 5.7 %collective-permute-start.5 = (f32[704,128]{1,0:T(8,128)S(1)}, f32[704,128]{1,0:T(8,128)S(1)}, u32[]{:S(2)}, u32[]{:S(2)}) collective-permute-start(f32[704,128]{1,0:T(8,128)S(1)} %get-tuple-element.59), channel_id=1, source_target_pairs={{0,15},{1,2},{2,1},{3,4},{4,3},{5,6},{6,5},{7,8},{8,7},{9,10},{10,... | collective-permute-start | bytes 1081352 | tf_op jit(solution)/shard_map/ppermute | solution.py:555
  10.5 0.1 collective-permute-start.1
  10.6 0.0 collective-permute-done.got_a
  10.6 4.4 %collective-permute-start.3 = (f32[512,128]{1,0:T(8,128)S(1)}, f32[512,128]{1,0:T(8,128)S(1)}, u32[]{:S(2)}, u32[]{:S(2)}) collective-permute-start(f32[512,128]{1,0:T(8,128)S(1)} %get-tuple-element.53), channel_id=1, source_target_pairs={{0,15},{1,2},{2,1},{3,4},{4,3},{5,6},{6,5},{7,8},{8,7},{9,10},{10,... | collective-permute-start | bytes 786440 | tf_op jit(solution)/shard_map/ppermute | solution.py:555
  14.9 3.2 %collective-permute-done.1.got_b = f32[336,128]{1,0:T(8,128)S(1)} collective-permute-done((f32[336,128]{1,0:T(8,128)S(1)}, f32[336,128]{1,0:T(8,128)S(1)}, u32[]{:S(2)}, u32[]{:S(2)}) %collective-permute-start.1) | collective-permute-done | bytes 172064 | tf_op jit(solution)/shard_map/ppermute | solution.py:555
  18.1 0.9 %shard_map.31 = (f32[2432,128]{1,0:T(8,128)S(1)}, f32[2432,128]{1,0:T(8,128)S(1)}, f32[320,128]{1,0:T(8,128)S(1)}, f32[320,128]{1,0:T(8,128)S(1)}, f32[96,128]{1...) custom-call(f32[96,128]{1,0:T(8,128)S(1)} %get-tuple-element.40.own.refs_0_, ...), custom_call_target="tpu_custom_call" | custom-call | flops 8192000 | bytes 4980736 | tf_op jit(solution)/shard_map/pallas_call | solution.py:540
  19.0 5.3 %collective-permute-start.6 = (f32[320,128]{1,0:T(8,128)S(1)}, f32[320,128]{1,0:T(8,128)S(1)}, u32[]{:S(2)}, u32[]{:S(2)}) collective-permute-start(f32[320,128]{1,0:T(8,128)S(1)} %get-tuple-element.63), channel_id=1, source_target_pairs={{0,1},{1,0},{2,3},{3,2},{4,5},{5,4},{6,7},{7,6},{8,9},{9,8},{10,11... | collective-permute-start | bytes 491528 | tf_op jit(solution)/shard_map/ppermute | solution.py:554
  24.3 4.8 %collective-permute-start.7 = (f32[320,128]{1,0:T(8,128)S(1)}, f32[320,128]{1,0:T(8,128)S(1)}, u32[]{:S(2)}, u32[]{:S(2)}) collective-permute-start(f32[320,128]{1,0:T(8,128)S(1)} %get-tuple-element.64), channel_id=1, source_target_pairs={{0,15},{1,2},{2,1},{3,4},{4,3},{5,6},{6,5},{7,8},{8,7},{9,10},{10,... | collective-permute-start | bytes 491528 | tf_op jit(solution)/shard_map/ppermute | solution.py:555
  29.1 1.1 %shard_map.32 = (f32[2432,128]{1,0:T(8,128)S(1)}, f32[896,128]{1,0:T(8,128)S(1)}, f32[2432,128]{1,0:T(8,128)S(1)}, f32[2432,128]{1,0:T(8,128)S(1)}, f32[320,128]{1,0:T(8,128)S(1)}, /*index=5*/f32[320,128]{1,0:T(8,128)S(1)}) custom-call(f32[96,128]{1,0:T(8,128)S(1)} %get-tuple-element.40.own.refs_0_, f32[96,128]{1,0:T(8,128)S(1)} %get-tuple-element.47.beside.refs_1_, ...), custom_call_target="tpu_custom_call" | custom-call | flops 12288000 | bytes 7471104 | tf_op jit(solution)/shard_map/pallas_call | solution.py:540
  30.3 0.1 collective-permute-start.8
  30.4 0.0 collective-permute-done.4.refs_8_
  30.4 1.8 %collective-permute-start.9 = (f32[320,128]{1,0:T(8,128)S(1)}, f32[320,128]{1,0:T(8,128)S(1)}, u32[]{:S(2)}, u32[]{:S(2)}) collective-permute-start(f32[320,128]{1,0:T(8,128)S(1)} %get-tuple-element.69), channel_id=1, source_target_pairs={{0,15},{1,2},{2,1},{3,4},{4,3},{5,6},{6,5},{7,8},{8,7},{9,10},{10,... | collective-permute-start | bytes 491528 | tf_op jit(solution)/shard_map/ppermute | solution.py:555
  32.1 1.5 %shard_map.33 = (f32[2432,128]{1,0:T(8,128)S(1)}, f32[2432,128]{1,0:T(8,128)S(1)}, f32[2432,128]{1,0:T(8,128)S(1)}, f32[320,128]{1,0:T(8,128)S(1)}, f32[320,128]{1,0:T(8,128)S(1)}) custom-call(f32[96,128]{1,0:T(8,128)S(1)} %get-tuple-element.40.own.refs_0_, f32[96,128]{1,0:T(8,128)S(1)} %get-tuple-element.47.beside.refs_1_, ...), custom_call_target="tpu_custom_call" | custom-call | flops 12288000 | bytes 7471104 | tf_op jit(solution)/shard_map/pallas_call | solution.py:540
  33.7 0.1 collective-permute-start.10
  33.8 2.8 %collective-permute-start.11 = (f32[320,128]{1,0:T(8,128)S(1)}, f32[320,128]{1,0:T(8,128)S(1)}, u32[]{:S(2)}, u32[]{:S(2)}) collective-permute-start(f32[320,128]{1,0:T(8,128)S(1)} %get-tuple-element.73), channel_id=1, source_target_pairs={{0,15},{1,2},{2,1},{3,4},{4,3},{5,6},{6,5},{7,8},{8,7},{9,10},{10,... | collective-permute-start | bytes 491528 | tf_op jit(solution)/shard_map/ppermute | solution.py:555
  36.6 1.3 %shard_map.34 = (f32[2432,128]{1,0:T(8,128)S(1)}, f32[2432,128]{1,0:T(8,128)S(1)}, f32[2432,128]{1,0:T(8,128)S(1)}) custom-call(f32[96,128]{1,0:T(8,128)S(1)} %get-tuple-element.40.own.refs_0_, f32[96,128]{1,0:T(8,128)S(1)} %get-tuple-element.47.beside.refs_1_, f32[2432,128]{1,0:T(8,128)S(1)} %get-tuple-element.54.refs_3_.refs_2_, ...), custom_call_target="tpu_custom_call" | custom-call | flops 12288000 | bytes 7471104 | tf_op jit(solution)/shard_map/pallas_call | solution.py:540
  37.9 2.1 %shard_map.35 = (f32[2432,128]{1,0:T(8,128)S(1)}, f32[2432,128]{1,0:T(8,128)S(1)}, f32[19,4,64,128]{3,2,1,0:T(8,128)}) custom-call(f32[96,128]{1,0:T(8,128)S(1)} %get-tuple-element.40.own.refs_0_, f32[96,128]{1,0:T(8,128)S(1)} %get-tuple-element.47.beside.refs_1_, f32[2432,128]{1,0:T(8,128)S(1)} %get-tuple-element.60.refs_3_.refs_2_, ...), custom_call_target="tpu_custom_call" | custom-call | flops 12288000 | bytes 7471104 | tf_op jit(solution)/shard_map/pallas_call | solution.py:540
  40.1 1.3 %collective-permute-done.11.refs_7_ = f32[320,128]{1,0:T(8,128)S(1)} collective-permute-done((f32[320,128]{1,0:T(8,128)S(1)}, f32[320,128]{1,0:T(8,128)S(1)}, u32[]{:S(2)}, u32[]{:S(2)}) %collective-permute-start.11) | collective-permute-done | bytes 163872 | tf_op jit(solution)/shard_map/ppermute | solution.py:555
  41.4 1.5 %shard_map.36 = f32[19,4,64,128]{3,2,1,0:T(8,128)} custom-call(f32[96,128]{1,0:T(8,128)S(1)} %get-tuple-element.40.own.refs_0_, f32[96,128]{1,0:T(8,128)S(1)} %get-tuple-element.47.beside.refs_1_, f32[2432,128]{1,0:T(8,128)S(1)} %get-tuple-element.65.refs_3_.refs_2_, f32[2432,128]{1,0:T(8,128)S(1)} %get-tuple-element.70.refs_3_, ...), custom_call_target="tpu_custom_call", output_to_operand_aliasing={{}: (8, {})} | custom-call | flops 12288000 | bytes 7471104 | tf_op jit(solution)/shard_map/pallas_call | solution.py:540
  (9 shorter events, 0.0 us)
Async XLA Ops:
  1.7 8.9 %collective-permute-start = (f32[336,128]{1,0:T(8,128)S(1)}, f32[336,128]{1,0:T(8,128)S(1)}, u32[]{:S(2)}, u32[]{:S(2)}) collective-permute-start(f32[336,128]{1,0:T(8,128)S(1)} %get-tuple-element.45), channel_id=1, source_target_pairs={{0,1},{1,0},{2,3},{3,2},{4,5},{5,4},{6,7},{7,6},{8,9},{9,8},{10,11... | collective-permute-start | bytes 516104 | tf_op jit(solution)/shard_map/ppermute | solution.py:554
  4.7 25.7 %collective-permute-start.4 = (f32[704,128]{1,0:T(8,128)S(1)}, f32[704,128]{1,0:T(8,128)S(1)}, u32[]{:S(2)}, u32[]{:S(2)}) collective-permute-start(f32[704,128]{1,0:T(8,128)S(1)} %get-tuple-element.58), channel_id=1, source_target_pairs={{0,1},{1,0},{2,3},{3,2},{4,5},{5,4},{6,7},{7,6},{8,9},{9,8},{10,11... | collective-permute-start | bytes 1081352 | tf_op jit(solution)/shard_map/ppermute | solution.py:554
  4.8 27.4 %collective-permute-start.5 = (f32[704,128]{1,0:T(8,128)S(1)}, f32[704,128]{1,0:T(8,128)S(1)}, u32[]{:S(2)}, u32[]{:S(2)}) collective-permute-start(f32[704,128]{1,0:T(8,128)S(1)} %get-tuple-element.59), channel_id=1, source_target_pairs={{0,15},{1,2},{2,1},{3,4},{4,3},{5,6},{6,5},{7,8},{8,7},{9,10},{10,... | collective-permute-start | bytes 1081352 | tf_op jit(solution)/shard_map/ppermute | solution.py:555
  10.5 7.6 %collective-permute-start.1 = (f32[336,128]{1,0:T(8,128)S(1)}, f32[336,128]{1,0:T(8,128)S(1)}, u32[]{:S(2)}, u32[]{:S(2)}) collective-permute-start(f32[336,128]{1,0:T(8,128)S(1)} %get-tuple-element.46), channel_id=1, source_target_pairs={{0,15},{1,2},{2,1},{3,4},{4,3},{5,6},{6,5},{7,8},{8,7},{9,10},{10,... | collective-permute-start | bytes 516104 | tf_op jit(solution)/shard_map/ppermute | solution.py:555
  10.5 13.8 %collective-permute-start.2 = (f32[512,128]{1,0:T(8,128)S(1)}, f32[512,128]{1,0:T(8,128)S(1)}, u32[]{:S(2)}, u32[]{:S(2)}) collective-permute-start(f32[512,128]{1,0:T(8,128)S(1)} %get-tuple-element.52), channel_id=1, source_target_pairs={{0,1},{1,0},{2,3},{3,2},{4,5},{5,4},{6,7},{7,6},{8,9},{9,8},{10,11... | collective-permute-start | bytes 786440 | tf_op jit(solution)/shard_map/ppermute | solution.py:554
  10.6 18.6 %collective-permute-start.3 = (f32[512,128]{1,0:T(8,128)S(1)}, f32[512,128]{1,0:T(8,128)S(1)}, u32[]{:S(2)}, u32[]{:S(2)}) collective-permute-start(f32[512,128]{1,0:T(8,128)S(1)} %get-tuple-element.53), channel_id=1, source_target_pairs={{0,15},{1,2},{2,1},{3,4},{4,3},{5,6},{6,5},{7,8},{8,7},{9,10},{10,... | collective-permute-start | bytes 786440 | tf_op jit(solution)/shard_map/ppermute | solution.py:555
  19.0 14.7 %collective-permute-start.6 = (f32[320,128]{1,0:T(8,128)S(1)}, f32[320,128]{1,0:T(8,128)S(1)}, u32[]{:S(2)}, u32[]{:S(2)}) collective-permute-start(f32[320,128]{1,0:T(8,128)S(1)} %get-tuple-element.63), channel_id=1, source_target_pairs={{0,1},{1,0},{2,3},{3,2},{4,5},{5,4},{6,7},{7,6},{8,9},{9,8},{10,11... | collective-permute-start | bytes 491528 | tf_op jit(solution)/shard_map/ppermute | solution.py:554
  24.3 12.2 %collective-permute-start.7 = (f32[320,128]{1,0:T(8,128)S(1)}, f32[320,128]{1,0:T(8,128)S(1)}, u32[]{:S(2)}, u32[]{:S(2)}) collective-permute-start(f32[320,128]{1,0:T(8,128)S(1)} %get-tuple-element.64), channel_id=1, source_target_pairs={{0,15},{1,2},{2,1},{3,4},{4,3},{5,6},{6,5},{7,8},{8,7},{9,10},{10,... | collective-permute-start | bytes 491528 | tf_op jit(solution)/shard_map/ppermute | solution.py:555
  30.3 7.6 %collective-permute-start.8 = (f32[320,128]{1,0:T(8,128)S(1)}, f32[320,128]{1,0:T(8,128)S(1)}, u32[]{:S(2)}, u32[]{:S(2)}) collective-permute-start(f32[320,128]{1,0:T(8,128)S(1)} %get-tuple-element.68), channel_id=1, source_target_pairs={{0,1},{1,0},{2,3},{3,2},{4,5},{5,4},{6,7},{7,6},{8,9},{9,8},{10,11... | collective-permute-start | bytes 491528 | tf_op jit(solution)/shard_map/ppermute | solution.py:554
  30.4 7.6 %collective-permute-start.9 = (f32[320,128]{1,0:T(8,128)S(1)}, f32[320,128]{1,0:T(8,128)S(1)}, u32[]{:S(2)}, u32[]{:S(2)}) collective-permute-start(f32[320,128]{1,0:T(8,128)S(1)} %get-tuple-element.69), channel_id=1, source_target_pairs={{0,15},{1,2},{2,1},{3,4},{4,3},{5,6},{6,5},{7,8},{8,7},{9,10},{10,... | collective-permute-start | bytes 491528 | tf_op jit(solution)/shard_map/ppermute | solution.py:555
  33.7 6.4 %collective-permute-start.10 = (f32[320,128]{1,0:T(8,128)S(1)}, f32[320,128]{1,0:T(8,128)S(1)}, u32[]{:S(2)}, u32[]{:S(2)}) collective-permute-start(f32[320,128]{1,0:T(8,128)S(1)} %get-tuple-element.72), channel_id=1, source_target_pairs={{0,1},{1,0},{2,3},{3,2},{4,5},{5,4},{6,7},{7,6},{8,9},{9,8},{10,11... | collective-permute-start | bytes 491528 | tf_op jit(solution)/shard_map/ppermute | solution.py:554
  33.8 7.6 %collective-permute-start.11 = (f32[320,128]{1,0:T(8,128)S(1)}, f32[320,128]{1,0:T(8,128)S(1)}, u32[]{:S(2)}, u32[]{:S(2)}) collective-permute-start(f32[320,128]{1,0:T(8,128)S(1)} %get-tuple-element.73), channel_id=1, source_target_pairs={{0,15},{1,2},{2,1},{3,4},{4,3},{5,6},{6,5},{7,8},{8,7},{9,10},{10,... | collective-permute-start | bytes 491528 | tf_op jit(solution)/shard_map/ppermute | solution.py:555

commit v4 on v3

--- a/solution.py
+++ b/solution.py
@@ -286,11 +286,16 @@
 def edge0_kernel(width, nz, pops, h_hbm, edge, out_a, out_b, own, buf, h, up, down, sem):
     ny = h.shape[1]
     edges = (0, width - 1)
-    copies = [pltpu.make_async_copy(pops.at[:, p], buf.at[:, e], sem.at[e]) for e, p in enumerate(edges)]
-    copies.append(pltpu.make_async_copy(h_hbm, h, sem.at[2]))
-    for c in copies:
+    part = nz // HEAD_PARTS
+    copies = []
+    for k in range(HEAD_PARTS):
+        rows = pl.ds(k * part, part)
+        for e, p in enumerate(edges):
+            copies.append(pltpu.make_async_copy(pops.at[:, p, rows], buf.at[:, e, rows], sem.at[2 * k + e]))
+    heights = pltpu.make_async_copy(h_hbm, h, sem.at[2 * HEAD_PARTS])
+    for c in copies + [heights]:
         c.start()
-    copies[2].wait()
+    heights.wait()
     hf = h[...].astype(jnp.float32)
     for p in range(width):
         row = jnp.broadcast_to(hf[p : p + 1], (SUB, ny))
@@ -299,21 +304,19 @@
             if first <= p < first + 2:
                 put_rows(out, NP * nz + (p - first) * SUB, row)
     field = Field(width, nz, edge)
-    copies[0].wait()
-    copies[1].wait()
-
-    def body(z):
-        for e, p in enumerate(edges):
-            post = collide([buf[i, e, pl.ds(z, SUB), :] for i in range(Q)], 0, STEPS)
-            for i in range(Q):
-                field.store(i, p, z, post[i])
-            for k in range(NP):
-                if e:
-                    put_rows(up, k * nz + z, post[PLUS[k]])
-                else:
-                    put_rows(down, k * nz + z, post[MINUS[k]])
-
-    over_rows(nz, body)
+    for k in range(HEAD_PARTS):
+        copies[2 * k].wait()
+        copies[2 * k + 1].wait()
+        for z in range(k * part, (k + 1) * part, SUB):
+            for e, p in enumerate(edges):
+                post = collide([buf[i, e, pl.ds(z, SUB), :] for i in range(Q)], 0, STEPS)
+                for i in range(Q):
+                    field.store(i, p, z, post[i])
+                for j in range(NP):
+                    if e:
+                        put_rows(up, j * nz + z, post[PLUS[j]])
+                    else:
+                        put_rows(down, j * nz + z, post[MINUS[j]])
     give(up, down, out_a, out_b)
 
 
@@ -441,19 +444,72 @@
     over_rows(nz, body)
 
 
-def write_planes(field, heights, nz, ny, planes, out, buf, sem):
+def runs(comps):
+    found = []
+    for i in range(Q):
+        if i in comps:
+            continue
+        if found and sum(found[-1]) == i:
+            found[-1] = (found[-1][0], found[-1][1] + 1)
+        else:
+            found.append((i, 1))
+    return found
+
+
+def last_planes(field, heights, width, nz, ny, out, done, sem):
     copies = []
-    for k, p in enumerate(planes):
-
-        def body(z, p=p, k=k):
+    for p in list(range(1, width - 1)) + [0, width - 1]:
+        late = {0: PLUS, width - 1: MINUS}.get(p, [])
+
+        def body(z, p=p, late=late):
             lev = levels(z, nz, ny)
             for i in range(Q):
-                buf[i, k, pl.ds(z, SUB), :] = pull(field, heights, lev, i, p, z)
+                if i not in late:
+                    done[i, p, pl.ds(z, SUB), :] = pull(field, heights, lev, i, p, z)
 
         over_rows(nz, body)
-        copies.append(pltpu.make_async_copy(buf.at[:, k], out.at[:, p], sem.at[k]))
-        copies[-1].start()
-    return copies
+        for first, count in runs(late):
+            part = pl.ds(first, count)
+            copies.append(pltpu.make_async_copy(done.at[part, p], out.at[part, p], sem.at[len(copies)]))
+            copies[-1].start()
+    for c in copies:
+        c.wait()
+
+
+def enter_kernel(
+    width, nz, own, beside, edge_old, edge, ghost_old, got_a, got_b, _, out, low, high, enter_low, enter_high, buf, sem
+):
+    ny = own.shape[1]
+    heights = Heights(width, own, beside)
+    copies = []
+    take(got_a, got_b, low, high)
+    old = Field(width, nz, edge_old, ghost=ghost_old, far=(low, high))
+    ghost = (enter_low, enter_high)
+    new = Field(width, nz, near=ghost)
+
+    def body(z):
+        lev = levels(z, nz, ny)
+        for p, comps in ((-1, PLUS), (width, MINUS)):
+            g = [pull(old, heights, lev, i, p, z) for i in range(Q)]
+            post = after(g, moments(g), STEPS - 1, STEPS, comps)
+            for i in comps:
+                new.store(i, p, z, post[i])
+
+    over_rows(nz, body)
+    field = Field(width, nz, edge, near=ghost)
+    for e, (p, comps) in enumerate(((0, PLUS), (width - 1, MINUS))):
+
+        def enter(z, e=e, p=p, comps=comps):
+            lev = levels(z, nz, ny)
+            for k, i in enumerate(comps):
+                buf[e, k, pl.ds(z, SUB), :] = pull(field, heights, lev, i, p, z)
+
+        over_rows(nz, enter)
+        for k, i in enumerate(comps):
+            copies.append(pltpu.make_async_copy(buf.at[e, k], out.at[i, p], sem.at[len(copies)]))
+            copies[-1].start()
+    for c in copies:
+        c.wait()
 
 
 def step_kernel(s, steps, width, nz, *refs):
@@ -464,51 +520,32 @@
         del refs[:n]
         return taken
 
-    own, beside, edge_old, edge, inner = pop(5)
-    inner_next = pop(1)[0] if s + 2 <= steps else None
-    (ghost_old,) = pop(1)
+    own, beside, edge_old, edge, inner, inner_next, ghost_old = pop(7)
     sums = pop(1)[0] if s == 2 else None
-    got_a, got_b = pop(2)
-    if s + 1 == steps:
-        pop(1)
+    got_a, got_b, ghost, edge_new, new = pop(5)
+    out_a, out_b = pop(2) if s + 3 < steps else (None, None)
+    low, high = pop(2)
+    flats = pop(1)[0] if s == 2 else None
+    done, sem = pop(2) if s + 2 == steps else (None, None)
     ny = own.shape[1]
     heights = Heights(width, own, beside)
-    ghost = edge_new = inner_new = out = out_a = out_b = None
-    if s + 1 < steps:
-        ghost, edge_new = pop(2)
-    if s + 2 < steps:
-        (inner_new,) = pop(1)
-    else:
-        (out,) = pop(1)
-    if s + 3 < steps:
-        out_a, out_b = pop(2)
-    low, high = pop(2)
-    if s + 1 == steps:
-        (ghost,) = pop(1)
     take(got_a, got_b, low, high)
-    flats = pop(1)[0] if s == 2 else None
     if s == 2:
         ghost_flats(width, nz, sums, low, high, flats)
     old = Field(width, nz, edge_old, ghost=ghost_old, far=(low, high), flats=flats)
     step_planes(s, steps, old, Field(width, nz, ghost=ghost), heights, (-1, width), nz, ny)
     field = Field(width, nz, edge, inner, ghost)
-    if s + 1 == steps:
-        buf, sem = refs
-        for c in write_planes(field, heights, nz, ny, (0, width - 1), out, buf, sem):
-            c.wait()
-        return
     step_planes(s + 1, steps, field, Field(width, nz, edge_new), heights, (0, width - 1), nz, ny)
     field = Field(width, nz, edge_new, inner_next)
     if s + 2 == steps:
-        buf, sem = refs
-        for c in write_planes(field, heights, nz, ny, range(1, width - 1), out, buf, sem):
-            c.wait()
+        last_planes(field, heights, width, nz, ny, new, done, sem)
         return
-    step_planes(s + 2, steps, field, Field(width, nz, None, inner_new), heights, range(1, width - 1), nz, ny)
+    step_planes(s + 2, steps, field, Field(width, nz, None, new), heights, range(1, width - 1), nz, ny)
     if s + 3 < steps:
-        give_second(inner_new, width, nz, out_a, out_b)
-
-
+        give_second(new, width, nz, out_a, out_b)
+
+
+HEAD_PARTS = 2
 VMEM_LIMIT = 24 * 1024 * 1024
 
 
@@ -516,7 +553,7 @@
     _, width, nz, ny = pops.shape
     pops, heights = (pltpu.with_memory_space_constraint(x, pltpu.HBM) for x in (pops, heights))
     devices = lax.axis_size("gx")
-    assert width >= 3 and nz % SUB == 0 and devices % 2 == 0 and STEPS >= 5
+    assert width >= 3 and nz % (HEAD_PARTS * SUB) == 0 and devices % 2 == 0 and STEPS >= 5
     pair_a = [(i, i ^ 1) for i in range(devices)]
     pair_b = [(i, (i + 1 if i % 2 else i - 1) % devices) for i in range(devices)]
 
@@ -565,7 +602,7 @@
             pltpu.VMEM((width, ny), jnp.int32),
             scratch(near_n),
             scratch(near_n),
-            dma((3,)),
+            dma((2 * HEAD_PARTS + 1,)),
         ],
         in_specs=[hbm, hbm],
     )
@@ -598,58 +635,45 @@
     messages[4] = exchange(a, b)
     edges, inners = {1: edge1, 2: edge2}, {2: inner2, 3: inner3}
     out_t = jax.ShapeDtypeStruct(pops.shape, pops.dtype)
-    out = None
-    for s in range(2, STEPS):
-        args = [own, beside, edges[s - 1], edges[s], inners[s]]
-        if s + 2 <= STEPS:
-            args.append(inners[s + 1])
-        args += [ghost, sums] if s == 2 else [ghost]
-        args += messages[s]
-        outs, spaces, aliases = [], [], {}
-        n = rest_n if s == 2 else far_n
-        extra = [scratch(n), scratch(n)]
+    for s in range(2, STEPS - 1):
+        args = [own, beside, edges[s - 1], edges[s], inners[s], inners[s + 1], ghost]
+        outs = [edge_t, edge_t, inner_t if s + 2 < STEPS else out_t]
+        n = far_n
+        extra = []
         if s == 2:
-            extra.append(scratch(2 * len(FLAT) * nz))
-        specs = [vmem] * len(args)
-        if s + 1 < STEPS:
-            outs += [edge_t, edge_t]
-        else:
-            aliases = {len(args): 0}
-            args.append(out)
-            specs.append(hbm)
-            extra.append(scratch(Q * 2 * nz))
-        spaces = [vmem] * len(outs)
-        if s + 2 < STEPS:
-            outs.append(inner_t)
-            spaces.append(vmem)
-        else:
-            outs.append(out_t)
-            spaces.append(hbm)
-            planes = 2 if s + 1 == STEPS else width - 2
-            extra += [pltpu.VMEM((Q, planes, nz, ny), jnp.float32), dma((planes,))]
+            args.append(sums)
+            n = rest_n
+            extra = [scratch(2 * len(FLAT) * nz)]
+        spaces = [vmem] * 3
         if s + 3 < STEPS:
             outs += [rows(far_n), rows(far_n)]
-            spaces += [vmem, vmem]
-        got = list(call(
+            spaces += [vmem] * 2
+        if s + 2 == STEPS:
+            spaces[2] = hbm
+            copies = width - 2 + 2 * len(runs(PLUS))
+            extra += [pltpu.VMEM((Q, width, nz, ny), jnp.float32), dma((copies,))]
+        ghost, edges[s + 1], inners[s + 2], *given = call(
             functools.partial(step_kernel, s, STEPS),
-            args,
+            args + messages[s],
             outs,
             width + 2,
-            extra,
-            in_specs=specs,
+            [scratch(n), scratch(n)] + extra,
             out_specs=spaces,
-            input_output_aliases=aliases,
-        ))
-        if s + 1 < STEPS:
-            ghost, edges[s + 1] = got[0], got[1]
-            del got[:2]
-        if s + 2 < STEPS:
-            inners[s + 2] = got[0]
-        else:
-            out = got[0]
-        if s + 3 < STEPS:
-            messages[s + 3] = exchange(got[1], got[2])
-    return out
+        )
+        if given:
+            messages[s + 3] = exchange(*given)
+    s = STEPS - 1
+    args = [own, beside, edges[s - 1], edges[s], ghost] + messages[s]
+    return call(
+        enter_kernel,
+        args + [inners[s + 1]],
+        [out_t],
+        2,
+        [scratch(far_n)] * 4 + [pltpu.VMEM((2, NP, nz, ny), jnp.float32), dma((2 * NP,))],
+        in_specs=[vmem] * len(args) + [hbm],
+        out_specs=[hbm],
+        input_output_aliases={len(args): 0},
+    )[0]
 
 
 def solution(mesh):

time: 43.1 us -> 42.7 us (level)
  transfers between devices with their start and end apart: 12 -> 12, of which waited for: 2 -> 2; matrix products, arithmetic and copies ran while one was open for 0% -> 0% of each run, Pallas kernels for 22% -> 23%
where the time goes in v4:
time: 42.7 us; the launch traced here: 42.5 us
  starting transfers between devices  25.6 us (60%)
  Pallas kernels  12.6 us (30%)
  waiting for transfers between devices  4.14 us (10%)
    ppermute x6, starting transfers between devices, exchange(): b = lax.ppermute(b, 'gx', pair_b)  19.5 us
    pallas_call x9, Pallas kernels, call(): pl.pallas_call(functools.partial(kernel, width, nz), out_shape=outs, in_s...  12.6 us
    ppermute x6, starting transfers between devices, exchange(): a = lax.ppermute(a, 'gx', pair_a)  6.08 us
    ppermute x6, waiting for transfers between devices, exchange(): b = lax.ppermute(b, 'gx', pair_b)  4.12 us
  transfers between devices with their start and end apart: 12, of which 2 were waited for; matrix products, arithmetic and copies ran while one was open for 0% of the time, Pallas kernels for 23%

profile of v4, /device:TPU:0, one launch (start us, length us, event | category | flops | bytes accessed | tf_op | source)
XLA Modules:
  0.0 42.5 jit_solution(14772803912104657175)
XLA Ops:
  0.0 1.6 %shard_map.28 = (f32[2432,128]{1,0:T(8,128)S(1)}, f32[336,128]{1,0:T(8,128)S(1)}, f32[336,128]{1,0:T(8,128)S(1)}, f32[96,128]{1,0:T(8,128)S(1)}) custom-call(f32[19,4,64,128]{3,2,1,0:T(8,128)} %pops.3, s32[4,128]{1,0:T(4,128)} %h_hbm.1), custom_call_target="tpu_custom_call" | custom-call | flops 4096000 | bytes 2490368 | tf_op jit(solution)/shard_map/pallas_call | solution.py:577
  1.6 0.6 %collective-permute-start = (f32[336,128]{1,0:T(8,128)S(1)}, f32[336,128]{1,0:T(8,128)S(1)}, u32[]{:S(2)}, u32[]{:S(2)}) collective-permute-start(f32[336,128]{1,0:T(8,128)S(1)} %get-tuple-element.45), channel_id=1, source_target_pairs={{0,1},{1,0},{2,3},{3,2},{4,5},{5,4},{6,7},{7,6},{8,9},{9,8},{10,11... | collective-permute-start | bytes 516104 | tf_op jit(solution)/shard_map/ppermute | solution.py:591
  2.2 1.8 %shard_map.29 = (f32[2432,128]{1,0:T(8,128)S(1)}, f32[512,128]{1,0:T(8,128)S(1)}, f32[512,128]{1,0:T(8,128)S(1)}, f32[768,128]{1,0:T(8,128)S(1)}) custom-call(f32[19,4,64,128]{3,2,1,0:T(8,128)} %pops.3, f32[96,128]{1,0:T(8,128)S(1)} %get-tuple-element.40.own.refs_0_, f32[2432,128]{1,0:T(8,128)S(1)} %get-tuple-element.41.edge.edge0), custom_call_target="tpu_custom_call" | custom-call | flops 8192000 | bytes 4980736 | tf_op jit(solution)/shard_map/pallas_call | solution.py:577
  4.1 0.5 %shard_map.30 = (f32[2432,128]{1,0:T(8,128)S(1)}, f32[704,128]{1,0:T(8,128)S(1)}, f32[704,128]{1,0:T(8,128)S(1)}) custom-call(f32[96,128]{1,0:T(8,128)S(1)} %get-tuple-element.40.own.refs_0_, f32[2432,128]{1,0:T(8,128)S(1)} %get-tuple-element.41.edge.edge0, f32[2432,128]{1,0:T(8,128)S(1)} %get-tuple-element.42.inner.inner0, ...), custom_call_target="tpu_custom_call" | custom-call | flops 4096000 | bytes 2490368 | tf_op jit(solution)/shard_map/pallas_call | solution.py:577
  4.6 0.1 collective-permute-start.4
  4.7 5.7 %collective-permute-start.5 = (f32[704,128]{1,0:T(8,128)S(1)}, f32[704,128]{1,0:T(8,128)S(1)}, u32[]{:S(2)}, u32[]{:S(2)}) collective-permute-start(f32[704,128]{1,0:T(8,128)S(1)} %get-tuple-element.59), channel_id=1, source_target_pairs={{0,15},{1,2},{2,1},{3,4},{4,3},{5,6},{6,5},{7,8},{8,7},{9,10},{10,... | collective-permute-start | bytes 1081352 | tf_op jit(solution)/shard_map/ppermute | solution.py:592
  10.4 0.1 collective-permute-start.1
  10.5 4.4 %collective-permute-start.3 = (f32[512,128]{1,0:T(8,128)S(1)}, f32[512,128]{1,0:T(8,128)S(1)}, u32[]{:S(2)}, u32[]{:S(2)}) collective-permute-start(f32[512,128]{1,0:T(8,128)S(1)} %get-tuple-element.53), channel_id=1, source_target_pairs={{0,15},{1,2},{2,1},{3,4},{4,3},{5,6},{6,5},{7,8},{8,7},{9,10},{10,... | collective-permute-start | bytes 786440 | tf_op jit(solution)/shard_map/ppermute | solution.py:592
  14.9 3.2 %collective-permute-done.1.got_b = f32[336,128]{1,0:T(8,128)S(1)} collective-permute-done((f32[336,128]{1,0:T(8,128)S(1)}, f32[336,128]{1,0:T(8,128)S(1)}, u32[]{:S(2)}, u32[]{:S(2)}) %collective-permute-start.1) | collective-permute-done | bytes 172064 | tf_op jit(solution)/shard_map/ppermute | solution.py:592
  18.0 0.9 %shard_map.31 = (f32[2432,128]{1,0:T(8,128)S(1)}, f32[2432,128]{1,0:T(8,128)S(1)}, f32[320,128]{1,0:T(8,128)S(1)}, f32[320,128]{1,0:T(8,128)S(1)}, f32[96,128]{1...) custom-call(f32[96,128]{1,0:T(8,128)S(1)} %get-tuple-element.40.own.refs_0_, ...), custom_call_target="tpu_custom_call" | custom-call | flops 8192000 | bytes 4980736 | tf_op jit(solution)/shard_map/pallas_call | solution.py:577
  19.0 5.3 %collective-permute-start.6 = (f32[320,128]{1,0:T(8,128)S(1)}, f32[320,128]{1,0:T(8,128)S(1)}, u32[]{:S(2)}, u32[]{:S(2)}) collective-permute-start(f32[320,128]{1,0:T(8,128)S(1)} %get-tuple-element.63), channel_id=1, source_target_pairs={{0,1},{1,0},{2,3},{3,2},{4,5},{5,4},{6,7},{7,6},{8,9},{9,8},{10,11... | collective-permute-start | bytes 491528 | tf_op jit(solution)/shard_map/ppermute | solution.py:591
  24.3 0.0 collective-permute-done.2.got_a
  24.3 4.8 %collective-permute-start.7 = (f32[320,128]{1,0:T(8,128)S(1)}, f32[320,128]{1,0:T(8,128)S(1)}, u32[]{:S(2)}, u32[]{:S(2)}) collective-permute-start(f32[320,128]{1,0:T(8,128)S(1)} %get-tuple-element.64), channel_id=1, source_target_pairs={{0,15},{1,2},{2,1},{3,4},{4,3},{5,6},{6,5},{7,8},{8,7},{9,10},{10,... | collective-permute-start | bytes 491528 | tf_op jit(solution)/shard_map/ppermute | solution.py:592
  29.1 0.0 collective-permute-done.3.got_b
  29.1 1.1 %shard_map.32 = (f32[2432,128]{1,0:T(8,128)S(1)}, f32[896,128]{1,0:T(8,128)S(1)}, f32[2432,128]{1,0:T(8,128)S(1)}, f32[2432,128]{1,0:T(8,128)S(1)}, f32[320,128]{1,0:T(8,128)S(1)}, /*index=5*/f32[320,128]{1,0:T(8,128)S(1)}) custom-call(f32[96,128]{1,0:T(8,128)S(1)} %get-tuple-element.40.own.refs_0_, f32[96,128]{1,0:T(8,128)S(1)} %get-tuple-element.47.beside.refs_1_, ...), custom_call_target="tpu_custom_call" | custom-call | flops 12288000 | bytes 7471104 | tf_op jit(solution)/shard_map/pallas_call | solution.py:577
  30.2 0.1 collective-permute-start.8
  30.3 1.8 %collective-permute-start.9 = (f32[320,128]{1,0:T(8,128)S(1)}, f32[320,128]{1,0:T(8,128)S(1)}, u32[]{:S(2)}, u32[]{:S(2)}) collective-permute-start(f32[320,128]{1,0:T(8,128)S(1)} %get-tuple-element.69), channel_id=1, source_target_pairs={{0,15},{1,2},{2,1},{3,4},{4,3},{5,6},{6,5},{7,8},{8,7},{9,10},{10,... | collective-permute-start | bytes 491528 | tf_op jit(solution)/shard_map/ppermute | solution.py:592
  32.1 1.5 %shard_map.33 = (f32[2432,128]{1,0:T(8,128)S(1)}, f32[2432,128]{1,0:T(8,128)S(1)}, f32[2432,128]{1,0:T(8,128)S(1)}, f32[320,128]{1,0:T(8,128)S(1)}, f32[320,128]{1,0:T(8,128)S(1)}) custom-call(f32[96,128]{1,0:T(8,128)S(1)} %get-tuple-element.40.own.refs_0_, f32[96,128]{1,0:T(8,128)S(1)} %get-tuple-element.47.beside.refs_1_, ...), custom_call_target="tpu_custom_call" | custom-call | flops 12288000 | bytes 7471104 | tf_op jit(solution)/shard_map/pallas_call | solution.py:577
  33.6 0.1 collective-permute-start.10
  33.7 2.8 %collective-permute-start.11 = (f32[320,128]{1,0:T(8,128)S(1)}, f32[320,128]{1,0:T(8,128)S(1)}, u32[]{:S(2)}, u32[]{:S(2)}) collective-permute-start(f32[320,128]{1,0:T(8,128)S(1)} %get-tuple-element.73), channel_id=1, source_target_pairs={{0,15},{1,2},{2,1},{3,4},{4,3},{5,6},{6,5},{7,8},{8,7},{9,10},{10,... | collective-permute-start | bytes 491528 | tf_op jit(solution)/shard_map/ppermute | solution.py:592
  36.5 1.3 %shard_map.34 = (f32[2432,128]{1,0:T(8,128)S(1)}, f32[2432,128]{1,0:T(8,128)S(1)}, f32[2432,128]{1,0:T(8,128)S(1)}) custom-call(f32[96,128]{1,0:T(8,128)S(1)} %get-tuple-element.40.own.refs_0_, f32[96,128]{1,0:T(8,128)S(1)} %get-tuple-element.47.beside.refs_1_, f32[2432,128]{1,0:T(8,128)S(1)} %get-tuple-element.54.refs_3_.refs_2_, ...), custom_call_target="tpu_custom_call" | custom-call | flops 12288000 | bytes 7471104 | tf_op jit(solution)/shard_map/pallas_call | solution.py:577
  37.9 2.5 %shard_map.35 = (f32[2432,128]{1,0:T(8,128)S(1)}, f32[2432,128]{1,0:T(8,128)S(1)}, f32[19,4,64,128]{3,2,1,0:T(8,128)}) custom-call(f32[96,128]{1,0:T(8,128)S(1)} %get-tuple-element.40.own.refs_0_, f32[96,128]{1,0:T(8,128)S(1)} %get-tuple-element.47.beside.refs_1_, f32[2432,128]{1,0:T(8,128)S(1)} %get-tuple-element.60.refs_3_.refs_2_, ...), custom_call_target="tpu_custom_call" | custom-call | flops 12288000 | bytes 7471104 | tf_op jit(solution)/shard_map/pallas_call | solution.py:577
  40.4 0.9 %collective-permute-done.11.got_b = f32[320,128]{1,0:T(8,128)S(1)} collective-permute-done((f32[320,128]{1,0:T(8,128)S(1)}, f32[320,128]{1,0:T(8,128)S(1)}, u32[]{:S(2)}, u32[]{:S(2)}) %collective-permute-start.11) | collective-permute-done | bytes 163872 | tf_op jit(solution)/shard_map/ppermute | solution.py:592
  41.3 1.2 %shard_map.36 = f32[19,4,64,128]{3,2,1,0:T(8,128)} custom-call(f32[96,128]{1,0:T(8,128)S(1)} %get-tuple-element.40.own.refs_0_, f32[96,128]{1,0:T(8,128)S(1)} %get-tuple-element.47.beside.refs_1_, f32[2432,128]{1,0:T(8,128)S(1)} %get-tuple-element.65.refs_3_.edge_old, f32[2432,128]{1,0:T(8,128)S(1)} %get-tuple-element.70.edge, ...), custom_call_target="tpu_custom_call", output_to_operand_aliasing={{}: (7, {})} | custom-call | flops 4096000 | bytes 2490368 | tf_op jit(solution)/shard_map/pallas_call | solution.py:577
  (9 shorter events, 0.0 us)
Async XLA Ops:
  1.6 8.8 %collective-permute-start = (f32[336,128]{1,0:T(8,128)S(1)}, f32[336,128]{1,0:T(8,128)S(1)}, u32[]{:S(2)}, u32[]{:S(2)}) collective-permute-start(f32[336,128]{1,0:T(8,128)S(1)} %get-tuple-element.45), channel_id=1, source_target_pairs={{0,1},{1,0},{2,3},{3,2},{4,5},{5,4},{6,7},{7,6},{8,9},{9,8},{10,11... | collective-permute-start | bytes 516104 | tf_op jit(solution)/shard_map/ppermute | solution.py:591
  4.6 25.7 %collective-permute-start.4 = (f32[704,128]{1,0:T(8,128)S(1)}, f32[704,128]{1,0:T(8,128)S(1)}, u32[]{:S(2)}, u32[]{:S(2)}) collective-permute-start(f32[704,128]{1,0:T(8,128)S(1)} %get-tuple-element.58), channel_id=1, source_target_pairs={{0,1},{1,0},{2,3},{3,2},{4,5},{5,4},{6,7},{7,6},{8,9},{9,8},{10,11... | collective-permute-start | bytes 1081352 | tf_op jit(solution)/shard_map/ppermute | solution.py:591
  4.7 27.4 %collective-permute-start.5 = (f32[704,128]{1,0:T(8,128)S(1)}, f32[704,128]{1,0:T(8,128)S(1)}, u32[]{:S(2)}, u32[]{:S(2)}) collective-permute-start(f32[704,128]{1,0:T(8,128)S(1)} %get-tuple-element.59), channel_id=1, source_target_pairs={{0,15},{1,2},{2,1},{3,4},{4,3},{5,6},{6,5},{7,8},{8,7},{9,10},{10,... | collective-permute-start | bytes 1081352 | tf_op jit(solution)/shard_map/ppermute | solution.py:592
  10.4 7.6 %collective-permute-start.1 = (f32[336,128]{1,0:T(8,128)S(1)}, f32[336,128]{1,0:T(8,128)S(1)}, u32[]{:S(2)}, u32[]{:S(2)}) collective-permute-start(f32[336,128]{1,0:T(8,128)S(1)} %get-tuple-element.46), channel_id=1, source_target_pairs={{0,15},{1,2},{2,1},{3,4},{4,3},{5,6},{6,5},{7,8},{8,7},{9,10},{10,... | collective-permute-start | bytes 516104 | tf_op jit(solution)/shard_map/ppermute | solution.py:592
  10.5 13.8 %collective-permute-start.2 = (f32[512,128]{1,0:T(8,128)S(1)}, f32[512,128]{1,0:T(8,128)S(1)}, u32[]{:S(2)}, u32[]{:S(2)}) collective-permute-start(f32[512,128]{1,0:T(8,128)S(1)} %get-tuple-element.52), channel_id=1, source_target_pairs={{0,1},{1,0},{2,3},{3,2},{4,5},{5,4},{6,7},{7,6},{8,9},{9,8},{10,11... | collective-permute-start | bytes 786440 | tf_op jit(solution)/shard_map/ppermute | solution.py:591
  10.5 18.6 %collective-permute-start.3 = (f32[512,128]{1,0:T(8,128)S(1)}, f32[512,128]{1,0:T(8,128)S(1)}, u32[]{:S(2)}, u32[]{:S(2)}) collective-permute-start(f32[512,128]{1,0:T(8,128)S(1)} %get-tuple-element.53), channel_id=1, source_target_pairs={{0,15},{1,2},{2,1},{3,4},{4,3},{5,6},{6,5},{7,8},{8,7},{9,10},{10,... | collective-permute-start | bytes 786440 | tf_op jit(solution)/shard_map/ppermute | solution.py:592
  19.0 14.7 %collective-permute-start.6 = (f32[320,128]{1,0:T(8,128)S(1)}, f32[320,128]{1,0:T(8,128)S(1)}, u32[]{:S(2)}, u32[]{:S(2)}) collective-permute-start(f32[320,128]{1,0:T(8,128)S(1)} %get-tuple-element.63), channel_id=1, source_target_pairs={{0,1},{1,0},{2,3},{3,2},{4,5},{5,4},{6,7},{7,6},{8,9},{9,8},{10,11... | collective-permute-start | bytes 491528 | tf_op jit(solution)/shard_map/ppermute | solution.py:591
  24.3 12.2 %collective-permute-start.7 = (f32[320,128]{1,0:T(8,128)S(1)}, f32[320,128]{1,0:T(8,128)S(1)}, u32[]{:S(2)}, u32[]{:S(2)}) collective-permute-start(f32[320,128]{1,0:T(8,128)S(1)} %get-tuple-element.64), channel_id=1, source_target_pairs={{0,15},{1,2},{2,1},{3,4},{4,3},{5,6},{6,5},{7,8},{8,7},{9,10},{10,... | collective-permute-start | bytes 491528 | tf_op jit(solution)/shard_map/ppermute | solution.py:592
  30.2 7.7 %collective-permute-start.8 = (f32[320,128]{1,0:T(8,128)S(1)}, f32[320,128]{1,0:T(8,128)S(1)}, u32[]{:S(2)}, u32[]{:S(2)}) collective-permute-start(f32[320,128]{1,0:T(8,128)S(1)} %get-tuple-element.68), channel_id=1, source_target_pairs={{0,1},{1,0},{2,3},{3,2},{4,5},{5,4},{6,7},{7,6},{8,9},{9,8},{10,11... | collective-permute-start | bytes 491528 | tf_op jit(solution)/shard_map/ppermute | solution.py:591
  30.3 7.6 %collective-permute-start.9 = (f32[320,128]{1,0:T(8,128)S(1)}, f32[320,128]{1,0:T(8,128)S(1)}, u32[]{:S(2)}, u32[]{:S(2)}) collective-permute-start(f32[320,128]{1,0:T(8,128)S(1)} %get-tuple-element.69), channel_id=1, source_target_pairs={{0,15},{1,2},{2,1},{3,4},{4,3},{5,6},{6,5},{7,8},{8,7},{9,10},{10,... | collective-permute-start | bytes 491528 | tf_op jit(solution)/shard_map/ppermute | solution.py:592
  33.6 6.8 %collective-permute-start.10 = (f32[320,128]{1,0:T(8,128)S(1)}, f32[320,128]{1,0:T(8,128)S(1)}, u32[]{:S(2)}, u32[]{:S(2)}) collective-permute-start(f32[320,128]{1,0:T(8,128)S(1)} %get-tuple-element.72), channel_id=1, source_target_pairs={{0,1},{1,0},{2,3},{3,2},{4,5},{5,4},{6,7},{7,6},{8,9},{9,8},{10,11... | collective-permute-start | bytes 491528 | tf_op jit(solution)/shard_map/ppermute | solution.py:591
  33.7 7.6 %collective-permute-start.11 = (f32[320,128]{1,0:T(8,128)S(1)}, f32[320,128]{1,0:T(8,128)S(1)}, u32[]{:S(2)}, u32[]{:S(2)}) collective-permute-start(f32[320,128]{1,0:T(8,128)S(1)} %get-tuple-element.73), channel_id=1, source_target_pairs={{0,15},{1,2},{2,1},{3,4},{4,3},{5,6},{6,5},{7,8},{8,7},{9,10},{10,... | collective-permute-start | bytes 491528 | tf_op jit(solution)/shard_map/ppermute | solution.py:592

commit v5 on v4

--- a/solution.py
+++ b/solution.py
@@ -247,14 +247,15 @@
 
 
 def step_planes(t, steps, field, new, heights, planes, nz, ny):
-    def body(z):
-        lev = levels(z, nz, ny)
-        for p in planes:
+    for p in planes:
+
+        def body(z, p=p):
+            lev = levels(z, nz, ny)
             post = collide([pull(field, heights, lev, i, p, z) for i in range(Q)], t, steps)
             for i in range(Q):
                 new.store(i, p, z, post[i])
 
-    over_rows(nz, body)
+        over_rows(nz, body)
 
 
 def give_second(inner, width, nz, out_a, out_b, rest=None):
@@ -283,50 +284,62 @@
         copy((out_b, out_a), width - 2, 1)
 
 
-def edge0_kernel(width, nz, pops, h_hbm, edge, out_a, out_b, own, buf, h, up, down, sem):
+def first_edge(nz, side, buf, edge, copies, part):
+    for k, copy in enumerate(copies):
+        copy.wait()
+        for z in range(k * part, (k + 1) * part, SUB):
+            post = collide([buf[i, pl.ds(z, SUB), :] for i in range(Q)], 0, STEPS)
+            for i in range(Q):
+                put_rows(edge, (2 * i + side) * nz + z, post[i])
+
+
+def near_message(width, nz, edge, own, low, out):
+    for cond, comps, e, first in ((low, MINUS, 0, 0), (jnp.logical_not(low), PLUS, 1, width - 2)):
+
+        @pl.when(cond)
+        def _(comps=comps, e=e, first=first):
+            for k, i in enumerate(comps):
+                for z in range(0, nz, SUB):
+                    put_rows(out, k * nz + z, rows_at(edge, (2 * i + e) * nz + z))
+            for k in range(2):
+                put_rows(out, NP * nz + k * SUB, rows_at(own, (3 * (first + k) + 1) * SUB))
+
+
+def edge0_kernel(width, nz, pops, h_hbm, edge, out_b, own, buf, h, sem):
     ny = h.shape[1]
-    edges = (0, width - 1)
+    odd = lax.rem(lax.axis_index("gx"), 2)
+    plane = odd * (width - 1)
     part = nz // HEAD_PARTS
     copies = []
     for k in range(HEAD_PARTS):
         rows = pl.ds(k * part, part)
-        for e, p in enumerate(edges):
-            copies.append(pltpu.make_async_copy(pops.at[:, p, rows], buf.at[:, e, rows], sem.at[2 * k + e]))
-    heights = pltpu.make_async_copy(h_hbm, h, sem.at[2 * HEAD_PARTS])
+        copies.append(pltpu.make_async_copy(pops.at[:, plane, rows], buf.at[:, rows], sem.at[k]))
+    heights = pltpu.make_async_copy(h_hbm, h, sem.at[HEAD_PARTS])
     for c in copies + [heights]:
         c.start()
     heights.wait()
     hf = h[...].astype(jnp.float32)
     for p in range(width):
-        row = jnp.broadcast_to(hf[p : p + 1], (SUB, ny))
-        put_heights(own, p, row)
-        for out, first in ((down, 0), (up, width - 2)):
-            if first <= p < first + 2:
-                put_rows(out, NP * nz + (p - first) * SUB, row)
-    field = Field(width, nz, edge)
-    for k in range(HEAD_PARTS):
-        copies[2 * k].wait()
-        copies[2 * k + 1].wait()
-        for z in range(k * part, (k + 1) * part, SUB):
-            for e, p in enumerate(edges):
-                post = collide([buf[i, e, pl.ds(z, SUB), :] for i in range(Q)], 0, STEPS)
-                for i in range(Q):
-                    field.store(i, p, z, post[i])
-                for j in range(NP):
-                    if e:
-                        put_rows(up, j * nz + z, post[PLUS[j]])
-                    else:
-                        put_rows(down, j * nz + z, post[MINUS[j]])
-    give(up, down, out_a, out_b)
-
-
-def inner0_kernel(width, nz, pops, own, edge, inner, out_a, out_b, rest, buf, up, down, sem):
+        put_heights(own, p, jnp.broadcast_to(hf[p : p + 1], (SUB, ny)))
+    first_edge(nz, odd, buf, edge, copies, part)
+    near_message(width, nz, edge, own, odd == 0, out_b)
+
+
+def inner0_kernel(
+    width, nz, pops, own, edge_b, edge, inner, near_a, out_a, out_b, rest, buf, edge_buf, up, down, sem
+):
     ny = own.shape[1]
-    copy = pltpu.make_async_copy(pops.at[:, 1 : width - 1], buf, sem)
-    copy.start()
+    even = 1 - lax.rem(lax.axis_index("gx"), 2)
+    copies = [
+        pltpu.make_async_copy(pops.at[:, even * (width - 1)], edge_buf, sem.at[0]),
+        pltpu.make_async_copy(pops.at[:, 1 : width - 1], buf, sem.at[1]),
+    ]
+    for c in copies:
+        c.start()
     field = Field(width, nz, edge, inner)
     heights = Heights(width, own)
-    copy.wait()
+    first_edge(nz, even, edge_buf, edge, copies[:1], nz)
+    copies[1].wait()
 
     def body(z):
         for p in range(1, width - 1):
@@ -349,6 +362,7 @@
 
     over_rows(nz, body_ghost)
     give(up, down, out_a, out_b)
+    near_message(width, nz, edge, own, even == 0, near_a)
 
 
 def inner1_kernel(width, nz, own, edge, inner, rest, new_inner, out_a, out_b):
@@ -592,29 +606,30 @@
         b = lax.ppermute(b, "gx", pair_b)
         return [a, b]
 
-    edge0, a, b, own = call(
+    edge0, near_b, own = call(
         edge0_kernel,
         [pops, heights],
-        [edge_t, rows(near_n), rows(near_n), rows(3 * width * SUB)],
-        2,
-        [
-            pltpu.VMEM((Q, 2, nz, ny), jnp.float32),
-            pltpu.VMEM((width, ny), jnp.int32),
-            scratch(near_n),
-            scratch(near_n),
-            dma((2 * HEAD_PARTS + 1,)),
-        ],
+        [edge_t, rows(near_n), rows(3 * width * SUB)],
+        1,
+        [pltpu.VMEM((Q, nz, ny), jnp.float32), pltpu.VMEM((width, ny), jnp.int32), dma((HEAD_PARTS + 1,))],
         in_specs=[hbm, hbm],
     )
-    near = exchange(a, b)
-    inner0, a, b, rest = call(
+    edge0, inner0, near_a, a, b, rest = call(
         inner0_kernel,
         [pops, own, edge0],
-        [inner_t, rows(sums_n), rows(sums_n), rows(2 * len(REST) * nz)],
+        [edge_t, inner_t, rows(near_n), rows(sums_n), rows(sums_n), rows(2 * len(REST) * nz)],
         width,
-        [pltpu.VMEM((Q, width - 2, nz, ny), jnp.float32), scratch(sums_n), scratch(sums_n), dma],
+        [
+            pltpu.VMEM((Q, width - 2, nz, ny), jnp.float32),
+            pltpu.VMEM((Q, nz, ny), jnp.float32),
+            scratch(sums_n),
+            scratch(sums_n),
+            dma((2,)),
+        ],
         in_specs=[hbm, vmem, vmem],
+        input_output_aliases={2: 0},
     )
+    near = exchange(near_a, near_b)
     first = exchange(a, b)
     inner1, a, b = call(inner1_kernel, [own, edge0, inner0, rest], [inner_t, rows(rest_n), rows(rest_n)], width - 2)
     messages = {2: exchange(a, b)}

time: 42.7 us -> 41.7 us (0.977)
  starting transfers between devices: 25.6 us -> 22.4 us
  waiting for transfers between devices: 4.14 us -> 6.72 us
    ppermute x6, starting transfers between devices: 19.5 us -> 15.6 us  [exchange(): b = lax.ppermute(b, 'gx', pair_b)]
    ppermute x6, waiting for transfers between devices: 4.12 us -> 6.71 us  [exchange(): b = lax.ppermute(b, 'gx', pair_b)]
    ppermute x6, starting transfers between devices: 6.08 us -> 6.84 us  [exchange(): a = lax.ppermute(a, 'gx', pair_a)]
  transfers between devices with their start and end apart: 12 -> 12, of which waited for: 2 -> 2; matrix products, arithmetic and copies ran while one was open for 0% -> 0% of each run, Pallas kernels for 23% -> 24%
where the time goes in v5:
time: 41.7 us; the launch traced here: 41.5 us
  starting transfers between devices  22.4 us (54%)
  Pallas kernels  12.3 us (29%)
  waiting for transfers between devices  6.72 us (16%)
    ppermute x6, starting transfers between devices, exchange(): b = lax.ppermute(b, 'gx', pair_b)  15.6 us
    pallas_call x9, Pallas kernels, call(): pl.pallas_call(functools.partial(kernel, width, nz), out_shape=outs, in_s...  12.3 us
    ppermute x6, starting transfers between devices, exchange(): a = lax.ppermute(a, 'gx', pair_a)  6.84 us
    ppermute x6, waiting for transfers between devices, exchange(): b = lax.ppermute(b, 'gx', pair_b)  6.71 us
  transfers between devices with their start and end apart: 12, of which 2 were waited for; matrix products, arithmetic and copies ran while one was open for 0% of the time, Pallas kernels for 24%

profile of v5, /device:TPU:0, one launch (start us, length us, event | category | flops | bytes accessed | tf_op | source)
XLA Modules:
  0.0 41.5 jit_solution(5719721467183289208)
XLA Ops:
  0.0 1.2 %shard_map.28 = (f32[2432,128]{1,0:T(8,128)S(1)}, f32[336,128]{1,0:T(8,128)S(1)}, f32[96,128]{1,0:T(8,128)S(1)}) custom-call(f32[19,4,64,128]{3,2,1,0:T(8,128)} %pops.3, s32[4,128]{1,0:T(4,128)} %h_hbm.1), custom_call_target="tpu_custom_call" | custom-call | flops 2048000 | bytes 1245184 | tf_op jit(solution)/shard_map/pallas_call | solution.py:591
  1.2 5.5 %collective-permute-start.1 = (f32[336,128]{1,0:T(8,128)S(1)}, f32[336,128]{1,0:T(8,128)S(1)}, u32[]{:S(2)}, u32[]{:S(2)}) collective-permute-start(f32[336,128]{1,0:T(8,128)S(1)} %get-tuple-element.48), channel_id=1, source_target_pairs={{0,15},{1,2},{2,1},{3,4},{4,3},{5,6},{6,5},{7,8},{8,7},{9,10},{10,... | collective-permute-start | bytes 516104 | tf_op jit(solution)/shard_map/ppermute | solution.py:606
  6.7 2.1 %shard_map.29 = (f32[2432,128]{1,0:T(8,128)S(1)}, f32[2432,128]{1,0:T(8,128)S(1)}, f32[336,128]{1,0:T(8,128)S(1)}, f32[512,128]{1,0:T(8,128)S(1)}, f32[512,128]{1,0:T(8,128)S(1)}, /*index=5*/f32[768,128]{1,0:T(8,128)S(1)}) custom-call(f32[19,4,64,128]{3,2,1,0:T(8,128)} %pops.3, ...), custom_call_target="tpu_custom_call", output_to_operand_aliasing={{0}: (2, {})} | custom-call | flops 8192000 | bytes 4980736 | tf_op jit(solution)/shard_map/pallas_call | solution.py:591
  8.8 0.5 %shard_map.30 = (f32[2432,128]{1,0:T(8,128)S(1)}, f32[704,128]{1,0:T(8,128)S(1)}, f32[704,128]{1,0:T(8,128)S(1)}) custom-call(f32[96,128]{1,0:T(8,128)S(1)} %get-tuple-element.41.own.refs_0_, f32[2432,128]{1,0:T(8,128)S(1)} %get-tuple-element.43.edge.edge0, f32[2432,128]{1,0:T(8,128)S(1)} %get-tuple-element.44.inner.inner0, ...), custom_call_target="tpu_custom_call" | custom-call | flops 4096000 | bytes 2490368 | tf_op jit(solution)/shard_map/pallas_call | solution.py:591
  9.3 0.1 collective-permute-start.4
  9.4 0.7 %collective-permute-start.5 = (f32[704,128]{1,0:T(8,128)S(1)}, f32[704,128]{1,0:T(8,128)S(1)}, u32[]{:S(2)}, u32[]{:S(2)}) collective-permute-start(f32[704,128]{1,0:T(8,128)S(1)} %get-tuple-element.61), channel_id=1, source_target_pairs={{0,15},{1,2},{2,1},{3,4},{4,3},{5,6},{6,5},{7,8},{8,7},{9,10},{10,... | collective-permute-start | bytes 1081352 | tf_op jit(solution)/shard_map/ppermute | solution.py:606
  10.1 0.5 %collective-permute-start.2 = (f32[512,128]{1,0:T(8,128)S(1)}, f32[512,128]{1,0:T(8,128)S(1)}, u32[]{:S(2)}, u32[]{:S(2)}) collective-permute-start(f32[512,128]{1,0:T(8,128)S(1)} %get-tuple-element.54), channel_id=1, source_target_pairs={{0,1},{1,0},{2,3},{3,2},{4,5},{5,4},{6,7},{7,6},{8,9},{9,8},{10,11... | collective-permute-start | bytes 786440 | tf_op jit(solution)/shard_map/ppermute | solution.py:605
  10.6 0.0 collective-permute-done.1.got_b
  10.6 3.8 %collective-permute-start.3 = (f32[512,128]{1,0:T(8,128)S(1)}, f32[512,128]{1,0:T(8,128)S(1)}, u32[]{:S(2)}, u32[]{:S(2)}) collective-permute-start(f32[512,128]{1,0:T(8,128)S(1)} %get-tuple-element.55), channel_id=1, source_target_pairs={{0,15},{1,2},{2,1},{3,4},{4,3},{5,6},{6,5},{7,8},{8,7},{9,10},{10,... | collective-permute-start | bytes 786440 | tf_op jit(solution)/shard_map/ppermute | solution.py:606
  14.4 0.9 %shard_map.31 = (f32[2432,128]{1,0:T(8,128)S(1)}, f32[2432,128]{1,0:T(8,128)S(1)}, f32[320,128]{1,0:T(8,128)S(1)}, f32[320,128]{1,0:T(8,128)S(1)}, f32[96,128]{1...) custom-call(f32[96,128]{1,0:T(8,128)S(1)} %get-tuple-element.41.own.refs_0_, ...), custom_call_target="tpu_custom_call" | custom-call | flops 8192000 | bytes 4980736 | tf_op jit(solution)/shard_map/pallas_call | solution.py:591
  15.4 0.1 collective-permute-start.6
  15.5 1.0 %collective-permute-start.7 = (f32[320,128]{1,0:T(8,128)S(1)}, f32[320,128]{1,0:T(8,128)S(1)}, u32[]{:S(2)}, u32[]{:S(2)}) collective-permute-start(f32[320,128]{1,0:T(8,128)S(1)} %get-tuple-element.66), channel_id=1, source_target_pairs={{0,15},{1,2},{2,1},{3,4},{4,3},{5,6},{6,5},{7,8},{8,7},{9,10},{10,... | collective-permute-start | bytes 491528 | tf_op jit(solution)/shard_map/ppermute | solution.py:606
  16.5 5.5 %collective-permute-done.3.got_b = f32[512,128]{1,0:T(8,128)S(1)} collective-permute-done((f32[512,128]{1,0:T(8,128)S(1)}, f32[512,128]{1,0:T(8,128)S(1)}, u32[]{:S(2)}, u32[]{:S(2)}) %collective-permute-start.3) | collective-permute-done | bytes 262176 | tf_op jit(solution)/shard_map/ppermute | solution.py:606
  21.9 1.2 %shard_map.32 = (f32[2432,128]{1,0:T(8,128)S(1)}, f32[896,128]{1,0:T(8,128)S(1)}, f32[2432,128]{1,0:T(8,128)S(1)}, f32[2432,128]{1,0:T(8,128)S(1)}, f32[320,128]{1,0:T(8,128)S(1)}, /*index=5*/f32[320,128]{1,0:T(8,128)S(1)}) custom-call(f32[96,128]{1,0:T(8,128)S(1)} %get-tuple-element.41.own.refs_0_, f32[96,128]{1,0:T(8,128)S(1)} %get-tuple-element.49.beside.refs_1_, ...), custom_call_target="tpu_custom_call" | custom-call | flops 12288000 | bytes 7471104 | tf_op jit(solution)/shard_map/pallas_call | solution.py:591
  23.1 6.1 %collective-permute-start.8 = (f32[320,128]{1,0:T(8,128)S(1)}, f32[320,128]{1,0:T(8,128)S(1)}, u32[]{:S(2)}, u32[]{:S(2)}) collective-permute-start(f32[320,128]{1,0:T(8,128)S(1)} %get-tuple-element.70), channel_id=1, source_target_pairs={{0,1},{1,0},{2,3},{3,2},{4,5},{5,4},{6,7},{7,6},{8,9},{9,8},{10,11... | collective-permute-start | bytes 491528 | tf_op jit(solution)/shard_map/ppermute | solution.py:605
  29.2 2.0 %collective-permute-start.9 = (f32[320,128]{1,0:T(8,128)S(1)}, f32[320,128]{1,0:T(8,128)S(1)}, u32[]{:S(2)}, u32[]{:S(2)}) collective-permute-start(f32[320,128]{1,0:T(8,128)S(1)} %get-tuple-element.71), channel_id=1, source_target_pairs={{0,15},{1,2},{2,1},{3,4},{4,3},{5,6},{6,5},{7,8},{8,7},{9,10},{10,... | collective-permute-start | bytes 491528 | tf_op jit(solution)/shard_map/ppermute | solution.py:606
  31.3 1.5 %shard_map.33 = (f32[2432,128]{1,0:T(8,128)S(1)}, f32[2432,128]{1,0:T(8,128)S(1)}, f32[2432,128]{1,0:T(8,128)S(1)}, f32[320,128]{1,0:T(8,128)S(1)}, f32[320,128]{1,0:T(8,128)S(1)}) custom-call(f32[96,128]{1,0:T(8,128)S(1)} %get-tuple-element.41.own.refs_0_, f32[96,128]{1,0:T(8,128)S(1)} %get-tuple-element.49.beside.refs_1_, ...), custom_call_target="tpu_custom_call" | custom-call | flops 12288000 | bytes 7471104 | tf_op jit(solution)/shard_map/pallas_call | solution.py:591
  32.8 0.1 collective-permute-start.10
  32.8 2.5 %collective-permute-start.11 = (f32[320,128]{1,0:T(8,128)S(1)}, f32[320,128]{1,0:T(8,128)S(1)}, u32[]{:S(2)}, u32[]{:S(2)}) collective-permute-start(f32[320,128]{1,0:T(8,128)S(1)} %get-tuple-element.75), channel_id=1, source_target_pairs={{0,15},{1,2},{2,1},{3,4},{4,3},{5,6},{6,5},{7,8},{8,7},{9,10},{10,... | collective-permute-start | bytes 491528 | tf_op jit(solution)/shard_map/ppermute | solution.py:606
  35.3 1.3 %shard_map.34 = (f32[2432,128]{1,0:T(8,128)S(1)}, f32[2432,128]{1,0:T(8,128)S(1)}, f32[2432,128]{1,0:T(8,128)S(1)}) custom-call(f32[96,128]{1,0:T(8,128)S(1)} %get-tuple-element.41.own.refs_0_, f32[96,128]{1,0:T(8,128)S(1)} %get-tuple-element.49.beside.refs_1_, f32[2432,128]{1,0:T(8,128)S(1)} %get-tuple-element.56.refs_3_.refs_2_, ...), custom_call_target="tpu_custom_call" | custom-call | flops 12288000 | bytes 7471104 | tf_op jit(solution)/shard_map/pallas_call | solution.py:591
  36.6 0.0 collective-permute-done.9.refs_8_
  36.7 2.5 %shard_map.35 = (f32[2432,128]{1,0:T(8,128)S(1)}, f32[2432,128]{1,0:T(8,128)S(1)}, f32[19,4,64,128]{3,2,1,0:T(8,128)}) custom-call(f32[96,128]{1,0:T(8,128)S(1)} %get-tuple-element.41.own.refs_0_, f32[96,128]{1,0:T(8,128)S(1)} %get-tuple-element.49.beside.refs_1_, f32[2432,128]{1,0:T(8,128)S(1)} %get-tuple-element.62.refs_3_.refs_2_, ...), custom_call_target="tpu_custom_call" | custom-call | flops 12288000 | bytes 7471104 | tf_op jit(solution)/shard_map/pallas_call | solution.py:591
  39.2 1.2 %collective-permute-done.11.got_b = f32[320,128]{1,0:T(8,128)S(1)} collective-permute-done((f32[320,128]{1,0:T(8,128)S(1)}, f32[320,128]{1,0:T(8,128)S(1)}, u32[]{:S(2)}, u32[]{:S(2)}) %collective-permute-start.11) | collective-permute-done | bytes 163872 | tf_op jit(solution)/shard_map/ppermute | solution.py:606
  40.3 1.2 %shard_map.36 = f32[19,4,64,128]{3,2,1,0:T(8,128)} custom-call(f32[96,128]{1,0:T(8,128)S(1)} %get-tuple-element.41.own.refs_0_, f32[96,128]{1,0:T(8,128)S(1)} %get-tuple-element.49.beside.refs_1_, f32[2432,128]{1,0:T(8,128)S(1)} %get-tuple-element.67.refs_3_.edge_old, f32[2432,128]{1,0:T(8,128)S(1)} %get-tuple-element.72.edge, ...), custom_call_target="tpu_custom_call", output_to_operand_aliasing={{}: (7, {})} | custom-call | flops 4096000 | bytes 2490368 | tf_op jit(solution)/shard_map/pallas_call | solution.py:591
  (9 shorter events, 0.0 us)
Async XLA Ops:
  1.2 9.4 %collective-permute-start.1 = (f32[336,128]{1,0:T(8,128)S(1)}, f32[336,128]{1,0:T(8,128)S(1)}, u32[]{:S(2)}, u32[]{:S(2)}) collective-permute-start(f32[336,128]{1,0:T(8,128)S(1)} %get-tuple-element.48), channel_id=1, source_target_pairs={{0,15},{1,2},{2,1},{3,4},{4,3},{5,6},{6,5},{7,8},{8,7},{9,10},{10,... | collective-permute-start | bytes 516104 | tf_op jit(solution)/shard_map/ppermute | solution.py:606
  9.3 19.9 %collective-permute-start.4 = (f32[704,128]{1,0:T(8,128)S(1)}, f32[704,128]{1,0:T(8,128)S(1)}, u32[]{:S(2)}, u32[]{:S(2)}) collective-permute-start(f32[704,128]{1,0:T(8,128)S(1)} %get-tuple-element.60), channel_id=1, source_target_pairs={{0,1},{1,0},{2,3},{3,2},{4,5},{5,4},{6,7},{7,6},{8,9},{9,8},{10,11... | collective-permute-start | bytes 1081352 | tf_op jit(solution)/shard_map/ppermute | solution.py:605
  9.4 21.9 %collective-permute-start.5 = (f32[704,128]{1,0:T(8,128)S(1)}, f32[704,128]{1,0:T(8,128)S(1)}, u32[]{:S(2)}, u32[]{:S(2)}) collective-permute-start(f32[704,128]{1,0:T(8,128)S(1)} %get-tuple-element.61), channel_id=1, source_target_pairs={{0,15},{1,2},{2,1},{3,4},{4,3},{5,6},{6,5},{7,8},{8,7},{9,10},{10,... | collective-permute-start | bytes 1081352 | tf_op jit(solution)/shard_map/ppermute | solution.py:606
  10.1 4.3 %collective-permute-start = (f32[336,128]{1,0:T(8,128)S(1)}, f32[336,128]{1,0:T(8,128)S(1)}, u32[]{:S(2)}, u32[]{:S(2)}) collective-permute-start(f32[336,128]{1,0:T(8,128)S(1)} %get-tuple-element.47), channel_id=1, source_target_pairs={{0,1},{1,0},{2,3},{3,2},{4,5},{5,4},{6,7},{7,6},{8,9},{9,8},{10,11... | collective-permute-start | bytes 516104 | tf_op jit(solution)/shard_map/ppermute | solution.py:605
  10.1 5.3 %collective-permute-start.2 = (f32[512,128]{1,0:T(8,128)S(1)}, f32[512,128]{1,0:T(8,128)S(1)}, u32[]{:S(2)}, u32[]{:S(2)}) collective-permute-start(f32[512,128]{1,0:T(8,128)S(1)} %get-tuple-element.54), channel_id=1, source_target_pairs={{0,1},{1,0},{2,3},{3,2},{4,5},{5,4},{6,7},{7,6},{8,9},{9,8},{10,11... | collective-permute-start | bytes 786440 | tf_op jit(solution)/shard_map/ppermute | solution.py:605
  10.6 11.3 %collective-permute-start.3 = (f32[512,128]{1,0:T(8,128)S(1)}, f32[512,128]{1,0:T(8,128)S(1)}, u32[]{:S(2)}, u32[]{:S(2)}) collective-permute-start(f32[512,128]{1,0:T(8,128)S(1)} %get-tuple-element.55), channel_id=1, source_target_pairs={{0,15},{1,2},{2,1},{3,4},{4,3},{5,6},{6,5},{7,8},{8,7},{9,10},{10,... | collective-permute-start | bytes 786440 | tf_op jit(solution)/shard_map/ppermute | solution.py:606
  15.4 17.5 %collective-permute-start.6 = (f32[320,128]{1,0:T(8,128)S(1)}, f32[320,128]{1,0:T(8,128)S(1)}, u32[]{:S(2)}, u32[]{:S(2)}) collective-permute-start(f32[320,128]{1,0:T(8,128)S(1)} %get-tuple-element.65), channel_id=1, source_target_pairs={{0,1},{1,0},{2,3},{3,2},{4,5},{5,4},{6,7},{7,6},{8,9},{9,8},{10,11... | collective-permute-start | bytes 491528 | tf_op jit(solution)/shard_map/ppermute | solution.py:605
  15.5 19.8 %collective-permute-start.7 = (f32[320,128]{1,0:T(8,128)S(1)}, f32[320,128]{1,0:T(8,128)S(1)}, u32[]{:S(2)}, u32[]{:S(2)}) collective-permute-start(f32[320,128]{1,0:T(8,128)S(1)} %get-tuple-element.66), channel_id=1, source_target_pairs={{0,15},{1,2},{2,1},{3,4},{4,3},{5,6},{6,5},{7,8},{8,7},{9,10},{10,... | collective-permute-start | bytes 491528 | tf_op jit(solution)/shard_map/ppermute | solution.py:606
  23.1 13.5 %collective-permute-start.8 = (f32[320,128]{1,0:T(8,128)S(1)}, f32[320,128]{1,0:T(8,128)S(1)}, u32[]{:S(2)}, u32[]{:S(2)}) collective-permute-start(f32[320,128]{1,0:T(8,128)S(1)} %get-tuple-element.70), channel_id=1, source_target_pairs={{0,1},{1,0},{2,3},{3,2},{4,5},{5,4},{6,7},{7,6},{8,9},{9,8},{10,11... | collective-permute-start | bytes 491528 | tf_op jit(solution)/shard_map/ppermute | solution.py:605
  29.2 7.5 %collective-permute-start.9 = (f32[320,128]{1,0:T(8,128)S(1)}, f32[320,128]{1,0:T(8,128)S(1)}, u32[]{:S(2)}, u32[]{:S(2)}) collective-permute-start(f32[320,128]{1,0:T(8,128)S(1)} %get-tuple-element.71), channel_id=1, source_target_pairs={{0,15},{1,2},{2,1},{3,4},{4,3},{5,6},{6,5},{7,8},{8,7},{9,10},{10,... | collective-permute-start | bytes 491528 | tf_op jit(solution)/shard_map/ppermute | solution.py:606
  32.8 6.4 %collective-permute-start.10 = (f32[320,128]{1,0:T(8,128)S(1)}, f32[320,128]{1,0:T(8,128)S(1)}, u32[]{:S(2)}, u32[]{:S(2)}) collective-permute-start(f32[320,128]{1,0:T(8,128)S(1)} %get-tuple-element.74), channel_id=1, source_target_pairs={{0,1},{1,0},{2,3},{3,2},{4,5},{5,4},{6,7},{7,6},{8,9},{9,8},{10,11... | collective-permute-start | bytes 491528 | tf_op jit(solution)/shard_map/ppermute | solution.py:605
  32.8 7.5 %collective-permute-start.11 = (f32[320,128]{1,0:T(8,128)S(1)}, f32[320,128]{1,0:T(8,128)S(1)}, u32[]{:S(2)}, u32[]{:S(2)}) collective-permute-start(f32[320,128]{1,0:T(8,128)S(1)} %get-tuple-element.75), channel_id=1, source_target_pairs={{0,15},{1,2},{2,1},{3,4},{4,3},{5,6},{6,5},{7,8},{8,7},{9,10},{10,... | collective-permute-start | bytes 491528 | tf_op jit(solution)/shard_map/ppermute | solution.py:606
